TPU v7x, 512 devices: a whole 4x4x16 slice. The times are simulated.
512 devices in a mesh: tiles: 128 (over y, z, core), samp: 4 (over x).
Axes of the slice: x: 4, y: 4, z: 16, core: 2. Of those that a mesh axis runs over, the one named last changes fastest.
Arguments:
- samples: bfloat16 [256, 131072], P('samp', 'tiles'), may hold values from -6 to 6
- omega: float32 [1280, 512, 512], P('tiles', 'samp'), may hold values from -1 to 2, as said below
- coords: int32 [1280, 2], P('tiles'), may hold values from 0 to 255, as said below
Outputs:
- updated: float32 [1280, 512, 512], P('tiles', 'samp')
Inputs may be any that keep to these rules, and one draw needn't show every extreme that they name: `coords`: tile k lies with index k // 10 of tiles. Write d for that index, and blocks d * 2 to (d + 1) * 2 - 1 as its own blocks; indices of devices wrap around. The first 2 tiles of d are the diagonal tiles (I, I) of its own blocks in order. Each other tile of d is (I, J) with I an own block and J a block of d + 1, or I a block of d - 1 and J a block of d + 1, or I < J both own blocks. No unordered pair of blocks appears twice in the whole list. `omega`: tiles with I == J are symmetric with diagonal entries from 0.5 to 2.
All inputs are finite; a program needn't handle non-finite values.
Results may differ from a plain program's by a relative error of at most 0.0023.
Values may be sent and summed in bfloat16 or wider, within the bound.
No kernel may reach another device: no remote copies, remote signals or barrier semaphores. Data moves between devices by JAX's collectives and lax.ppermute only.
A program may use at most 64 MiB of HBM per device.

v0:
```python
import jax
import jax.numpy as jnp
from jax import lax
from jax.sharding import PartitionSpec as P

BLK_DEV = 2
ITERS = 2


step_size = 0.25
penalty = 0.2


def with_halo(shard, sides, width):
    for axis, dim in sides:
        size, length = (lax.axis_size(axis), shard.shape[dim])
        up = [(i, (i + 1) % size) for i in range(size)]
        down = [(j, i) for i, j in up]
        last = lax.slice_in_dim(shard, length - width, length, axis=dim)
        leading = lax.slice_in_dim(shard, 0, width, axis=dim)
        before = lax.ppermute(last, axis, up)
        after = lax.ppermute(leading, axis, down)
        shard = jnp.concatenate([before, shard, after], axis=dim)
    return shard


def columns(matrix, start, count):
    return lax.dynamic_slice_in_dim(matrix, start, count, 1)


def add_columns(totals, block, start):
    current = lax.dynamic_slice_in_dim(totals, start, block.shape[1], 1)
    return lax.dynamic_update_slice_in_dim(totals, current + block, start, 1)


def shards(samples, omega, coords):
    quarter = lax.axis_index("samp")
    tile_rows = omega.shape[1]
    width = omega.shape[2]
    own_width = samples.shape[1]
    blocks_all = BLK_DEV * lax.axis_size("tiles")
    first_block = (lax.axis_index("tiles") - 1) * BLK_DEV
    local = (coords - first_block + blocks_all) % blocks_all
    off_diagonal = (coords[:, 0] != coords[:, 1]).astype(jnp.float32)
    offset = quarter * tile_rows
    full_rows = lax.all_gather(samples, "samp", axis=0, tiled=True)
    sample_win = with_halo(full_rows, (("tiles", 1),), own_width)
    count = sample_win.shape[0]
    row_ids = offset + lax.broadcasted_iota(jnp.int32, (tile_rows, width), 0)
    col_ids = lax.broadcasted_iota(jnp.int32, (tile_rows, width), 1)
    diagonal_cells = row_ids == col_ids
    contract_cols = (((1,), (1,)), ((), ()))
    contract_rows = (((0,), (0,)), ((), ()))
    for iteration in range(ITERS):
        omega_low = omega.astype(jnp.bfloat16)
        totals = jnp.zeros((count, 3 * own_width), jnp.float32)
        for tile_slot in range(omega.shape[0]):
            row_start = local[tile_slot, 0] * width
            col_start = local[tile_slot, 1] * width
            rows_low = omega_low[tile_slot]
            row_part = columns(sample_win, row_start + offset, tile_rows)
            col_block = columns(sample_win, col_start, width)
            to_col = jnp.dot(row_part, rows_low, preferred_element_type=jnp.float32)
            to_row = lax.dot_general(
                col_block, rows_low, contract_cols, preferred_element_type=jnp.float32
            )
            totals = add_columns(totals, to_col, col_start)
            totals = add_columns(totals, to_row * off_diagonal[tile_slot], row_start + offset)
        returned = with_halo(totals, (("tiles", 1),), own_width)
        partial_value = (
            totals[:, own_width : 2 * own_width]
            + returned[:, :own_width]
            + returned[:, 4 * own_width :]
        )
        summed = lax.psum(partial_value, "samp")
        product_own = summed.astype(jnp.bfloat16)
        product_win = with_halo(product_own, (("tiles", 1),), own_width)
        new_tiles = []
        for tile_slot in range(omega.shape[0]):
            row_start = local[tile_slot, 0] * width
            col_start = local[tile_slot, 1] * width
            product_rows = columns(product_win, row_start + offset, tile_rows)
            sample_rows = columns(sample_win, row_start + offset, tile_rows)
            sample_cols = columns(sample_win, col_start, width)
            product_cols = columns(product_win, col_start, width)
            first = lax.dot_general(
                product_rows, sample_cols, contract_rows, preferred_element_type=jnp.float32
            )
            second = lax.dot_general(
                sample_rows, product_cols, contract_rows, preferred_element_type=jnp.float32
            )
            grad = (first + second) / (2.0 * count)
            value = omega[tile_slot] - step_size * grad
            shrunk = jnp.sign(value) * jnp.maximum(jnp.abs(value) - step_size * penalty, 0.0)
            positive = 0.5 * (value + jnp.sqrt(value * value + 4.0 * step_size))
            same_block = coords[tile_slot, 0] == coords[tile_slot, 1]
            new_tiles.append(jnp.where(diagonal_cells & same_block, positive, shrunk))
        omega = jnp.stack(new_tiles)
    return omega


def solution(mesh):
    in_specs = (P("samp", "tiles"), P("tiles", "samp", None), P("tiles", None))
    out_specs = P("tiles", "samp", None)
    return jax.shard_map(shards, mesh=mesh, in_specs=in_specs, out_specs=out_specs, check_vma=False)
```

profile of v0, /device:TPU:4, one launch (start us, length us, event | category | flops | bytes accessed | tf_op | source)
XLA Modules:
  0.0 228.5 jit_solution(8097895202772696019)
XLA Ops:
  0.0 16.8 %all_gather.3 = bf16[256,1024]{1,0:T(8,128)(2,1)S(1)} all-gather(bf16[64,1024]{1,0:T(8,128)(2,1)} %param.3), channel_id=1, replica_groups=mesh['tiles'=128,'samp'=4] {'samp'}, dimensions={0}, use_global_device_ids=true | all-gather | bytes 655360 | tf_op jit(solution)/shard_map/all_gather | solution.py:46
  16.8 1.9 collective-permute-start
  18.7 7.0 %collective-permute-start.1 = (bf16[256,1024]{1,0:T(8,128)(2,1)S(1)}, bf16[256,1024]{1,0:T(8,128)(2,1)}, u32[]{:S(2)}, u32[]{:S(2)}) collective-permute-start(bf16[256,1024]{1,0:T(8,128)(2,1)S(1)} %all_gather.3), channel_id=1, source_target_pairs={{4,0},{8,4},{12,8},{16,12},{20,16},{24,20},{28,24},{32,28},{36,32}... | collective-permute-start | bytes 1572872 | tf_op jit(solution)/shard_map/ppermute | solution.py:22
  40.3 1.9 convert_element_type.14
  43.1 1.1 constant_dynamic-update-slice_fusion.2
  44.2 1.1 constant_dynamic-update-slice_fusion
  56.7 1.9 collective-permute-start.2
  58.6 7.0 %collective-permute-start.3 = (f32[256,1024]{1,0:T(8,128)S(1)}, f32[256,1024]{1,0:T(8,128)S(1)}, u32[]{:S(2)}, u32[]{:S(2)}) collective-permute-start(f32[256,1024]{1,0:T(8,128)S(1)} %get-tuple-element.8), channel_id=1, source_target_pairs={{4,0},{8,4},{12,8},{16,12},{20,16},{24,20},{28,24},{32,28},{36,32}... | collective-permute-start | bytes 3145736 | tf_op jit(solution)/shard_map/ppermute | solution.py:22
  65.6 10.5 %collective-permute-done.2 = f32[256,1024]{1,0:T(8,128)S(1)} collective-permute-done((f32[256,1024]{1,0:T(8,128)S(1)}, f32[256,1024]{1,0:T(8,128)S(1)}, u32[]{:S(2)}, u32[]{:S(2)}) %collective-permute-start.2) | collective-permute-done | bytes 1048608 | tf_op jit(solution)/shard_map/ppermute | solution.py:21
  76.1 1.8 collective-permute-done.3
  78.2 28.7 %all-reduce.2 = bf16[256,1024]{1,0:T(8,128)(2,1)S(1)} all-reduce(f32[256,1024]{1,0:T(8,128)S(1)} %fusion.61), channel_id=1, replica_groups=mesh['tiles'=128,'samp'=4] {'samp'}, use_global_device_ids=true, to_apply=%region_0.1 | all-reduce | flops 262144 | bytes 1572864 | tf_op jit(solution)/shard_map/psum | solution.py:75
  106.9 1.9 collective-permute-start.4
  108.8 7.1 %collective-permute-start.5 = (bf16[256,1024]{1,0:T(8,128)(2,1)S(1)}, bf16[256,1024]{1,0:T(8,128)(2,1)S(1)}, u32[]{:S(2)}, u32[]{:S(2)}) collective-permute-start(bf16[256,1024]{1,0:T(8,128)(2,1)S(1)} %all-reduce.2), channel_id=1, source_target_pairs={{4,0},{8,4},{12,8},{16,12},{20,16},{24,20},{28,24},{32,28},{36,32}... | collective-permute-start | bytes 1572872 | tf_op jit(solution)/shard_map/ppermute | solution.py:22
  149.9 1.9 collective-permute-start.6
  151.9 7.0 %collective-permute-start.7 = (f32[256,1024]{1,0:T(8,128)S(1)}, f32[256,1024]{1,0:T(8,128)S(1)}, u32[]{:S(2)}, u32[]{:S(2)}) collective-permute-start(f32[256,1024]{1,0:T(8,128)S(1)} %get-tuple-element.6), channel_id=1, source_target_pairs={{4,0},{8,4},{12,8},{16,12},{20,16},{24,20},{28,24},{32,28},{36,32}... | collective-permute-start | bytes 3145736 | tf_op jit(solution)/shard_map/ppermute | solution.py:22
  158.8 10.5 %collective-permute-done.6 = f32[256,1024]{1,0:T(8,128)S(1)} collective-permute-done((f32[256,1024]{1,0:T(8,128)S(1)}, f32[256,1024]{1,0:T(8,128)S(1)}, u32[]{:S(2)}, u32[]{:S(2)}) %collective-permute-start.6) | collective-permute-done | bytes 1048608 | tf_op jit(solution)/shard_map/ppermute | solution.py:21
  169.4 1.8 collective-permute-done.7
  171.4 31.7 %all-reduce.3 = bf16[256,1024]{1,0:T(8,128)(2,1)S(1)} all-reduce(f32[256,1024]{1,0:T(8,128)S(1)} %fusion.60), channel_id=1, replica_groups=mesh['tiles'=128,'samp'=4] {'samp'}, use_global_device_ids=true, to_apply=%region_1.2 | all-reduce | flops 262144 | bytes 1572864 | tf_op jit(solution)/shard_map/psum | solution.py:75
  203.1 1.9 collective-permute-start.8
  205.1 7.2 %collective-permute-start.9 = (bf16[256,1024]{1,0:T(8,128)(2,1)S(1)}, bf16[256,1024]{1,0:T(8,128)(2,1)S(1)}, u32[]{:S(2)}, u32[]{:S(2)}) collective-permute-start(bf16[256,1024]{1,0:T(8,128)(2,1)S(1)} %all-reduce.3), channel_id=1, source_target_pairs={{4,0},{8,4},{12,8},{16,12},{20,16},{24,20},{28,24},{32,28},{36,32}... | collective-permute-start | bytes 1572872 | tf_op jit(solution)/shard_map/ppermute | solution.py:22
  212.2 4.7 %collective-permute-done.8 = bf16[256,1024]{1,0:T(8,128)(2,1)S(1)} collective-permute-done((bf16[256,1024]{1,0:T(8,128)(2,1)S(1)}, bf16[256,1024]{1,0:T(8,128)(2,1)S(1)}, u32[]{:S(2)}, u32[]{:S(2)}) %collective-permute-start.8) | collective-permute-done | bytes 524320 | tf_op jit(solution)/shard_map/ppermute | solution.py:21
  216.9 1.8 collective-permute-done.9
  225.8 1.5 copy-done.20
  227.3 1.2 bitcast_dynamic-update-slice_fusion
  (141 shorter events, 42.4 us)
Async XLA Ops:
  16.8 26.3 %collective-permute-start = (bf16[256,1024]{1,0:T(8,128)(2,1)S(1)}, bf16[256,1024]{1,0:T(8,128)(2,1)}, u32[]{:S(2)}, u32[]{:S(2)}) collective-permute-start(bf16[256,1024]{1,0:T(8,128)(2,1)S(1)} %all_gather.3), channel_id=1, source_target_pairs={{0,4},{4,8},{8,12},{12,16},{16,20},{20,24},{24,28},{28,32},{32,36}... | collective-permute-start | bytes 1572872 | tf_op jit(solution)/shard_map/ppermute | solution.py:21
  18.7 25.5 %collective-permute-start.1 = (bf16[256,1024]{1,0:T(8,128)(2,1)S(1)}, bf16[256,1024]{1,0:T(8,128)(2,1)}, u32[]{:S(2)}, u32[]{:S(2)}) collective-permute-start(bf16[256,1024]{1,0:T(8,128)(2,1)S(1)} %all_gather.3), channel_id=1, source_target_pairs={{4,0},{8,4},{12,8},{16,12},{20,16},{24,20},{28,24},{32,28},{36,32}... | collective-permute-start | bytes 1572872 | tf_op jit(solution)/shard_map/ppermute | solution.py:22
  40.3 2.1 copy-start.19
  56.7 19.4 %collective-permute-start.2 = (f32[256,1024]{1,0:T(8,128)S(1)}, f32[256,1024]{1,0:T(8,128)S(1)}, u32[]{:S(2)}, u32[]{:S(2)}) collective-permute-start(f32[256,1024]{1,0:T(8,128)S(1)} %get-tuple-element.7), channel_id=1, source_target_pairs={{0,4},{4,8},{8,12},{12,16},{16,20},{20,24},{24,28},{28,32},{32,36}... | collective-permute-start | bytes 3145736 | tf_op jit(solution)/shard_map/ppermute | solution.py:21
  58.6 19.3 %collective-permute-start.3 = (f32[256,1024]{1,0:T(8,128)S(1)}, f32[256,1024]{1,0:T(8,128)S(1)}, u32[]{:S(2)}, u32[]{:S(2)}) collective-permute-start(f32[256,1024]{1,0:T(8,128)S(1)} %get-tuple-element.8), channel_id=1, source_target_pairs={{4,0},{8,4},{12,8},{16,12},{20,16},{24,20},{28,24},{32,28},{36,32}... | collective-permute-start | bytes 3145736 | tf_op jit(solution)/shard_map/ppermute | solution.py:22
  106.9 22.9 %collective-permute-start.4 = (bf16[256,1024]{1,0:T(8,128)(2,1)S(1)}, bf16[256,1024]{1,0:T(8,128)(2,1)S(1)}, u32[]{:S(2)}, u32[]{:S(2)}) collective-permute-start(bf16[256,1024]{1,0:T(8,128)(2,1)S(1)} %all-reduce.2), channel_id=1, source_target_pairs={{0,4},{4,8},{8,12},{12,16},{16,20},{20,24},{24,28},{28,32},{32,36}... | collective-permute-start | bytes 1572872 | tf_op jit(solution)/shard_map/ppermute | solution.py:21
  108.8 21.0 %collective-permute-start.5 = (bf16[256,1024]{1,0:T(8,128)(2,1)S(1)}, bf16[256,1024]{1,0:T(8,128)(2,1)S(1)}, u32[]{:S(2)}, u32[]{:S(2)}) collective-permute-start(bf16[256,1024]{1,0:T(8,128)(2,1)S(1)} %all-reduce.2), channel_id=1, source_target_pairs={{4,0},{8,4},{12,8},{16,12},{20,16},{24,20},{28,24},{32,28},{36,32}... | collective-permute-start | bytes 1572872 | tf_op jit(solution)/shard_map/ppermute | solution.py:22
  131.1 1.7 copy-start
  135.3 1.6 copy-start.3
  136.9 1.6 copy-start.5
  138.4 1.7 copy-start.7
  140.1 1.5 copy-start.9
  141.7 1.7 copy-start.11
  143.3 1.6 copy-start.13
  144.9 1.5 copy-start.15
  146.5 1.6 copy-start.17
  149.9 19.4 %collective-permute-start.6 = (f32[256,1024]{1,0:T(8,128)S(1)}, f32[256,1024]{1,0:T(8,128)S(1)}, u32[]{:S(2)}, u32[]{:S(2)}) collective-permute-start(f32[256,1024]{1,0:T(8,128)S(1)} %get-tuple-element.5), channel_id=1, source_target_pairs={{0,4},{4,8},{8,12},{12,16},{16,20},{20,24},{24,28},{28,32},{32,36}... | collective-permute-start | bytes 3145736 | tf_op jit(solution)/shard_map/ppermute | solution.py:21
  151.9 19.3 %collective-permute-start.7 = (f32[256,1024]{1,0:T(8,128)S(1)}, f32[256,1024]{1,0:T(8,128)S(1)}, u32[]{:S(2)}, u32[]{:S(2)}) collective-permute-start(f32[256,1024]{1,0:T(8,128)S(1)} %get-tuple-element.6), channel_id=1, source_target_pairs={{4,0},{8,4},{12,8},{16,12},{20,16},{24,20},{28,24},{32,28},{36,32}... | collective-permute-start | bytes 3145736 | tf_op jit(solution)/shard_map/ppermute | solution.py:22
  203.1 13.8 %collective-permute-start.8 = (bf16[256,1024]{1,0:T(8,128)(2,1)S(1)}, bf16[256,1024]{1,0:T(8,128)(2,1)S(1)}, u32[]{:S(2)}, u32[]{:S(2)}) collective-permute-start(bf16[256,1024]{1,0:T(8,128)(2,1)S(1)} %all-reduce.3), channel_id=1, source_target_pairs={{0,4},{4,8},{8,12},{12,16},{16,20},{20,24},{24,28},{28,32},{32,36}... | collective-permute-start | bytes 1572872 | tf_op jit(solution)/shard_map/ppermute | solution.py:21
  205.1 13.6 %collective-permute-start.9 = (bf16[256,1024]{1,0:T(8,128)(2,1)S(1)}, bf16[256,1024]{1,0:T(8,128)(2,1)S(1)}, u32[]{:S(2)}, u32[]{:S(2)}) collective-permute-start(bf16[256,1024]{1,0:T(8,128)(2,1)S(1)} %all-reduce.3), channel_id=1, source_target_pairs={{4,0},{8,4},{12,8},{16,12},{20,16},{24,20},{28,24},{32,28},{36,32}... | collective-permute-start | bytes 1572872 | tf_op jit(solution)/shard_map/ppermute | solution.py:22
  220.4 1.2 copy-start.4
  220.9 1.3 copy-start.6
  224.8 2.5 %copy-start.2 = (f32[128,512]{1,0:T(8,128)S(1)}, f32[128,512]{1,0:T(8,128)}, u32[]{:S(2)}) copy-start(f32[128,512]{1,0:T(8,128)} %copy-done.1) | copy-start | bytes 786436
  225.8 1.5 copy-start.20
  (7 other events, 6.9 us)
where the time goes:
time: 230 us; the launch traced here: 228 us
  blocking collectives  77.2 us (34%)
  starting transfers between devices  44.8 us (19%)
  matrix products  36.4 us (16%)
  waiting for transfers between devices  31.1 us (14%)
  between operations  26.3 us (11%)
  local copies, waits for them, and re-layouts  9.34 us (4%)
  other arithmetic  3.42 us (1%)
    psum x2, blocking collectives, shards(): summed = lax.psum(partial_value, 'samp')  60.4 us
    ppermute x5, starting transfers between devices, with_halo(): after = lax.ppermute(leading, axis, down)  35.2 us
    ppermute x5, waiting for transfers between devices, with_halo(): before = lax.ppermute(last, axis, up)  25.8 us
    dot_general x20, matrix products, shards(): lax.dot_general(col_block, rows_low, contract_cols, preferred_element_typ...  17 us
    all_gather x1, blocking collectives, shards(): full_rows = lax.all_gather(samples, 'samp', axis=0, tiled=True)  16.8 us
    dot_general x20, matrix products, shards(): lax.dot_general(product_rows, sample_cols, contract_rows, preferred_eleme...  10.6 us
    ppermute x5, starting transfers between devices, with_halo(): before = lax.ppermute(last, axis, up)  9.59 us
    ppermute x5, waiting for transfers between devices, with_halo(): after = lax.ppermute(leading, axis, down)  5.27 us
  transfers between devices with their start and end apart: 10, of which 6 were waited for; matrix products, arithmetic and copies ran while one was open for 3% of the time, Pallas kernels for 0%

commit v1 on v0

v1 whole, which is shorter than its diff:
```python
import functools

import jax
import jax.numpy as jnp
from jax import lax
from jax.experimental import pallas as pl
from jax.experimental.pallas import tpu as pltpu
from jax.sharding import PartitionSpec as P

BLK_DEV = 2
step_size = 0.25
penalty = 0.2

VMEM = pl.BlockSpec(memory_space=pltpu.VMEM)
SMEM = pl.BlockSpec(memory_space=pltpu.SMEM)


def dot_nn(a, b):
    return jnp.dot(a, b, preferred_element_type=jnp.float32)


def dot_nt(a, b):
    return lax.dot_general(a, b, (((1,), (1,)), ((), ())), preferred_element_type=jnp.float32)


def shrink(value):
    level = step_size * penalty
    return value - jnp.clip(value, -level, level)


def position(coords, slot, side, first, blocks):
    at = coords[slot, side] - first
    at = jnp.where(at < 0, at + blocks, at)
    return jnp.where(at >= blocks, at - blocks, at)


def transpose_kernel(x_ref, o_ref):
    o_ref[...] = x_ref[...].T


def fill_samples(st, before, own, after):
    width = st.shape[1]
    for side, ref in enumerate((before, own, after)):
        for blk in range(BLK_DEV):
            st[side * BLK_DEV + blk] = ref[pl.ds(blk * width, width), :]


def fill_products(pt, before, own, after):
    rows = own.shape[1] // BLK_DEV
    for side, ref in enumerate((before, own, after)):
        for blk in range(BLK_DEV):
            for part in range(own.shape[0]):
                pt[side * BLK_DEV + blk, pl.ds(part * rows, rows), :] = ref[part, pl.ds(blk * rows, rows), :]


def put_totals(acc, down_ref, own_ref, up_ref):
    rows = acc.shape[1]
    for blk in range(BLK_DEV):
        at = pl.ds(blk * rows, rows)
        down_ref[at, :] = acc[blk].astype(jnp.bfloat16)
        own_ref[at, :] = acc[BLK_DEV + blk]
        up_ref[at, :] = acc[2 * BLK_DEV + blk].astype(jnp.bfloat16)


def first_kernel(blocks, coords, omega, parts, before, own, after, down_ref, own_ref, up_ref, ct_ref, st, acc):
    first = (lax.axis_index("tiles") - 1) * BLK_DEV
    tiles, rows, width = omega.shape
    fill_samples(st, before, own, after)
    acc[...] = jnp.zeros_like(acc)
    for slot in range(BLK_DEV):
        at = BLK_DEV + slot
        acc[at] = dot_nn(omega[slot].astype(jnp.bfloat16), st[at])

    def step(slot, carry):
        row = position(coords, slot, 0, first, blocks)
        col = position(coords, slot, 1, first, blocks)
        side = slot - BLK_DEV
        for part in range(width // rows):
            ct_ref[side, :, pl.ds(part * rows, rows)] = parts[part, side].T
        acc[row] += dot_nn(omega[slot].astype(jnp.bfloat16), st[col])
        acc[col] += dot_nn(ct_ref[side], st[row])
        return carry

    lax.fori_loop(BLK_DEV, tiles, step, 0)
    put_totals(acc, down_ref, own_ref, up_ref)


def gradient(pt, st, row, col, here):
    return dot_nt(pt[row, here, :], st[col]) + dot_nt(st[row, here, :], pt[col])


def diagonal(value, quarter):
    rows, width = value.shape
    row_ids = quarter * rows + lax.broadcasted_iota(jnp.int32, (rows, width), 0)
    col_ids = lax.broadcasted_iota(jnp.int32, (rows, width), 1)
    positive = 0.5 * (value + jnp.sqrt(value * value + 4.0 * step_size))
    return jnp.where(row_ids == col_ids, positive, shrink(value))


def middle_kernel(
    blocks, coords, omega, ct_ref, before, own, after, p_before, p_own, p_after,
    new_ref, down_ref, own_ref, up_ref, st, pt, acc,
):
    first = (lax.axis_index("tiles") - 1) * BLK_DEV
    quarter = lax.axis_index("samp")
    tiles, rows, width = omega.shape
    scale = step_size / (2.0 * st.shape[2])
    here = pl.ds(pl.multiple_of(quarter * rows, rows), rows)
    fill_samples(st, before, own, after)
    fill_products(pt, p_before, p_own, p_after)
    acc[...] = jnp.zeros_like(acc)
    for slot in range(BLK_DEV):
        at = BLK_DEV + slot
        tile = diagonal(omega[slot] - scale * gradient(pt, st, at, at, here), quarter)
        new_ref[slot] = tile
        acc[at] = dot_nn(tile.astype(jnp.bfloat16), st[at])

    def step(slot, carry):
        row = position(coords, slot, 0, first, blocks)
        col = position(coords, slot, 1, first, blocks)
        tile = shrink(omega[slot] - scale * gradient(pt, st, row, col, here))
        new_ref[slot] = tile
        acc[row] += dot_nn(tile.astype(jnp.bfloat16), st[col])
        held = ct_ref[slot - BLK_DEV].astype(jnp.float32)
        turned = shrink(held - scale * gradient(pt, st, col, row, here))
        acc[col] += dot_nn(turned.astype(jnp.bfloat16), st[row])
        return carry

    lax.fori_loop(BLK_DEV, tiles, step, 0)
    put_totals(acc, down_ref, own_ref, up_ref)


def last_kernel(blocks, coords, omega, before, own, after, p_before, p_own, p_after, new_ref, st, pt):
    first = (lax.axis_index("tiles") - 1) * BLK_DEV
    quarter = lax.axis_index("samp")
    tiles, rows, width = omega.shape
    scale = step_size / (2.0 * st.shape[2])
    here = pl.ds(pl.multiple_of(quarter * rows, rows), rows)
    fill_samples(st, before, own, after)
    fill_products(pt, p_before, p_own, p_after)
    for slot in range(BLK_DEV):
        at = BLK_DEV + slot
        new_ref[slot] = diagonal(omega[slot] - scale * gradient(pt, st, at, at, here), quarter)

    def step(slot, carry):
        row = position(coords, slot, 0, first, blocks)
        col = position(coords, slot, 1, first, blocks)
        new_ref[slot] = shrink(omega[slot] - scale * gradient(pt, st, row, col, here))
        return carry

    lax.fori_loop(BLK_DEV, tiles, step, 0)


def shards(samples, omega, coords):
    size = lax.axis_size("tiles")
    parts = lax.axis_size("samp")
    blocks = BLK_DEV * size
    tiles, rows, width = omega.shape
    others = tiles - BLK_DEV
    count = samples.shape[0] * parts
    own_width = samples.shape[1]
    up = [(i, (i + 1) % size) for i in range(size)]
    down = [(j, i) for i, j in up]
    bf16, f32 = jnp.bfloat16, jnp.float32

    def around(x):
        return lax.ppermute(x, "tiles", up), lax.ppermute(x, "tiles", down)

    gathered = lax.all_gather(samples, "samp", axis=0, tiled=True)
    st_own = pl.pallas_call(
        transpose_kernel, out_shape=jax.ShapeDtypeStruct((own_width, count), bf16),
        in_specs=[VMEM], out_specs=VMEM,
    )(gathered)
    st_before, st_after = around(st_own)
    pieces = omega[BLK_DEV:].astype(bf16).reshape(others, rows, parts, rows).transpose(2, 0, 1, 3)
    turned = lax.all_to_all(pieces, "samp", 0, 0)
    part_rows = BLK_DEV * rows
    half = jax.ShapeDtypeStruct((part_rows, count), bf16)
    whole = jax.ShapeDtypeStruct((part_rows, count), f32)
    st_scratch = pltpu.VMEM((3 * BLK_DEV, width, count), bf16)
    acc_scratch = pltpu.VMEM((3 * BLK_DEV, rows, count), f32)
    params = pltpu.CompilerParams(vmem_limit_bytes=48 << 20)
    down_part, own_part, up_part, ct = pl.pallas_call(
        functools.partial(first_kernel, blocks),
        out_shape=(half, whole, half, jax.ShapeDtypeStruct((others, rows, width), bf16)),
        in_specs=[SMEM] + [VMEM] * 5, out_specs=(VMEM,) * 4,
        scratch_shapes=[st_scratch, acc_scratch], compiler_params=params,
    )(coords, omega, turned, st_before, st_own, st_after)

    def products(down_part, own_part, up_part):
        from_before = lax.ppermute(up_part, "tiles", up)
        from_after = lax.ppermute(down_part, "tiles", down)
        total = own_part + from_before.astype(f32) + from_after.astype(f32)
        p_own = lax.all_gather(total.astype(bf16), "samp", axis=0, tiled=False)
        p_before, p_after = around(p_own)
        return p_before, p_own, p_after

    p = products(down_part, own_part, up_part)
    tile_shape = jax.ShapeDtypeStruct(omega.shape, f32)
    omega, down_part, own_part, up_part = pl.pallas_call(
        functools.partial(middle_kernel, blocks),
        out_shape=(tile_shape, half, whole, half),
        in_specs=[SMEM] + [VMEM] * 8, out_specs=(VMEM,) * 4,
        scratch_shapes=[st_scratch, st_scratch, acc_scratch], compiler_params=params,
    )(coords, omega, ct, st_before, st_own, st_after, *p)
    p = products(down_part, own_part, up_part)
    return pl.pallas_call(
        functools.partial(last_kernel, blocks),
        out_shape=tile_shape,
        in_specs=[SMEM] + [VMEM] * 7, out_specs=VMEM,
        scratch_shapes=[st_scratch, st_scratch], compiler_params=params,
    )(coords, omega, st_before, st_own, st_after, *p)


def solution(mesh):
    in_specs = (P("samp", "tiles"), P("tiles", "samp", None), P("tiles", None))
    out_specs = P("tiles", "samp", None)
    return jax.shard_map(shards, mesh=mesh, in_specs=in_specs, out_specs=out_specs, check_vma=False)
```

time: 230 us -> 165 us (0.72)
  the two profiles are of different devices: /device:TPU:4 before, /device:TPU:2 now
where the time goes in v1:
time: 165 us; the launch traced here: 164 us
  starting transfers between devices  51 us (31%)
  blocking collectives  43.7 us (26%)
  waiting for transfers between devices  40.8 us (25%)
  Pallas kernels  21.8 us (13%)
  local copies, waits for them, and re-layouts  6.59 us (4%)
    ppermute x6, waiting for transfers between devices, around(): return (lax.ppermute(x, 'tiles', up), lax.ppermute(x, 'tiles', down))  35.8 us
    all_gather x2, blocking collectives, products(): p_own = lax.all_gather(total.astype(bf16), 'samp', axis=0, tiled=False)  25.6 us
    ppermute x6, starting transfers between devices, around(): return (lax.ppermute(x, 'tiles', up), lax.ppermute(x, 'tiles', down))  23.9 us
    all_gather x1, blocking collectives, shards(): gathered = lax.all_gather(samples, 'samp', axis=0, tiled=True)  18.1 us
    ppermute x2, starting transfers between devices, products(): from_after = lax.ppermute(down_part, 'tiles', down)  13.9 us
    pallas_call x1, Pallas kernels, shards(): pl.pallas_call(functools.partial(middle_kernel, blocks), out_shape=(tile_...  9.99 us
    all_to_all x1, starting transfers between devices, shards(): turned = lax.all_to_all(pieces, 'samp', 0, 0)  9.36 us
    pallas_call x1, Pallas kernels, shards(): pl.pallas_call(functools.partial(last_kernel, blocks), out_shape=tile_sha...  5.5 us
  transfers between devices with their start and end apart: 11, of which 10 were waited for; matrix products, arithmetic and copies ran while one was open for 0% of the time, Pallas kernels for 1%

profile of v1, /device:TPU:2, one launch (start us, length us, event | category | flops | bytes accessed | tf_op | source)
XLA Modules:
  0.0 164.1 jit_solution(3682090577059720059)
XLA Ops:
  3.7 9.4 %all-to-all-start = ((bf16[4,8,128,128]{3,2,1,0:T(8,128)(2,1)}), bf16[4,8,128,128]{3,2,1,0:T(8,128)(2,1)S(1)}, u32[]{:S(2)}, u32[]{:S(2)}) async-start(bf16[4,8,128,128]{3,2,1,0:T(8,128)(2,1)} %bitcast.1), calls=%async_computation | async-start | bytes 2097152 | tf_op jit(solution)/shard_map/all_to_all | solution.py:176
  13.1 18.1 %all_gather.15.x_ref = bf16[256,1024]{1,0:T(8,128)(2,1)} all-gather(bf16[64,1024]{1,0:T(8,128)(2,1)S(1)} %copy-done.3), channel_id=1, replica_groups=mesh['tiles'=128,'samp'=4] {'samp'}, dimensions={0}, use_global_device_ids=true | all-gather | bytes 655360 | tf_op jit(solution)/shard_map/all_gather | solution.py:169
  31.2 2.0 %shard_map.37.own = bf16[1024,256]{1,0:T(8,128)(2,1)} custom-call(bf16[256,1024]{1,0:T(8,128)(2,1)} %all_gather.15.x_ref), custom_call_target="tpu_custom_call" | custom-call | tf_op jit(solution)/shard_map/pallas_call | solution.py:170
  33.3 9.7 %collective-permute-start.1 = (bf16[1024,256]{1,0:T(8,128)(2,1)}, bf16[1024,256]{1,0:T(8,128)(2,1)S(1)}, u32[]{:S(2)}, u32[]{:S(2)}) collective-permute-start(bf16[1024,256]{1,0:T(8,128)(2,1)} %shard_map.37.own), channel_id=1, source_target_pairs={{4,0},{8,4},{12,8},{16,12},{20,16},{24,20},{28,24},{32,28},{36,32}... | collective-permute-start | bytes 1572872 | tf_op jit(solution)/shard_map/ppermute | solution.py:167
  43.0 1.9 %collective-permute-start = (bf16[1024,256]{1,0:T(8,128)(2,1)}, bf16[1024,256]{1,0:T(8,128)(2,1)S(1)}, u32[]{:S(2)}, u32[]{:S(2)}) collective-permute-start(bf16[1024,256]{1,0:T(8,128)(2,1)} %shard_map.37.own), channel_id=1, source_target_pairs={{0,4},{4,8},{8,12},{12,16},{16,20},{20,24},{24,28},{28,32},{32,36}... | collective-permute-start | bytes 1572872 | tf_op jit(solution)/shard_map/ppermute | solution.py:167
  45.0 5.0 %collective-permute-done.1.after = bf16[1024,256]{1,0:T(8,128)(2,1)S(1)} collective-permute-done((bf16[1024,256]{1,0:T(8,128)(2,1)}, bf16[1024,256]{1,0:T(8,128)(2,1)S(1)}, u32[]{:S(2)}, u32[]{:S(2)}) %collective-permute-start.1) | collective-permute-done | bytes 524320 | tf_op jit(solution)/shard_map/ppermute | solution.py:167
  50.0 7.0 %collective-permute-done.before = bf16[1024,256]{1,0:T(8,128)(2,1)S(1)} collective-permute-done((bf16[1024,256]{1,0:T(8,128)(2,1)}, bf16[1024,256]{1,0:T(8,128)(2,1)S(1)}, u32[]{:S(2)}, u32[]{:S(2)}) %collective-permute-start) | collective-permute-done | bytes 524320 | tf_op jit(solution)/shard_map/ppermute | solution.py:167
  58.1 4.2 %shard_map.38 = (bf16[256,256]{1,0:T(8,128)(2,1)S(1)}, f32[256,256]{1,0:T(8,128)S(1)}, bf16[256,256]{1,0:T(8,128)(2,1)S(1)}, bf16[8,128,512]{2,1,0:T(8,128)(2,1)S(1)}) custom-call(s32[10,2]{1,0:T(8,128)S(1)} %copy.11.coords, f32[10,128,512]{2,1,0:T(8,128)} %omega.3, bf16[4,8,128,128]{3,2,1,0:T(8,128)(2,1)S(1)} %all-to-all-done.parts, ...), custom_call_target="tpu_custom_call" | custom-call | tf_op jit(solution)/shard_map/pallas_call | solution.py:183
  62.3 1.9 %collective-permute-start.2 = (bf16[256,256]{1,0:T(8,128)(2,1)S(1)}, bf16[256,256]{1,0:T(8,128)(2,1)S(1)}, u32[]{:S(2)}, u32[]{:S(2)}) collective-permute-start(bf16[256,256]{1,0:T(8,128)(2,1)S(1)} %get-tuple-element.15), channel_id=1, source_target_pairs={{0,4},{4,8},{8,12},{12,16},{16,20},{20,24},{24,28},{28,32},{32,36}... | collective-permute-start | bytes 393224 | tf_op jit(solution)/shard_map/ppermute | solution.py:191
  64.2 7.0 %collective-permute-start.3 = (bf16[256,256]{1,0:T(8,128)(2,1)S(1)}, bf16[256,256]{1,0:T(8,128)(2,1)S(1)}, u32[]{:S(2)}, u32[]{:S(2)}) collective-permute-start(bf16[256,256]{1,0:T(8,128)(2,1)S(1)} %get-tuple-element.16), channel_id=1, source_target_pairs={{4,0},{8,4},{12,8},{16,12},{20,16},{24,20},{28,24},{32,28},{36,32}... | collective-permute-start | bytes 393224 | tf_op jit(solution)/shard_map/ppermute | solution.py:192
  73.8 12.8 %all-gather = bf16[1024,256]{1,0:T(8,128)(2,1)S(1)} all-gather(bf16[256,256]{1,0:T(8,128)(2,1)S(1)} %add_convert_fusion.1), channel_id=2, replica_groups=mesh['tiles'=128,'samp'=4] {'samp'}, dimensions={0}, use_global_device_ids=true | all-gather | bytes 655360 | tf_op jit(solution)/shard_map/all_gather | solution.py:194
  86.5 4.2 %collective-permute-start.5 = (bf16[4,256,256]{2,1,0:T(8,128)(2,1)S(1)}, bf16[4,256,256]{2,1,0:T(8,128)(2,1)S(1)}, u32[]{:S(2)}, u32[]{:S(2)}) collective-permute-start(bf16[4,256,256]{2,1,0:T(8,128)(2,1)S(1)} %bitcast.7), channel_id=1, source_target_pairs={{4,0},{8,4},{12,8},{16,12},{20,16},{24,20},{28,24},{32,28},{36,32}... | collective-permute-start | bytes 1572872 | tf_op jit(solution)/shard_map/ppermute | solution.py:167
  90.7 1.9 %collective-permute-start.4 = (bf16[4,256,256]{2,1,0:T(8,128)(2,1)S(1)}, bf16[4,256,256]{2,1,0:T(8,128)(2,1)S(1)}, u32[]{:S(2)}, u32[]{:S(2)}) collective-permute-start(bf16[4,256,256]{2,1,0:T(8,128)(2,1)S(1)} %bitcast.8), channel_id=1, source_target_pairs={{0,4},{4,8},{8,12},{12,16},{16,20},{20,24},{24,28},{28,32},{32,36}... | collective-permute-start | bytes 1572872 | tf_op jit(solution)/shard_map/ppermute | solution.py:167
  92.7 4.7 %collective-permute-done.5.p_after = bf16[4,256,256]{2,1,0:T(8,128)(2,1)S(1)} collective-permute-done((bf16[4,256,256]{2,1,0:T(8,128)(2,1)S(1)}, bf16[4,256,256]{2,1,0:T(8,128)(2,1)S(1)}, u32[]{:S(2)}, u32[]{:S(2)}) %collective-permute-start.5) | collective-permute-done | bytes 524320 | tf_op jit(solution)/shard_map/ppermute | solution.py:167
  97.4 7.1 %collective-permute-done.4.p_before = bf16[4,256,256]{2,1,0:T(8,128)(2,1)S(1)} collective-permute-done((bf16[4,256,256]{2,1,0:T(8,128)(2,1)S(1)}, bf16[4,256,256]{2,1,0:T(8,128)(2,1)S(1)}, u32[]{:S(2)}, u32[]{:S(2)}) %collective-permute-start.4) | collective-permute-done | bytes 524320 | tf_op jit(solution)/shard_map/ppermute | solution.py:167
  104.6 10.0 %shard_map.39 = (f32[10,128,512]{2,1,0:T(8,128)}, bf16[256,256]{1,0:T(8,128)(2,1)S(1)}, f32[256,256]{1,0:T(8,128)S(1)}, bf16[256,256]{1,0:T(8,128)(2,1)S(1)}) custom-call(s32[10,2]{1,0:T(8,128)S(1)} %copy.11.coords, f32[10,128,512]{2,1,0:T(8,128)} %omega.3, bf16[8,128,512]{2,1,0:T(8,128)(2,1)S(1)} %get-tuple-element.13.ct_ref, ...), custom_call_target="tpu_custom_call" | custom-call | tf_op jit(solution)/shard_map/pallas_call | solution.py:200
  114.6 1.9 %collective-permute-start.6 = (bf16[256,256]{1,0:T(8,128)(2,1)S(1)}, bf16[256,256]{1,0:T(8,128)(2,1)S(1)}, u32[]{:S(2)}, u32[]{:S(2)}) collective-permute-start(bf16[256,256]{1,0:T(8,128)(2,1)S(1)} %get-tuple-element.19), channel_id=1, source_target_pairs={{0,4},{4,8},{8,12},{12,16},{16,20},{20,24},{24,28},{28,32},{32,36}... | collective-permute-start | bytes 393224 | tf_op jit(solution)/shard_map/ppermute | solution.py:191
  116.5 7.0 %collective-permute-start.7 = (bf16[256,256]{1,0:T(8,128)(2,1)S(1)}, bf16[256,256]{1,0:T(8,128)(2,1)S(1)}, u32[]{:S(2)}, u32[]{:S(2)}) collective-permute-start(bf16[256,256]{1,0:T(8,128)(2,1)S(1)} %get-tuple-element.20), channel_id=1, source_target_pairs={{4,0},{8,4},{12,8},{16,12},{20,16},{24,20},{28,24},{32,28},{36,32}... | collective-permute-start | bytes 393224 | tf_op jit(solution)/shard_map/ppermute | solution.py:192
  126.0 12.8 %all-gather.1 = bf16[1024,256]{1,0:T(8,128)(2,1)S(1)} all-gather(bf16[256,256]{1,0:T(8,128)(2,1)S(1)} %add_convert_fusion), channel_id=3, replica_groups=mesh['tiles'=128,'samp'=4] {'samp'}, dimensions={0}, use_global_device_ids=true | all-gather | bytes 655360 | tf_op jit(solution)/shard_map/all_gather | solution.py:194
  138.8 4.2 %collective-permute-start.9 = (bf16[4,256,256]{2,1,0:T(8,128)(2,1)S(1)}, bf16[4,256,256]{2,1,0:T(8,128)(2,1)S(1)}, u32[]{:S(2)}, u32[]{:S(2)}) collective-permute-start(bf16[4,256,256]{2,1,0:T(8,128)(2,1)S(1)} %bitcast.4), channel_id=1, source_target_pairs={{4,0},{8,4},{12,8},{16,12},{20,16},{24,20},{28,24},{32,28},{36,32}... | collective-permute-start | bytes 1572872 | tf_op jit(solution)/shard_map/ppermute | solution.py:167
  143.0 1.9 %collective-permute-start.8 = (bf16[4,256,256]{2,1,0:T(8,128)(2,1)S(1)}, bf16[4,256,256]{2,1,0:T(8,128)(2,1)S(1)}, u32[]{:S(2)}, u32[]{:S(2)}) collective-permute-start(bf16[4,256,256]{2,1,0:T(8,128)(2,1)S(1)} %bitcast.5), channel_id=1, source_target_pairs={{0,4},{4,8},{8,12},{12,16},{16,20},{20,24},{24,28},{28,32},{32,36}... | collective-permute-start | bytes 1572872 | tf_op jit(solution)/shard_map/ppermute | solution.py:167
  144.9 4.7 %collective-permute-done.9.p_after = bf16[4,256,256]{2,1,0:T(8,128)(2,1)S(1)} collective-permute-done((bf16[4,256,256]{2,1,0:T(8,128)(2,1)S(1)}, bf16[4,256,256]{2,1,0:T(8,128)(2,1)S(1)}, u32[]{:S(2)}, u32[]{:S(2)}) %collective-permute-start.9) | collective-permute-done | bytes 524320 | tf_op jit(solution)/shard_map/ppermute | solution.py:167
  149.7 7.1 %collective-permute-done.8.p_before = bf16[4,256,256]{2,1,0:T(8,128)(2,1)S(1)} collective-permute-done((bf16[4,256,256]{2,1,0:T(8,128)(2,1)S(1)}, bf16[4,256,256]{2,1,0:T(8,128)(2,1)S(1)}, u32[]{:S(2)}, u32[]{:S(2)}) %collective-permute-start.8) | collective-permute-done | bytes 524320 | tf_op jit(solution)/shard_map/ppermute | solution.py:167
  158.6 5.5 %shard_map.40 = f32[10,128,512]{2,1,0:T(8,128)} custom-call(s32[10,2]{1,0:T(8,128)S(1)} %copy.11.coords, f32[10,128,512]{2,1,0:T(8,128)S(1)} %copy-done.2, bf16[1024,256]{1,0:T(8,128)(2,1)S(1)} %collective-permute-done.before, bf16[1024,256]{1,0:T(8,128)(2,1)S(1)} %copy-done.1, bf16[1024,256]{1,0:T(8,128)(2,1)S(1)} %collective-permute-done.1.after, ...), custom_call_target="tpu_custom_call" | custom-call | tf_op jit(solution)/shard_map/pallas_call | solution.py:207
  (21 shorter events, 11.7 us)
Async XLA Ops:
  2.4 10.7 %copy-start.3 = (bf16[64,1024]{1,0:T(8,128)(2,1)S(1)}, bf16[64,1024]{1,0:T(8,128)(2,1)}, u32[]{:S(2)}) copy-start(bf16[64,1024]{1,0:T(8,128)(2,1)} %param.3) | copy-start | bytes 393220
  2.4 42.5 %copy-start.4 = (s32[10,2]{0,1:T(2,128)S(1)}, s32[10,2]{0,1:T(2,128)}, u32[]{:S(2)}) copy-start(s32[10,2]{0,1:T(2,128)} %param.5) | copy-start | bytes 244
  3.7 53.3 %all-to-all-start = ((bf16[4,8,128,128]{3,2,1,0:T(8,128)(2,1)}), bf16[4,8,128,128]{3,2,1,0:T(8,128)(2,1)S(1)}, u32[]{:S(2)}, u32[]{:S(2)}) async-start(bf16[4,8,128,128]{3,2,1,0:T(8,128)(2,1)} %bitcast.1), calls=%async_computation | async-start | bytes 2097152 | tf_op jit(solution)/shard_map/all_to_all | solution.py:176
  33.3 16.7 %collective-permute-start.1 = (bf16[1024,256]{1,0:T(8,128)(2,1)}, bf16[1024,256]{1,0:T(8,128)(2,1)S(1)}, u32[]{:S(2)}, u32[]{:S(2)}) collective-permute-start(bf16[1024,256]{1,0:T(8,128)(2,1)} %shard_map.37.own), channel_id=1, source_target_pairs={{4,0},{8,4},{12,8},{16,12},{20,16},{24,20},{28,24},{32,28},{36,32}... | collective-permute-start | bytes 1572872 | tf_op jit(solution)/shard_map/ppermute | solution.py:167
  43.0 14.0 %collective-permute-start = (bf16[1024,256]{1,0:T(8,128)(2,1)}, bf16[1024,256]{1,0:T(8,128)(2,1)S(1)}, u32[]{:S(2)}, u32[]{:S(2)}) collective-permute-start(bf16[1024,256]{1,0:T(8,128)(2,1)} %shard_map.37.own), channel_id=1, source_target_pairs={{0,4},{4,8},{8,12},{12,16},{16,20},{20,24},{24,28},{28,32},{32,36}... | collective-permute-start | bytes 1572872 | tf_op jit(solution)/shard_map/ppermute | solution.py:167
  57.0 1.0 copy-start
  58.1 46.5 %copy-start.1 = (bf16[1024,256]{1,0:T(8,128)(2,1)S(1)}, bf16[1024,256]{1,0:T(8,128)(2,1)}, u32[]{:S(2)}) copy-start(bf16[1024,256]{1,0:T(8,128)(2,1)} %shard_map.37.own) | copy-start | bytes 1572868
  62.3 9.6 %collective-permute-start.2 = (bf16[256,256]{1,0:T(8,128)(2,1)S(1)}, bf16[256,256]{1,0:T(8,128)(2,1)S(1)}, u32[]{:S(2)}, u32[]{:S(2)}) collective-permute-start(bf16[256,256]{1,0:T(8,128)(2,1)S(1)} %get-tuple-element.15), channel_id=1, source_target_pairs={{0,4},{4,8},{8,12},{12,16},{16,20},{20,24},{24,28},{28,32},{32,36}... | collective-permute-start | bytes 393224 | tf_op jit(solution)/shard_map/ppermute | solution.py:191
  64.2 9.5 %collective-permute-start.3 = (bf16[256,256]{1,0:T(8,128)(2,1)S(1)}, bf16[256,256]{1,0:T(8,128)(2,1)S(1)}, u32[]{:S(2)}, u32[]{:S(2)}) collective-permute-start(bf16[256,256]{1,0:T(8,128)(2,1)S(1)} %get-tuple-element.16), channel_id=1, source_target_pairs={{4,0},{8,4},{12,8},{16,12},{20,16},{24,20},{28,24},{32,28},{36,32}... | collective-permute-start | bytes 393224 | tf_op jit(solution)/shard_map/ppermute | solution.py:192
  86.5 10.9 %collective-permute-start.5 = (bf16[4,256,256]{2,1,0:T(8,128)(2,1)S(1)}, bf16[4,256,256]{2,1,0:T(8,128)(2,1)S(1)}, u32[]{:S(2)}, u32[]{:S(2)}) collective-permute-start(bf16[4,256,256]{2,1,0:T(8,128)(2,1)S(1)} %bitcast.7), channel_id=1, source_target_pairs={{4,0},{8,4},{12,8},{16,12},{20,16},{24,20},{28,24},{32,28},{36,32}... | collective-permute-start | bytes 1572872 | tf_op jit(solution)/shard_map/ppermute | solution.py:167
  90.7 13.8 %collective-permute-start.4 = (bf16[4,256,256]{2,1,0:T(8,128)(2,1)S(1)}, bf16[4,256,256]{2,1,0:T(8,128)(2,1)S(1)}, u32[]{:S(2)}, u32[]{:S(2)}) collective-permute-start(bf16[4,256,256]{2,1,0:T(8,128)(2,1)S(1)} %bitcast.8), channel_id=1, source_target_pairs={{0,4},{4,8},{8,12},{12,16},{16,20},{20,24},{24,28},{28,32},{32,36}... | collective-permute-start | bytes 1572872 | tf_op jit(solution)/shard_map/ppermute | solution.py:167
  114.6 9.6 %collective-permute-start.6 = (bf16[256,256]{1,0:T(8,128)(2,1)S(1)}, bf16[256,256]{1,0:T(8,128)(2,1)S(1)}, u32[]{:S(2)}, u32[]{:S(2)}) collective-permute-start(bf16[256,256]{1,0:T(8,128)(2,1)S(1)} %get-tuple-element.19), channel_id=1, source_target_pairs={{0,4},{4,8},{8,12},{12,16},{16,20},{20,24},{24,28},{28,32},{32,36}... | collective-permute-start | bytes 393224 | tf_op jit(solution)/shard_map/ppermute | solution.py:191
  116.5 9.5 %collective-permute-start.7 = (bf16[256,256]{1,0:T(8,128)(2,1)S(1)}, bf16[256,256]{1,0:T(8,128)(2,1)S(1)}, u32[]{:S(2)}, u32[]{:S(2)}) collective-permute-start(bf16[256,256]{1,0:T(8,128)(2,1)S(1)} %get-tuple-element.20), channel_id=1, source_target_pairs={{4,0},{8,4},{12,8},{16,12},{20,16},{24,20},{28,24},{32,28},{36,32}... | collective-permute-start | bytes 393224 | tf_op jit(solution)/shard_map/ppermute | solution.py:192
  138.8 10.9 %collective-permute-start.9 = (bf16[4,256,256]{2,1,0:T(8,128)(2,1)S(1)}, bf16[4,256,256]{2,1,0:T(8,128)(2,1)S(1)}, u32[]{:S(2)}, u32[]{:S(2)}) collective-permute-start(bf16[4,256,256]{2,1,0:T(8,128)(2,1)S(1)} %bitcast.4), channel_id=1, source_target_pairs={{4,0},{8,4},{12,8},{16,12},{20,16},{24,20},{28,24},{32,28},{36,32}... | collective-permute-start | bytes 1572872 | tf_op jit(solution)/shard_map/ppermute | solution.py:167
  143.0 13.8 %collective-permute-start.8 = (bf16[4,256,256]{2,1,0:T(8,128)(2,1)S(1)}, bf16[4,256,256]{2,1,0:T(8,128)(2,1)S(1)}, u32[]{:S(2)}, u32[]{:S(2)}) collective-permute-start(bf16[4,256,256]{2,1,0:T(8,128)(2,1)S(1)} %bitcast.5), channel_id=1, source_target_pairs={{0,4},{4,8},{8,12},{12,16},{16,20},{20,24},{24,28},{28,32},{32,36}... | collective-permute-start | bytes 1572872 | tf_op jit(solution)/shard_map/ppermute | solution.py:167
  156.8 1.7 %copy-start.2 = (f32[10,128,512]{2,1,0:T(8,128)S(1)}, f32[10,128,512]{2,1,0:T(8,128)}, u32[]{:S(2)}) copy-start(f32[10,128,512]{2,1,0:T(8,128)} %get-tuple-element.17.omega) | copy-start | bytes 7864324

commit v2 on v0

v2 whole, which is shorter than its diff:
```python
import functools

import jax
import jax.numpy as jnp
from jax import lax
from jax.experimental import pallas as pl
from jax.experimental.pallas import tpu as pltpu
from jax.sharding import PartitionSpec as P


BLK_DEV = 2
step_size = 0.25
penalty = 0.2

VMEM = pl.BlockSpec(memory_space=pltpu.VMEM)
SMEM = pl.BlockSpec(memory_space=pltpu.SMEM)
ANY = pl.BlockSpec(memory_space=pl.ANY)
bf16, f32 = jnp.bfloat16, jnp.float32

OWN_PAIR = 8
LIMIT = 12 << 20


def dot_nn(a, b):
    return jnp.dot(a, b, preferred_element_type=f32)


def dot_nt(a, b):
    return lax.dot_general(a, b, (((1,), (1,)), ((), ())), preferred_element_type=f32)


def shrink(value):
    level = step_size * penalty
    return value - jnp.clip(value, -level, level)


def shrink_diagonal(value, quarter):
    rows, width = value.shape
    row_ids = quarter * rows + lax.broadcasted_iota(jnp.int32, (rows, width), 0)
    col_ids = lax.broadcasted_iota(jnp.int32, (rows, width), 1)
    positive = 0.5 * (value + jnp.sqrt(value * value + 4.0 * step_size))
    return jnp.where(row_ids == col_ids, positive, shrink(value))


def find_slots(blocks, coords, slot_of):
    first = (lax.axis_index("tiles") - 1) * BLK_DEV
    for pair in range(OWN_PAIR + 1):
        slot_of[pair] = 0

    def place(slot, side):
        at = coords[slot, side] - first
        at = jnp.where(at < 0, at + blocks, at)
        return jnp.where(at >= blocks, at - blocks, at)

    for slot in range(BLK_DEV, coords.shape[0]):
        row, col = place(slot, 0), place(slot, 1)
        pair = jnp.where(col >= 2 * BLK_DEV, (col - 2 * BLK_DEV) * 2 * BLK_DEV + row, OWN_PAIR)
        slot_of[pair] = slot


def is_even():
    return lax.rem(lax.axis_index("tiles"), 2) == 0


def cut_kernel(omega, gathered, out, held, sems):
    rows = omega.shape[1]
    copies = []
    for part in range(out.shape[0]):
        for slot in range(BLK_DEV, omega.shape[0]):
            held[part, slot - BLK_DEV] = omega[slot, :, part * rows : (part + 1) * rows].astype(bf16)
        copies.append(pltpu.make_async_copy(held.at[part], out.at[part], sems.at[part]))
        copies[-1].start()
    for copy in copies:
        copy.wait()


def rows_kernel(
    blocks, coords, omega, s_own, s_cross, s_chip,
    s_before, s_after, stq, t_before, t_own, slot_of, mats,
):
    rows, width = omega.shape[1:]
    quarter = lax.axis_index("samp")
    find_slots(blocks, coords, slot_of)

    @pl.when(is_even())
    def _():
        s_before[...] = s_cross[...]
        s_after[...] = s_chip[...]

    @pl.when(jnp.logical_not(is_even()))
    def _():
        s_before[...] = s_chip[...]
        s_after[...] = s_cross[...]

    for side, ref in enumerate((s_before, s_own, s_after)):
        for blk in range(BLK_DEV):
            at = pl.multiple_of(blk * width + quarter * rows, rows)
            stq[side, blk * rows : (blk + 1) * rows, :] = ref[:, pl.ds(at, rows)].T

    def convert(pair, carry):
        slot = slot_of[pair]

        @pl.when(slot > 0)
        def _():
            mats[pair] = omega[slot].astype(bf16)

        @pl.when(slot == 0)
        def _():
            mats[pair] = jnp.zeros_like(mats[pair])

        return carry

    lax.fori_loop(0, OWN_PAIR + 1, convert, 0)
    total = dot_nt(mats[0:4].reshape(4 * rows, width), s_after[:, :width])
    total += dot_nt(mats[4:8].reshape(4 * rows, width), s_after[:, width:])
    t_before[...] = total[: 2 * rows].astype(bf16)
    left, right = s_own[:, :width], s_own[:, width:]
    t_own[:rows] = total[2 * rows : 3 * rows] + (
        dot_nt(omega[0].astype(bf16), left) + dot_nt(mats[OWN_PAIR], right)
    )
    t_own[rows:] = total[3 * rows :] + dot_nt(omega[1].astype(bf16), right)


def send_halves(cross, chip, before, after):
    @pl.when(is_even())
    def _():
        cross[...] = before
        chip[...] = after

    @pl.when(jnp.logical_not(is_even()))
    def _():
        cross[...] = after
        chip[...] = before


def cols_kernel(
    blocks, coords, parts, s_before, s_own, s_after, t_before, t_own,
    turned, cross, chip, own, slot_of,
):
    count, rows = parts.shape[0], parts.shape[2]
    width = count * rows
    find_slots(blocks, coords, slot_of)

    def convert(pair, carry):
        slot = slot_of[pair]
        unit = jnp.where(pair == OWN_PAIR, OWN_PAIR, lax.rem(pair, 4) * 2 + pair // 4)

        @pl.when(slot > 0)
        def _():
            for part in range(count):
                turned[unit, :, part * rows : (part + 1) * rows] = parts[part, slot - BLK_DEV].T

        @pl.when(slot == 0)
        def _():
            turned[unit] = jnp.zeros_like(turned[unit])

        return carry

    lax.fori_loop(0, OWN_PAIR + 1, convert, 0)
    total = jnp.zeros(own.shape, f32)
    for a in range(2 * BLK_DEV):
        source = (s_before, s_own)[a // BLK_DEV]
        blk = a % BLK_DEV
        total += dot_nt(turned[2 * a : 2 * a + 2].reshape(2 * rows, width), source[:, blk * width : (blk + 1) * width])
    send_halves(cross, chip, t_before[...], total.astype(bf16))
    own[:rows] = t_own[:rows]
    own[rows:] = t_own[rows:] + dot_nt(turned[OWN_PAIR], s_own[:, :width])


def natural(out, pieces):
    count, both = pieces.shape[0], pieces.shape[1]
    rows = both // BLK_DEV
    for blk in range(BLK_DEV):
        for part in range(count):
            at = (blk * count + part) * rows
            out[at : at + rows, :] = pieces[part, blk * rows : (blk + 1) * rows, :]


def own_kernel(blocks, last, *refs):
    if last:
        coords, held, s_own, stq, p_own, out, slot_of, grad, nat_own, tiles, sems = refs
    else:
        coords, omega, turned, s_own, stq, p_own, tiles, t_own, nat_own, slot_of, grad, mats = refs
    rows, width = grad.shape[0] // 2, grad.shape[1] // 2
    quarter = lax.axis_index("samp")
    scale = step_size / (2.0 * s_own.shape[0])
    find_slots(blocks, coords, slot_of)
    natural(nat_own, p_own)
    grad[...] = dot_nn(p_own[quarter], s_own[...]) + dot_nt(stq[1], nat_own[...])
    slot = slot_of[OWN_PAIR]
    for i in range(BLK_DEV):
        old = held[i] if last else omega[i]
        here = grad[i * rows : (i + 1) * rows, i * width : (i + 1) * width]
        tiles[i] = shrink_diagonal(old - scale * here, quarter)
    old = held[2] if last else omega[slot]
    tiles[2] = shrink(old - scale * grad[:rows, width:])
    if last:
        copies = [pltpu.make_async_copy(tiles.at[i], out.at[i], sems.at[i]) for i in range(BLK_DEV)]
        for copy in copies:
            copy.start()

        @pl.when(slot > 0)
        def _():
            copy = pltpu.make_async_copy(tiles.at[2], out.at[slot], sems.at[2])
            copy.start()
            copy.wait()

        for copy in copies:
            copy.wait()
        return
    mats[:rows, :width] = tiles[0].astype(bf16)
    mats[rows:, width:] = tiles[1].astype(bf16)

    @pl.when(slot > 0)
    def _():
        mats[:rows, width:] = tiles[2].astype(bf16)
        there = turned[OWN_PAIR].astype(f32) - scale * grad[rows:, :width]
        mats[rows:, :width] = shrink(there).astype(bf16)

    @pl.when(slot == 0)
    def _():
        mats[:rows, width:] = jnp.zeros((rows, width), bf16)
        mats[rows:, :width] = jnp.zeros((rows, width), bf16)

    t_own[...] = dot_nt(mats[...], s_own[...])


def order_halo(nat, ptq, p_cross, p_chip, quarter):
    even = is_even()
    for ref, at in ((p_cross, jnp.where(even, 0, 1)), (p_chip, jnp.where(even, 1, 0))):
        natural(nat.at[at], ref)
        ptq[at] = ref[quarter]


def update_rows(slot_of, source, grad, a_base, scale, tiles, mats):
    rows, width = grad.shape[0] // 2, grad.shape[1] // 2
    for a in range(2):
        for b in range(2):
            slot = slot_of[b * 4 + a_base + a]
            here = grad[a * rows : (a + 1) * rows, b * width : (b + 1) * width]
            tile = shrink(source[slot] - scale * here)
            tiles[a * 2 + b] = tile
            spot = (slice(a * rows, (a + 1) * rows), slice(b * width, (b + 1) * width))
            mats[spot] = jnp.where(slot > 0, tile, 0.0).astype(bf16)


def outer_kernel(
    blocks, coords, omega, turned, s_before, s_own, s_after, stq, nat_own, p_cross, p_chip,
    tiles, cross, chip, slot_of, nat, ptq, grad, mats, half,
):
    rows, width = omega.shape[1:]
    quarter = lax.axis_index("samp")
    scale = step_size / (2.0 * s_own.shape[0])
    find_slots(blocks, coords, slot_of)
    order_halo(nat, ptq, p_cross, p_chip, quarter)
    total = jnp.zeros(cross.shape, f32)
    for a in range(2 * BLK_DEV):
        blk = a % BLK_DEV
        at = slice(blk * width, (blk + 1) * width)
        source = (s_before, s_own)[a // BLK_DEV][:, at]
        product = (nat.at[0], nat_own)[a // BLK_DEV][at, :]
        half[...] = dot_nn(ptq[1], source) + dot_nt(stq[2], product)
        for b in range(BLK_DEV):
            tile = shrink(turned[2 * a + b].astype(f32) - scale * half[b * rows : (b + 1) * rows, :])
            tile = jnp.where(slot_of[b * 4 + a] > 0, tile, 0.0)
            mats[b * rows : (b + 1) * rows, at] = tile.astype(bf16)
        total += dot_nt(mats[:, at], source)
    after = total.astype(bf16)
    grad[...] = dot_nn(ptq[0], s_after[...]) + dot_nt(stq[0], nat[1])
    update_rows(slot_of, omega, grad, 0, scale, tiles, mats)
    before = dot_nt(mats[...], s_after[...]).astype(bf16)
    send_halves(cross, chip, before, after)


def inner_kernel(
    blocks, coords, omega, s_own, s_after, stq, p_own, p_cross, p_chip, t_own,
    tiles, own, slot_of, nat, ptq, grad, mats,
):
    quarter = lax.axis_index("samp")
    scale = step_size / (2.0 * s_own.shape[0])
    find_slots(blocks, coords, slot_of)
    order_halo(nat, ptq, p_cross, p_chip, quarter)
    grad[...] = dot_nn(p_own[quarter], s_after[...]) + dot_nt(stq[1], nat[1])
    update_rows(slot_of, omega, grad, BLK_DEV, scale, tiles, mats)
    own[...] = t_own[...] + dot_nt(mats[...], s_after[...])


def last_kernel(
    blocks, coords, outer, inner, s_after, stq, p_own, p_cross, p_chip, begun,
    out, slot_of, nat, ptq, grad, tiles, sems,
):
    rows, width = tiles.shape[1:]
    quarter = lax.axis_index("samp")
    scale = step_size / (2.0 * s_after.shape[0])
    find_slots(blocks, coords, slot_of)
    order_halo(nat, ptq, p_cross, p_chip, quarter)
    for group in range(2):
        lhs = ptq[0] if group == 0 else p_own[quarter]
        grad[group] = dot_nn(lhs, s_after[...]) + dot_nt(stq[group], nat[1])
        for a in range(2):
            for b in range(2):
                unit = group * 4 + a * 2 + b
                slot = slot_of[b * 4 + group * 2 + a]
                here = grad[group, a * rows : (a + 1) * rows, b * width : (b + 1) * width]
                tiles[unit] = shrink((outer, inner)[group][a * 2 + b] - scale * here)

                @pl.when(slot > 0)
                def _(unit=unit, slot=slot):
                    pltpu.make_async_copy(tiles.at[unit], out.at[slot], sems.at[unit]).start()

    for group in range(2):
        for a in range(2):
            for b in range(2):
                unit = group * 4 + a * 2 + b
                slot = slot_of[b * 4 + group * 2 + a]

                @pl.when(slot > 0)
                def _(unit=unit, slot=slot):
                    pltpu.make_async_copy(tiles.at[unit], out.at[slot], sems.at[unit]).wait()


def shards(samples, omega, coords):
    size = lax.axis_size("tiles")
    parts = lax.axis_size("samp")
    blocks = BLK_DEV * size
    tiles, rows, width = omega.shape
    others = tiles - BLK_DEV
    count = samples.shape[0] * parts
    wide = samples.shape[1]
    both = BLK_DEV * rows
    chip = [(i, i ^ 1) for i in range(size)]
    cross = [(i, (i - 1) % size if i % 2 == 0 else (i + 1) % size) for i in range(size)]
    shape = jax.ShapeDtypeStruct
    slots = pltpu.SMEM((OWN_PAIR + 1,), jnp.int32)
    params = pltpu.CompilerParams(vmem_limit_bytes=LIMIT)

    def call(body, in_specs, outs, scratch, macs, moved, aliases=None, out_specs=None):
        several = isinstance(outs, tuple)
        specs = out_specs or ((VMEM,) * len(outs) if several else VMEM)
        return pl.pallas_call(
            body, out_shape=outs, in_specs=in_specs, out_specs=specs, scratch_shapes=scratch,
            compiler_params=params, input_output_aliases=aliases or {},
            cost_estimate=pl.CostEstimate(flops=2 * macs, bytes_accessed=moved, transcendentals=0),
        )

    def exchange(to_cross, to_chip):
        from_chip = lax.ppermute(to_chip, "tiles", chip)
        from_cross = lax.ppermute(to_cross, "tiles", cross)
        return from_cross, from_chip

    s_own = lax.all_gather(samples, "samp", axis=0, tiled=True)
    pieces = call(
        cut_kernel, [VMEM, ANY], shape((parts, others, rows, rows), bf16),
        [pltpu.VMEM((parts, others, rows, rows), bf16), pltpu.SemaphoreType.DMA((parts,))], 0, 4 << 20, out_specs=ANY,
    )(omega, s_own)
    turned_parts = lax.all_to_all(pieces, "samp", 0, 0)
    s_cross, s_chip = exchange(s_own, s_own)

    window = shape((count, wide), bf16)
    part = shape((both, count), bf16)
    full = shape((both, count), f32)
    held = pltpu.VMEM((OWN_PAIR + 1, rows, width), bf16)
    unit = rows * width * count
    s_before, s_after, stq, t_before, t_own = call(
        functools.partial(rows_kernel, blocks), [SMEM] + [VMEM] * 4,
        (window, window, shape((3, both, count), bf16), part, full), [slots, held], 11 * unit, 4 << 20,
    )(coords, omega, s_own, s_cross, s_chip)
    turned, to_cross, to_chip, own = call(
        functools.partial(cols_kernel, blocks), [SMEM] + [VMEM] * 6,
        (shape((OWN_PAIR + 1, rows, width), bf16), part, part, full), [slots], 9 * unit, 3 << 20,
    )(coords, turned_parts, s_before, s_own, s_after, t_before, t_own)

    def products(to_cross, to_chip, finish):
        from_cross, from_chip = exchange(to_cross, to_chip)
        tiles, own = finish()
        total = own + from_cross.astype(f32) + from_chip.astype(f32)
        p_own = lax.all_gather(total.astype(bf16), "samp", axis=0, tiled=False)
        p_cross, p_chip = exchange(p_own, p_own)
        return tiles, p_own, p_cross, p_chip

    grad = pltpu.VMEM((both, wide), f32)
    mats = pltpu.VMEM((both, wide), bf16)
    nat = pltpu.VMEM((2, wide, count), bf16)
    ptq = pltpu.VMEM((2, both, count), bf16)
    four = shape((4, rows, width), f32)

    _, p_own, p_cross, p_chip = products(to_cross, to_chip, lambda: (None, own))
    mine, t_own, nat_own = call(
        functools.partial(own_kernel, blocks, False), [SMEM] + [VMEM] * 5,
        (shape((3, rows, width), f32), full, shape((wide, count), bf16)), [slots, grad, mats], 12 * unit, 4 << 20,
    )(coords, omega, turned, s_own, stq, p_own)
    outer, to_cross, to_chip = call(
        functools.partial(outer_kernel, blocks), [SMEM] + [VMEM] * 9,
        (four, part, part), [slots, nat, ptq, grad, mats, pltpu.VMEM((both, width), f32)], 36 * unit, 6 << 20,
    )(coords, omega, turned, s_before, s_own, s_after, stq, nat_own, p_cross, p_chip)

    def finish():
        return call(
            functools.partial(inner_kernel, blocks), [SMEM] + [VMEM] * 8,
            (four, full), [slots, nat, ptq, grad, mats], 12 * unit, 4 << 20,
        )(coords, omega, s_own, s_after, stq, p_own, p_cross, p_chip, t_own)

    inner, p_own, p_cross, p_chip = products(to_cross, to_chip, finish)
    whole = shape(omega.shape, f32)
    begun = call(
        functools.partial(own_kernel, blocks, True), [SMEM] + [VMEM] * 4, whole,
        [slots, grad, pltpu.VMEM((wide, count), bf16), pltpu.VMEM((3, rows, width), f32), pltpu.SemaphoreType.DMA((3,))],
        8 * unit, 3 << 20, out_specs=ANY,
    )(coords, mine, s_own, stq, p_own)
    return call(
        functools.partial(last_kernel, blocks), [SMEM] + [VMEM] * 7 + [ANY], whole,
        [slots, nat, ptq, pltpu.VMEM((2, both, wide), f32), pltpu.VMEM((8, rows, width), f32), pltpu.SemaphoreType.DMA((8,))],
        16 * unit, 6 << 20, aliases={8: 0}, out_specs=ANY,
    )(coords, outer, inner, s_after, stq, p_own, p_cross, p_chip, begun)


def solution(mesh):
    in_specs = (P("samp", "tiles"), P("tiles", "samp", None), P("tiles", None))
    out_specs = P("tiles", "samp", None)

    return jax.shard_map(shards, mesh=mesh, in_specs=in_specs, out_specs=out_specs, check_vma=False)
```

time: 230 us -> 140 us (0.61)
  the two profiles are of different devices: /device:TPU:4 before, /device:TPU:2 now
where the time goes in v2:
time: 140 us; the launch traced here: 139 us
  starting transfers between devices  43.2 us (31%)
  blocking collectives  42.1 us (30%)
  waiting for transfers between devices  27.4 us (20%)
  Pallas kernels  16.6 us (12%)
  local copies, waits for them, and re-layouts  9.71 us (7%)
    ppermute x5, waiting for transfers between devices, exchange(): from_cross = lax.ppermute(to_cross, 'tiles', cross)  26.8 us
    all_gather x2, blocking collectives, products(): p_own = lax.all_gather(total.astype(bf16), 'samp', axis=0, tiled=False)  26.4 us
    ppermute x5, starting transfers between devices, exchange(): from_cross = lax.ppermute(to_cross, 'tiles', cross)  26.2 us
    all_gather x1, blocking collectives, shards(): s_own = lax.all_gather(samples, 'samp', axis=0, tiled=True)  15.7 us
    unnamed x29, local copies, waits for them, and re-layouts  9.71 us
    ppermute x5, starting transfers between devices, exchange(): from_chip = lax.ppermute(to_chip, 'tiles', chip)  9.57 us
    all_to_all x1, starting transfers between devices, shards(): turned_parts = lax.all_to_all(pieces, 'samp', 0, 0)  7.37 us
    pallas_call x1, Pallas kernels, shards(): call(functools.partial(cols_kernel, blocks), [SMEM] + [VMEM] * 6, (shape(...  2.97 us
  transfers between devices with their start and end apart: 11, of which 6 were waited for; matrix products, arithmetic and copies ran while one was open for 0% of the time, Pallas kernels for 6%

profile of v2, /device:TPU:2, one launch (start us, length us, event | category | flops | bytes accessed | tf_op | source)
XLA Modules:
  0.0 139.2 jit_solution(13197388907697698161)
XLA Ops:
  0.0 15.7 %all_gather.15.gathered.s_own.refs_3_.refs_2_ = bf16[256,1024]{1,0:T(8,128)(2,1)S(1)} all-gather(bf16[64,1024]{1,0:T(8,128)(2,1)} %param.3), channel_id=1, replica_groups=mesh['tiles'=128,'samp'=4] {'samp'}, dimensions={0}, use_global_device_ids=true | all-gather | bytes 655360 | tf_op jit(solution)/shard_map/all_gather | solution.py:351
  18.8 7.4 %all-to-all-start = ((bf16[4,8,128,128]{3,2,1,0:T(8,128)(2,1)}), bf16[4,8,128,128]{3,2,1,0:T(8,128)(2,1)}, u32[]{:S(2)}, u32[]{:S(2)}) async-start(bf16[4,8,128,128]{3,2,1,0:T(8,128)(2,1)} %copy-done.5), calls=%async_computation | async-start | bytes 2097152 | tf_op jit(solution)/shard_map/all_to_all | solution.py:356
  26.2 1.9 %collective-permute-start.1 = (bf16[256,1024]{1,0:T(8,128)(2,1)S(1)}, bf16[256,1024]{1,0:T(8,128)(2,1)}, u32[]{:S(2)}, u32[]{:S(2)}) collective-permute-start(bf16[256,1024]{1,0:T(8,128)(2,1)S(1)} %all_gather.15.gathered.s_own.refs_3_.refs_2_), channel_id=1, source_target_pairs={{0,4},{4,0},{8,12},{12,8},{16,20},{20,16},{24,28},{28,24},{32,36},... | collective-permute-start | bytes 1572872 | tf_op jit(solution)/shard_map/ppermute | solution.py:347
  28.1 9.0 %collective-permute-start = (bf16[256,1024]{1,0:T(8,128)(2,1)S(1)}, bf16[256,1024]{1,0:T(8,128)(2,1)}, u32[]{:S(2)}, u32[]{:S(2)}) collective-permute-start(bf16[256,1024]{1,0:T(8,128)(2,1)S(1)} %all_gather.15.gathered.s_own.refs_3_.refs_2_), channel_id=1, source_target_pairs={{0,508},{4,8},{8,4},{12,16},{16,12},{20,24},{24,20},{28,32},{32,28... | collective-permute-start | bytes 1572872 | tf_op jit(solution)/shard_map/ppermute | solution.py:348
  37.2 6.8 %collective-permute-done.s_cross = bf16[256,1024]{1,0:T(8,128)(2,1)} collective-permute-done((bf16[256,1024]{1,0:T(8,128)(2,1)S(1)}, bf16[256,1024]{1,0:T(8,128)(2,1)}, u32[]{:S(2)}, u32[]{:S(2)}) %collective-permute-start) | collective-permute-done | bytes 524320 | tf_op jit(solution)/shard_map/ppermute | solution.py:348
  44.1 2.4 %shard_map.38 = (bf16[256,1024]{1,0:T(8,128)(2,1)S(1)}, bf16[256,1024]{1,0:T(8,128)(2,1)S(1)}, bf16[3,256,256]{2,1,0:T(8,128)(2,1)S(1)}, bf16[256,256]{1,0:T(8,128)(2,1)S(1)}, f32[256,256]{1,0:T(8,128)S(1)}) custom-call(s32[10,2]{1,0:T(8,128)S(1)} %copy.11.coords.refs_0_, f32[10,128,512]{2,1,0:T(8,128)S(1)} %copy-done.1, ...), custom_call_target="tpu_custom_call" | custom-call | flops 369098752 | bytes 4194304 | tf_op jit(solution)/shard_map/pallas_call | solution.py:364
  53.4 3.0 %shard_map.39 = (bf16[9,128,512]{2,1,0:T(8,128)(2,1)S(1)}, bf16[256,256]{1,0:T(8,128)(2,1)S(1)}, bf16[256,256]{1,0:T(8,128)(2,1)S(1)}, f32[256,256]{1,0:T(8,128)S(1)}) custom-call(s32[10,2]{1,0:T(8,128)S(1)} %copy.11.coords.refs_0_, bf16[4,8,128,128]{3,2,1,0:T(8,128)(2,1)} %all-to-all-done.parts, bf16[256,1024]{1,0:T(8,128)(2,1)S(1)} %copy-done.7, ...), custom_call_target="tpu_custom_call" | custom-call | flops 301989888 | bytes 3145728 | tf_op jit(solution)/shard_map/pallas_call | solution.py:368
  56.4 7.0 %collective-permute-start.2 = (bf16[256,256]{1,0:T(8,128)(2,1)S(1)}, bf16[256,256]{1,0:T(8,128)(2,1)S(1)}, u32[]{:S(2)}, u32[]{:S(2)}) collective-permute-start(bf16[256,256]{1,0:T(8,128)(2,1)S(1)} %get-tuple-element.29), channel_id=1, source_target_pairs={{0,508},{4,8},{8,4},{12,16},{16,12},{20,24},{24,20},{28,32},{32,28... | collective-permute-start | bytes 393224 | tf_op jit(solution)/shard_map/ppermute | solution.py:348
  63.4 1.9 %collective-permute-start.3 = (bf16[256,256]{1,0:T(8,128)(2,1)S(1)}, bf16[256,256]{1,0:T(8,128)(2,1)S(1)}, u32[]{:S(2)}, u32[]{:S(2)}) collective-permute-start(bf16[256,256]{1,0:T(8,128)(2,1)S(1)} %get-tuple-element.30), channel_id=1, source_target_pairs={{0,4},{4,0},{8,12},{12,8},{16,20},{20,16},{24,28},{28,24},{32,36},... | collective-permute-start | bytes 393224 | tf_op jit(solution)/shard_map/ppermute | solution.py:347
  66.7 13.5 %all-gather = bf16[1024,256]{1,0:T(8,128)(2,1)S(1)} all-gather(bf16[256,256]{1,0:T(8,128)(2,1)S(1)} %add_convert_fusion.1), channel_id=2, replica_groups=mesh['tiles'=128,'samp'=4] {'samp'}, dimensions={0}, use_global_device_ids=true | all-gather | bytes 655360 | tf_op jit(solution)/shard_map/all_gather | solution.py:377
  80.1 1.9 %collective-permute-start.5 = (bf16[4,256,256]{2,1,0:T(8,128)(2,1)S(1)}, bf16[4,256,256]{2,1,0:T(8,128)(2,1)S(1)}, u32[]{:S(2)}, u32[]{:S(2)}) collective-permute-start(bf16[4,256,256]{2,1,0:T(8,128)(2,1)S(1)} %bitcast.2), channel_id=1, source_target_pairs={{0,4},{4,0},{8,12},{12,8},{16,20},{20,16},{24,28},{28,24},{32,36},... | collective-permute-start | bytes 1572872 | tf_op jit(solution)/shard_map/ppermute | solution.py:347
  82.1 3.3 %collective-permute-start.4 = (bf16[4,256,256]{2,1,0:T(8,128)(2,1)S(1)}, bf16[4,256,256]{2,1,0:T(8,128)(2,1)S(1)}, u32[]{:S(2)}, u32[]{:S(2)}) collective-permute-start(bf16[4,256,256]{2,1,0:T(8,128)(2,1)S(1)} %bitcast.3), channel_id=1, source_target_pairs={{0,508},{4,8},{8,4},{12,16},{16,12},{20,24},{24,20},{28,32},{32,28... | collective-permute-start | bytes 1572872 | tf_op jit(solution)/shard_map/ppermute | solution.py:348
  85.4 1.9 %shard_map.40 = (f32[3,128,512]{2,1,0:T(8,128)S(1)}, f32[256,256]{1,0:T(8,128)S(1)}, bf16[1024,256]{1,0:T(8,128)(2,1)S(1)}) custom-call(s32[10,2]{1,0:T(8,128)S(1)} %copy.11.coords.refs_0_, f32[10,128,512]{2,1,0:T(8,128)S(1)} %copy-done.1, bf16[9,128,512]{2,1,0:T(8,128)(2,1)S(1)} %get-tuple-element.26.refs_2_.turned, ...), custom_call_target="tpu_custom_call" | custom-call | flops 402653184 | bytes 4194304 | tf_op jit(solution)/shard_map/pallas_call | solution.py:388
  87.3 8.5 %collective-permute-done.4.p_cross = bf16[4,256,256]{2,1,0:T(8,128)(2,1)S(1)} collective-permute-done((bf16[4,256,256]{2,1,0:T(8,128)(2,1)S(1)}, bf16[4,256,256]{2,1,0:T(8,128)(2,1)S(1)}, u32[]{:S(2)}, u32[]{:S(2)}) %collective-permute-start.4) | collective-permute-done | bytes 524320 | tf_op jit(solution)/shard_map/ppermute | solution.py:348
  95.9 2.5 %shard_map.41 = (f32[4,128,512]{2,1,0:T(8,128)S(1)}, bf16[256,256]{1,0:T(8,128)(2,1)S(1)}, bf16[256,256]{1,0:T(8,128)(2,1)S(1)}) custom-call(s32[10,2]{1,0:T(8,128)S(1)} %copy.11.coords.refs_0_, f32[10,128,512]{2,1,0:T(8,128)S(1)} %copy-done.1, bf16[9,128,512]{2,1,0:T(8,128)(2,1)S(1)} %get-tuple-element.26.refs_2_.turned, bf16[256,1024]{1,0:T(8,128)(2,1)S(1)} %copy-done.8, ...), custom_call_target="tpu_custom_call" | custom-call | flops 1207959552 | bytes 6291456 | tf_op jit(solution)/shard_map/pallas_call | solution.py:392
  98.4 3.3 %collective-permute-start.6 = (bf16[256,256]{1,0:T(8,128)(2,1)S(1)}, bf16[256,256]{1,0:T(8,128)(2,1)S(1)}, u32[]{:S(2)}, u32[]{:S(2)}) collective-permute-start(bf16[256,256]{1,0:T(8,128)(2,1)S(1)} %get-tuple-element.36), channel_id=1, source_target_pairs={{0,508},{4,8},{8,4},{12,16},{16,12},{20,24},{24,20},{28,32},{32,28... | collective-permute-start | bytes 393224 | tf_op jit(solution)/shard_map/ppermute | solution.py:348
  101.8 1.9 %collective-permute-start.7 = (bf16[256,256]{1,0:T(8,128)(2,1)S(1)}, bf16[256,256]{1,0:T(8,128)(2,1)S(1)}, u32[]{:S(2)}, u32[]{:S(2)}) collective-permute-start(bf16[256,256]{1,0:T(8,128)(2,1)S(1)} %get-tuple-element.37), channel_id=1, source_target_pairs={{0,4},{4,0},{8,12},{12,8},{16,20},{20,16},{24,28},{28,24},{32,36},... | collective-permute-start | bytes 393224 | tf_op jit(solution)/shard_map/ppermute | solution.py:347
  105.2 2.8 %collective-permute-done.6 = bf16[256,256]{1,0:T(8,128)(2,1)S(1)} collective-permute-done((bf16[256,256]{1,0:T(8,128)(2,1)S(1)}, bf16[256,256]{1,0:T(8,128)(2,1)S(1)}, u32[]{:S(2)}, u32[]{:S(2)}) %collective-permute-start.6) | collective-permute-done | bytes 131104 | tf_op jit(solution)/shard_map/ppermute | solution.py:348
  108.1 12.9 %all-gather.1 = bf16[1024,256]{1,0:T(8,128)(2,1)S(1)} all-gather(bf16[256,256]{1,0:T(8,128)(2,1)S(1)} %add_convert_fusion), channel_id=3, replica_groups=mesh['tiles'=128,'samp'=4] {'samp'}, dimensions={0}, use_global_device_ids=true | all-gather | bytes 655360 | tf_op jit(solution)/shard_map/all_gather | solution.py:377
  121.0 1.9 %collective-permute-start.9 = (bf16[4,256,256]{2,1,0:T(8,128)(2,1)S(1)}, bf16[4,256,256]{2,1,0:T(8,128)(2,1)S(1)}, u32[]{:S(2)}, u32[]{:S(2)}) collective-permute-start(bf16[4,256,256]{2,1,0:T(8,128)(2,1)S(1)} %bitcast.6), channel_id=1, source_target_pairs={{0,4},{4,0},{8,12},{12,8},{16,20},{20,16},{24,28},{28,24},{32,36},... | collective-permute-start | bytes 1572872 | tf_op jit(solution)/shard_map/ppermute | solution.py:347
  122.9 3.6 %collective-permute-start.8 = (bf16[4,256,256]{2,1,0:T(8,128)(2,1)S(1)}, bf16[4,256,256]{2,1,0:T(8,128)(2,1)S(1)}, u32[]{:S(2)}, u32[]{:S(2)}) collective-permute-start(bf16[4,256,256]{2,1,0:T(8,128)(2,1)S(1)} %bitcast.7), channel_id=1, source_target_pairs={{0,508},{4,8},{8,4},{12,16},{16,12},{20,24},{24,20},{28,32},{32,28... | collective-permute-start | bytes 1572872 | tf_op jit(solution)/shard_map/ppermute | solution.py:348
  126.5 2.3 %shard_map.43.begun = f32[10,128,512]{2,1,0:T(8,128)} custom-call(s32[10,2]{1,0:T(8,128)S(1)} %copy.11.coords.refs_0_, f32[3,128,512]{2,1,0:T(8,128)S(1)} %get-tuple-element.38.refs_1_, bf16[256,1024]{1,0:T(8,128)(2,1)S(1)} %all_gather.15.gathered.s_own.refs_3_.refs_2_, bf16[3,256,256]{2,1,0:T(8,128)(2,1)S(1)} %get-tuple-element.27.refs_4_.stq.refs_3_, ...), custom_call_target="tpu_custom_call" | custom-call | flops 268435456 | bytes 3145728 | tf_op jit(solution)/shard_map/pallas_call | solution.py:405
  128.8 7.9 %collective-permute-done.8.p_cross = bf16[4,256,256]{2,1,0:T(8,128)(2,1)S(1)} collective-permute-done((bf16[4,256,256]{2,1,0:T(8,128)(2,1)S(1)}, bf16[4,256,256]{2,1,0:T(8,128)(2,1)S(1)}, u32[]{:S(2)}, u32[]{:S(2)}) %collective-permute-start.8) | collective-permute-done | bytes 524320 | tf_op jit(solution)/shard_map/ppermute | solution.py:348
  136.7 2.5 %shard_map.44 = f32[10,128,512]{2,1,0:T(8,128)} custom-call(s32[10,2]{1,0:T(8,128)S(1)} %copy.11.coords.refs_0_, f32[4,128,512]{2,1,0:T(8,128)S(1)} %get-tuple-element.32.outer, f32[4,128,512]{2,1,0:T(8,128)S(1)} %get-tuple-element.34.inner, bf16[256,1024]{1,0:T(8,128)(2,1)S(1)} %copy-done.4, ...), custom_call_target="tpu_custom_call", output_to_operand_aliasing={{}: (8, {})} | custom-call | flops 536870912 | bytes 6291456 | tf_op jit(solution)/shard_map/pallas_call | solution.py:410
  (40 shorter events, 13.0 us)
Async XLA Ops:
  15.7 1.7 %copy-start = (f32[10,128,512]{2,1,0:T(8,128)S(1)}, f32[10,128,512]{2,1,0:T(8,128)}, u32[]{:S(2)}) copy-start(f32[10,128,512]{2,1,0:T(8,128)} %omega.7) | copy-start | bytes 7864324
  17.4 19.7 %copy-start.13 = (s32[10,2]{0,1:T(2,128)S(1)}, s32[10,2]{0,1:T(2,128)}, u32[]{:S(2)}) copy-start(s32[10,2]{0,1:T(2,128)} %param.5) | copy-start | bytes 244
  17.5 26.6 %copy-start.1 = (f32[10,128,512]{2,1,0:T(8,128)S(1)}, f32[10,128,512]{2,1,0:T(8,128)}, u32[]{:S(2)}) copy-start(f32[10,128,512]{2,1,0:T(8,128)} %omega.7) | copy-start | bytes 7864324
  17.9 1.0 copy-start.5
  18.8 30.6 %all-to-all-start = ((bf16[4,8,128,128]{3,2,1,0:T(8,128)(2,1)}), bf16[4,8,128,128]{3,2,1,0:T(8,128)(2,1)}, u32[]{:S(2)}, u32[]{:S(2)}) async-start(bf16[4,8,128,128]{3,2,1,0:T(8,128)(2,1)} %copy-done.5), calls=%async_computation | async-start | bytes 2097152 | tf_op jit(solution)/shard_map/all_to_all | solution.py:356
  26.2 11.0 %collective-permute-start.1 = (bf16[256,1024]{1,0:T(8,128)(2,1)S(1)}, bf16[256,1024]{1,0:T(8,128)(2,1)}, u32[]{:S(2)}, u32[]{:S(2)}) collective-permute-start(bf16[256,1024]{1,0:T(8,128)(2,1)S(1)} %all_gather.15.gathered.s_own.refs_3_.refs_2_), channel_id=1, source_target_pairs={{0,4},{4,0},{8,12},{12,8},{16,20},{20,16},{24,28},{28,24},{32,36},... | collective-permute-start | bytes 1572872 | tf_op jit(solution)/shard_map/ppermute | solution.py:347
  28.1 16.0 %collective-permute-start = (bf16[256,1024]{1,0:T(8,128)(2,1)S(1)}, bf16[256,1024]{1,0:T(8,128)(2,1)}, u32[]{:S(2)}, u32[]{:S(2)}) collective-permute-start(bf16[256,1024]{1,0:T(8,128)(2,1)S(1)} %all_gather.15.gathered.s_own.refs_3_.refs_2_), channel_id=1, source_target_pairs={{0,508},{4,8},{8,4},{12,16},{16,12},{20,24},{24,20},{28,32},{32,28... | collective-permute-start | bytes 1572872 | tf_op jit(solution)/shard_map/ppermute | solution.py:348
  46.5 0.8 copy-start.2
  47.3 0.8 copy-start.6
  48.1 0.7 copy-start.9
  49.5 1.0 copy-start.3
  50.5 1.0 copy-start.7
  51.6 0.9 copy-start.10
  52.5 0.9 copy-start.12
  56.4 9.6 %collective-permute-start.2 = (bf16[256,256]{1,0:T(8,128)(2,1)S(1)}, bf16[256,256]{1,0:T(8,128)(2,1)S(1)}, u32[]{:S(2)}, u32[]{:S(2)}) collective-permute-start(bf16[256,256]{1,0:T(8,128)(2,1)S(1)} %get-tuple-element.29), channel_id=1, source_target_pairs={{0,508},{4,8},{8,4},{12,16},{16,12},{20,24},{24,20},{28,32},{32,28... | collective-permute-start | bytes 393224 | tf_op jit(solution)/shard_map/ppermute | solution.py:348
  63.4 3.2 %collective-permute-start.3 = (bf16[256,256]{1,0:T(8,128)(2,1)S(1)}, bf16[256,256]{1,0:T(8,128)(2,1)S(1)}, u32[]{:S(2)}, u32[]{:S(2)}) collective-permute-start(bf16[256,256]{1,0:T(8,128)(2,1)S(1)} %get-tuple-element.30), channel_id=1, source_target_pairs={{0,4},{4,0},{8,12},{12,8},{16,20},{20,16},{24,28},{28,24},{32,36},... | collective-permute-start | bytes 393224 | tf_op jit(solution)/shard_map/ppermute | solution.py:347
  80.1 7.2 %collective-permute-start.5 = (bf16[4,256,256]{2,1,0:T(8,128)(2,1)S(1)}, bf16[4,256,256]{2,1,0:T(8,128)(2,1)S(1)}, u32[]{:S(2)}, u32[]{:S(2)}) collective-permute-start(bf16[4,256,256]{2,1,0:T(8,128)(2,1)S(1)} %bitcast.2), channel_id=1, source_target_pairs={{0,4},{4,0},{8,12},{12,8},{16,20},{20,16},{24,28},{28,24},{32,36},... | collective-permute-start | bytes 1572872 | tf_op jit(solution)/shard_map/ppermute | solution.py:347
  82.1 13.8 %collective-permute-start.4 = (bf16[4,256,256]{2,1,0:T(8,128)(2,1)S(1)}, bf16[4,256,256]{2,1,0:T(8,128)(2,1)S(1)}, u32[]{:S(2)}, u32[]{:S(2)}) collective-permute-start(bf16[4,256,256]{2,1,0:T(8,128)(2,1)S(1)} %bitcast.3), channel_id=1, source_target_pairs={{0,508},{4,8},{8,4},{12,16},{16,12},{20,24},{24,20},{28,32},{32,28... | collective-permute-start | bytes 1572872 | tf_op jit(solution)/shard_map/ppermute | solution.py:348
  85.4 10.5 %copy-start.8 = (bf16[256,1024]{1,0:T(8,128)(2,1)S(1)}, bf16[256,1024]{1,0:T(8,128)(2,1)}, u32[]{:S(2)}) copy-start(bf16[256,1024]{1,0:T(8,128)(2,1)} %copy-done.6) | copy-start | bytes 1572868
  98.4 9.6 %collective-permute-start.6 = (bf16[256,256]{1,0:T(8,128)(2,1)S(1)}, bf16[256,256]{1,0:T(8,128)(2,1)S(1)}, u32[]{:S(2)}, u32[]{:S(2)}) collective-permute-start(bf16[256,256]{1,0:T(8,128)(2,1)S(1)} %get-tuple-element.36), channel_id=1, source_target_pairs={{0,508},{4,8},{8,4},{12,16},{16,12},{20,24},{24,20},{28,32},{32,28... | collective-permute-start | bytes 393224 | tf_op jit(solution)/shard_map/ppermute | solution.py:348
  101.8 6.3 %collective-permute-start.7 = (bf16[256,256]{1,0:T(8,128)(2,1)S(1)}, bf16[256,256]{1,0:T(8,128)(2,1)S(1)}, u32[]{:S(2)}, u32[]{:S(2)}) collective-permute-start(bf16[256,256]{1,0:T(8,128)(2,1)S(1)} %get-tuple-element.37), channel_id=1, source_target_pairs={{0,4},{4,0},{8,12},{12,8},{16,20},{20,16},{24,28},{28,24},{32,36},... | collective-permute-start | bytes 393224 | tf_op jit(solution)/shard_map/ppermute | solution.py:347
  108.1 28.7 %copy-start.4 = (bf16[256,1024]{1,0:T(8,128)(2,1)S(1)}, bf16[256,1024]{1,0:T(8,128)(2,1)}, u32[]{:S(2)}) copy-start(bf16[256,1024]{1,0:T(8,128)(2,1)} %copy-done.2) | copy-start | bytes 1572868
  121.0 7.8 %collective-permute-start.9 = (bf16[4,256,256]{2,1,0:T(8,128)(2,1)S(1)}, bf16[4,256,256]{2,1,0:T(8,128)(2,1)S(1)}, u32[]{:S(2)}, u32[]{:S(2)}) collective-permute-start(bf16[4,256,256]{2,1,0:T(8,128)(2,1)S(1)} %bitcast.6), channel_id=1, source_target_pairs={{0,4},{4,0},{8,12},{12,8},{16,20},{20,16},{24,28},{28,24},{32,36},... | collective-permute-start | bytes 1572872 | tf_op jit(solution)/shard_map/ppermute | solution.py:347
  122.9 13.8 %collective-permute-start.8 = (bf16[4,256,256]{2,1,0:T(8,128)(2,1)S(1)}, bf16[4,256,256]{2,1,0:T(8,128)(2,1)S(1)}, u32[]{:S(2)}, u32[]{:S(2)}) collective-permute-start(bf16[4,256,256]{2,1,0:T(8,128)(2,1)S(1)} %bitcast.7), channel_id=1, source_target_pairs={{0,508},{4,8},{8,4},{12,16},{16,12},{20,24},{24,20},{28,32},{32,28... | collective-permute-start | bytes 1572872 | tf_op jit(solution)/shard_map/ppermute | solution.py:348
  (1 other events, 0.6 us)

commit v3 on v2

--- a/solution.py
+++ b/solution.py
@@ -62,21 +62,40 @@
     return lax.rem(lax.axis_index("tiles"), 2) == 0
 
 
-def cut_kernel(omega, gathered, out, held, sems):
+def cut_kernel(omega, out, held, pieces, in_sems, out_sems):
     rows = omega.shape[1]
-    copies = []
-    for part in range(out.shape[0]):
-        for slot in range(BLK_DEV, omega.shape[0]):
-            held[part, slot - BLK_DEV] = omega[slot, :, part * rows : (part + 1) * rows].astype(bf16)
-        copies.append(pltpu.make_async_copy(held.at[part], out.at[part], sems.at[part]))
-        copies[-1].start()
-    for copy in copies:
-        copy.wait()
-
-
-def rows_kernel(
-    blocks, coords, omega, s_own, s_cross, s_chip,
-    s_before, s_after, stq, t_before, t_own, slot_of, mats,
+    others = held.shape[0]
+    loads = [
+        pltpu.make_async_copy(omega.at[BLK_DEV + k], held.at[k], in_sems.at[k]) for k in range(others)
+    ]
+    for load in loads:
+        load.start()
+    stores = []
+    for k in range(others):
+        loads[k].wait()
+        for part in range(out.shape[0]):
+            pieces[part, k] = held[k, :, part * rows : (part + 1) * rows].astype(bf16)
+        stores.append(pltpu.make_async_copy(pieces.at[:, k], out.at[:, k], out_sems.at[k]))
+        stores[-1].start()
+    for store in stores:
+        store.wait()
+
+
+def send_halves(cross, chip, before, after):
+    @pl.when(is_even())
+    def _():
+        cross[...] = before
+        chip[...] = after
+
+    @pl.when(jnp.logical_not(is_even()))
+    def _():
+        cross[...] = after
+        chip[...] = before
+
+
+def begin_kernel(
+    blocks, coords, omega, parts, s_own, s_cross, s_chip,
+    s_before, s_after, stq, turned, cross, chip, own, slot_of, mats,
 ):
     rows, width = omega.shape[1:]
     quarter = lax.axis_index("samp")
@@ -92,79 +111,43 @@
         s_before[...] = s_chip[...]
         s_after[...] = s_cross[...]
 
+    def convert(pair, carry):
+        slot = slot_of[pair]
+        unit = jnp.where(pair == OWN_PAIR, OWN_PAIR, lax.rem(pair, 4) * 2 + pair // 4)
+
+        @pl.when(slot > 0)
+        def _():
+            mats[pair] = omega[slot].astype(bf16)
+            for part in range(width // rows):
+                turned[unit, :, part * rows : (part + 1) * rows] = parts[part, slot - BLK_DEV].T
+
+        @pl.when(slot == 0)
+        def _():
+            mats[pair] = jnp.zeros_like(mats[pair])
+            turned[unit] = jnp.zeros_like(turned[unit])
+
+        return carry
+
+    lax.fori_loop(0, OWN_PAIR + 1, convert, 0)
+    total = dot_nt(mats[0:4].reshape(4 * rows, width), s_after[:, :width])
+    total += dot_nt(mats[4:8].reshape(4 * rows, width), s_after[:, width:])
+    left, right = s_own[:, :width], s_own[:, width:]
+    own[:rows] = total[2 * rows : 3 * rows] + (
+        dot_nt(omega[0].astype(bf16), left) + dot_nt(mats[OWN_PAIR], right)
+    )
+    own[rows:] = total[3 * rows :] + (
+        dot_nt(omega[1].astype(bf16), right) + dot_nt(turned[OWN_PAIR], left)
+    )
+    after = jnp.zeros(own.shape, f32)
+    for a in range(2 * BLK_DEV):
+        source = (s_before, s_own)[a // BLK_DEV]
+        blk = a % BLK_DEV
+        after += dot_nt(turned[2 * a : 2 * a + 2].reshape(2 * rows, width), source[:, blk * width : (blk + 1) * width])
+    send_halves(cross, chip, total[: 2 * rows].astype(bf16), after.astype(bf16))
     for side, ref in enumerate((s_before, s_own, s_after)):
         for blk in range(BLK_DEV):
             at = pl.multiple_of(blk * width + quarter * rows, rows)
             stq[side, blk * rows : (blk + 1) * rows, :] = ref[:, pl.ds(at, rows)].T
-
-    def convert(pair, carry):
-        slot = slot_of[pair]
-
-        @pl.when(slot > 0)
-        def _():
-            mats[pair] = omega[slot].astype(bf16)
-
-        @pl.when(slot == 0)
-        def _():
-            mats[pair] = jnp.zeros_like(mats[pair])
-
-        return carry
-
-    lax.fori_loop(0, OWN_PAIR + 1, convert, 0)
-    total = dot_nt(mats[0:4].reshape(4 * rows, width), s_after[:, :width])
-    total += dot_nt(mats[4:8].reshape(4 * rows, width), s_after[:, width:])
-    t_before[...] = total[: 2 * rows].astype(bf16)
-    left, right = s_own[:, :width], s_own[:, width:]
-    t_own[:rows] = total[2 * rows : 3 * rows] + (
-        dot_nt(omega[0].astype(bf16), left) + dot_nt(mats[OWN_PAIR], right)
-    )
-    t_own[rows:] = total[3 * rows :] + dot_nt(omega[1].astype(bf16), right)
-
-
-def send_halves(cross, chip, before, after):
-    @pl.when(is_even())
-    def _():
-        cross[...] = before
-        chip[...] = after
-
-    @pl.when(jnp.logical_not(is_even()))
-    def _():
-        cross[...] = after
-        chip[...] = before
-
-
-def cols_kernel(
-    blocks, coords, parts, s_before, s_own, s_after, t_before, t_own,
-    turned, cross, chip, own, slot_of,
-):
-    count, rows = parts.shape[0], parts.shape[2]
-    width = count * rows
-    find_slots(blocks, coords, slot_of)
-
-    def convert(pair, carry):
-        slot = slot_of[pair]
-        unit = jnp.where(pair == OWN_PAIR, OWN_PAIR, lax.rem(pair, 4) * 2 + pair // 4)
-
-        @pl.when(slot > 0)
-        def _():
-            for part in range(count):
-                turned[unit, :, part * rows : (part + 1) * rows] = parts[part, slot - BLK_DEV].T
-
-        @pl.when(slot == 0)
-        def _():
-            turned[unit] = jnp.zeros_like(turned[unit])
-
-        return carry
-
-    lax.fori_loop(0, OWN_PAIR + 1, convert, 0)
-    total = jnp.zeros(own.shape, f32)
-    for a in range(2 * BLK_DEV):
-        source = (s_before, s_own)[a // BLK_DEV]
-        blk = a % BLK_DEV
-        total += dot_nt(turned[2 * a : 2 * a + 2].reshape(2 * rows, width), source[:, blk * width : (blk + 1) * width])
-    send_halves(cross, chip, t_before[...], total.astype(bf16))
-    own[:rows] = t_own[:rows]
-    own[rows:] = t_own[rows:] + dot_nt(turned[OWN_PAIR], s_own[:, :width])
 
 
 def natural(out, pieces):
@@ -348,33 +331,36 @@
         from_cross = lax.ppermute(to_cross, "tiles", cross)
         return from_cross, from_chip
 
-    s_own = lax.all_gather(samples, "samp", axis=0, tiled=True)
+    def spread(x):
+        return lax.all_to_all(jnp.broadcast_to(x[None], (parts,) + x.shape), "samp", 0, 0)
+
+    s_own = spread(samples).reshape(count, wide)
     pieces = call(
-        cut_kernel, [VMEM, ANY], shape((parts, others, rows, rows), bf16),
-        [pltpu.VMEM((parts, others, rows, rows), bf16), pltpu.SemaphoreType.DMA((parts,))], 0, 4 << 20, out_specs=ANY,
-    )(omega, s_own)
+        cut_kernel, [ANY], shape((parts, others, rows, rows), bf16),
+        [
+            pltpu.VMEM((others, rows, width), f32), pltpu.VMEM((parts, others, rows, rows), bf16),
+            pltpu.SemaphoreType.DMA((others,)), pltpu.SemaphoreType.DMA((others,)),
+        ],
+        0, 4 << 20, out_specs=ANY,
+    )(omega)
     turned_parts = lax.all_to_all(pieces, "samp", 0, 0)
     s_cross, s_chip = exchange(s_own, s_own)
 
     window = shape((count, wide), bf16)
     part = shape((both, count), bf16)
     full = shape((both, count), f32)
-    held = pltpu.VMEM((OWN_PAIR + 1, rows, width), bf16)
     unit = rows * width * count
-    s_before, s_after, stq, t_before, t_own = call(
-        functools.partial(rows_kernel, blocks), [SMEM] + [VMEM] * 4,
-        (window, window, shape((3, both, count), bf16), part, full), [slots, held], 11 * unit, 4 << 20,
-    )(coords, omega, s_own, s_cross, s_chip)
-    turned, to_cross, to_chip, own = call(
-        functools.partial(cols_kernel, blocks), [SMEM] + [VMEM] * 6,
-        (shape((OWN_PAIR + 1, rows, width), bf16), part, part, full), [slots], 9 * unit, 3 << 20,
-    )(coords, turned_parts, s_before, s_own, s_after, t_before, t_own)
+    s_before, s_after, stq, turned, to_cross, to_chip, own = call(
+        functools.partial(begin_kernel, blocks), [SMEM] + [VMEM] * 5,
+        (window, window, shape((3, both, count), bf16), shape((OWN_PAIR + 1, rows, width), bf16), part, part, full),
+        [slots, pltpu.VMEM((OWN_PAIR + 1, rows, width), bf16)], 20 * unit, 6 << 20,
+    )(coords, omega, turned_parts, s_own, s_cross, s_chip)
 
     def products(to_cross, to_chip, finish):
         from_cross, from_chip = exchange(to_cross, to_chip)
         tiles, own = finish()
         total = own + from_cross.astype(f32) + from_chip.astype(f32)
-        p_own = lax.all_gather(total.astype(bf16), "samp", axis=0, tiled=False)
+        p_own = spread(total.astype(bf16))
         p_cross, p_chip = exchange(p_own, p_own)
         return tiles, p_own, p_cross, p_chip
 

time: 140 us -> 128 us (0.914)
  blocking collectives: 42.1 us -> 23.4 us
  starting transfers between devices: 43.2 us -> 54.4 us
  local copies, waits for them, and re-layouts: 9.71 us -> 4.65 us
    all_gather x3 -> x0, blocking collectives: 42.1 us -> none  [the longest x2 26.4 us: products(): p_own = lax.all_gather(total.astype(bf16), 'samp', axis=0, tiled=False)]
    all_to_all x0 -> x2, blocking collectives: none -> 23.4 us  [spread(): lax.all_to_all(jnp.broadcast_to(x[None], (parts,) + x.shape), 'samp', 0, 0)]
    all_to_all x0 -> x1, starting transfers between devices: none -> 9.32 us  [spread(): lax.all_to_all(jnp.broadcast_to(x[None], (parts,) + x.shape), 'samp', 0, 0)]
    unnamed x29 -> x9, local copies, waits for them, and re-layouts: 9.71 us -> 2.81 us
    ppermute x5, starting transfers between devices: 26.2 us -> 29.8 us  [exchange(): from_cross = lax.ppermute(to_cross, 'tiles', cross)]
    all_to_all x0 -> x1, waiting for transfers between devices: none -> 3.02 us  [spread(): lax.all_to_all(jnp.broadcast_to(x[None], (parts,) + x.shape), 'samp', 0, 0)]
    broadcast_in_dim x0 -> x3, local copies, waits for them, and re-layouts: none -> 1.84 us  [spread(): jnp.broadcast_to(x[None], (parts,) + x.shape)]
    ppermute x5, waiting for transfers between devices: 26.8 us -> 25 us  [exchange(): from_cross = lax.ppermute(to_cross, 'tiles', cross)]
  transfers between devices with their start and end apart: 11 -> 12, of which waited for: 6 -> 7; matrix products, arithmetic and copies ran while one was open for 0% -> 0% of each run, Pallas kernels for 6% -> 5%
where the time goes in v3:
time: 128 us; the launch traced here: 127 us
  starting transfers between devices  54.4 us (42%)
  waiting for transfers between devices  28.6 us (22%)
  blocking collectives  23.4 us (18%)
  Pallas kernels  15.5 us (12%)
  local copies, waits for them, and re-layouts  4.65 us (4%)
    ppermute x5, starting transfers between devices, exchange(): from_cross = lax.ppermute(to_cross, 'tiles', cross)  29.8 us
    ppermute x5, waiting for transfers between devices, exchange(): from_cross = lax.ppermute(to_cross, 'tiles', cross)  25 us
    all_to_all x2, blocking collectives, spread(): lax.all_to_all(jnp.broadcast_to(x[None], (parts,) + x.shape), 'samp', 0, 0)  23.4 us
    ppermute x5, starting transfers between devices, exchange(): from_chip = lax.ppermute(to_chip, 'tiles', chip)  9.57 us
    all_to_all x1, starting transfers between devices, spread(): lax.all_to_all(jnp.broadcast_to(x[None], (parts,) + x.shape), 'samp', 0, 0)  9.32 us
    all_to_all x1, starting transfers between devices, shards(): turned_parts = lax.all_to_all(pieces, 'samp', 0, 0)  5.66 us
    pallas_call x1, Pallas kernels, shards(): call(functools.partial(begin_kernel, blocks), [SMEM] + [VMEM] * 5, (windo...  3.73 us
    all_to_all x1, waiting for transfers between devices, spread(): lax.all_to_all(jnp.broadcast_to(x[None], (parts,) + x.shape), 'samp', 0, 0)  3.02 us
  transfers between devices with their start and end apart: 12, of which 7 were waited for; matrix products, arithmetic and copies ran while one was open for 0% of the time, Pallas kernels for 5%

profile of v3, /device:TPU:2, one launch (start us, length us, event | category | flops | bytes accessed | tf_op | source)
XLA Modules:
  0.0 126.9 jit_solution(17751622379659784386)
XLA Ops:
  1.8 9.3 %all-to-all-start.1 = ((bf16[4,64,1024]{2,1,0:T(8,128)(2,1)}), bf16[4,64,1024]{2,1,0:T(8,128)(2,1)S(1)}, u32[]{:S(2)}, u32[]{:S(2)}) async-start(bf16[4,64,1024]{2,1,0:T(8,128)(2,1)} %broadcast_in_dim.6), calls=%async_computation.1 | async-start | bytes 1048576 | tf_op jit(solution)/shard_map/all_to_all | solution.py:335
  14.7 3.0 %all-to-all-done.1 = bf16[4,64,1024]{2,1,0:T(8,128)(2,1)S(1)} async-done(((bf16[4,64,1024]{2,1,0:T(8,128)(2,1)}), bf16[4,64,1024]{2,1,0:T(8,128)(2,1)S(1)}, u32[]{:S(2)}, u32[]{:S(2)}) %all-to-all-start.1) | async-done | bytes 524320 | tf_op jit(solution)/shard_map/all_to_all | solution.py:335
  17.7 5.7 %all-to-all-start = ((bf16[4,8,128,128]{3,2,1,0:T(8,128)(2,1)}), bf16[4,8,128,128]{3,2,1,0:T(8,128)(2,1)}, u32[]{:S(2)}, u32[]{:S(2)}) async-start(bf16[4,8,128,128]{3,2,1,0:T(8,128)(2,1)} %copy-done.2), calls=%async_computation | async-start | bytes 2097152 | tf_op jit(solution)/shard_map/all_to_all | solution.py:346
  23.4 1.9 %collective-permute-start.1 = (bf16[256,1024]{1,0:T(8,128)(2,1)S(1)}, bf16[256,1024]{1,0:T(8,128)(2,1)}, u32[]{:S(2)}, u32[]{:S(2)}) collective-permute-start(bf16[256,1024]{1,0:T(8,128)(2,1)S(1)} %bitcast.1), channel_id=1, source_target_pairs={{0,4},{4,0},{8,12},{12,8},{16,20},{20,16},{24,28},{28,24},{32,36},... | collective-permute-start | bytes 1572872 | tf_op jit(solution)/shard_map/ppermute | solution.py:330
  25.3 10.9 %collective-permute-start = (bf16[256,1024]{1,0:T(8,128)(2,1)S(1)}, bf16[256,1024]{1,0:T(8,128)(2,1)}, u32[]{:S(2)}, u32[]{:S(2)}) collective-permute-start(bf16[256,1024]{1,0:T(8,128)(2,1)S(1)} %bitcast.2), channel_id=1, source_target_pairs={{0,508},{4,8},{8,4},{12,16},{16,12},{20,24},{24,20},{28,32},{32,28... | collective-permute-start | bytes 1572872 | tf_op jit(solution)/shard_map/ppermute | solution.py:331
  36.3 6.8 %collective-permute-done.s_cross = bf16[256,1024]{1,0:T(8,128)(2,1)} collective-permute-done((bf16[256,1024]{1,0:T(8,128)(2,1)S(1)}, bf16[256,1024]{1,0:T(8,128)(2,1)}, u32[]{:S(2)}, u32[]{:S(2)}) %collective-permute-start) | collective-permute-done | bytes 524320 | tf_op jit(solution)/shard_map/ppermute | solution.py:331
  43.1 3.7 %shard_map.38 = (bf16[256,1024]{1,0:T(8,128)(2,1)S(1)}, bf16[256,1024]{1,0:T(8,128)(2,1)S(1)}, bf16[3,256,256]{2,1,0:T(8,128)(2,1)S(1)}, bf16[9,128,512]{2,1,0:T...) custom-call(s32[10,2]{1,0:T(8,128)S(1)} %copy.10.coords.refs_0_, ...), custom_call_target="tpu_custom_call" | custom-call | flops 671088640 | bytes 6291456 | tf_op jit(solution)/shard_map/pallas_call | solution.py:353
  46.9 7.0 %collective-permute-start.2 = (bf16[256,256]{1,0:T(8,128)(2,1)S(1)}, bf16[256,256]{1,0:T(8,128)(2,1)S(1)}, u32[]{:S(2)}, u32[]{:S(2)}) collective-permute-start(bf16[256,256]{1,0:T(8,128)(2,1)S(1)} %get-tuple-element.25), channel_id=1, source_target_pairs={{0,508},{4,8},{8,4},{12,16},{16,12},{20,24},{24,20},{28,32},{32,28... | collective-permute-start | bytes 393224 | tf_op jit(solution)/shard_map/ppermute | solution.py:331
  53.8 1.9 %collective-permute-start.3 = (bf16[256,256]{1,0:T(8,128)(2,1)S(1)}, bf16[256,256]{1,0:T(8,128)(2,1)S(1)}, u32[]{:S(2)}, u32[]{:S(2)}) collective-permute-start(bf16[256,256]{1,0:T(8,128)(2,1)S(1)} %get-tuple-element.26), channel_id=1, source_target_pairs={{0,4},{4,0},{8,12},{12,8},{16,20},{20,16},{24,28},{28,24},{32,36},... | collective-permute-start | bytes 393224 | tf_op jit(solution)/shard_map/ppermute | solution.py:330
  57.2 12.9 %all_to_all.20.refs_5_.p_own = bf16[4,256,256]{2,1,0:T(8,128)(2,1)S(1)} all-to-all(bf16[4,256,256]{2,1,0:T(8,128)(2,1)S(1)} %broadcast_in_dim.7), channel_id=1, replica_groups=mesh['tiles'=128,'samp'=4] {'samp'}, dimensions={0} | all-to-all | bytes 1048576 | tf_op jit(solution)/shard_map/all_to_all | solution.py:335
  70.1 1.9 %collective-permute-start.5 = (bf16[4,256,256]{2,1,0:T(8,128)(2,1)S(1)}, bf16[4,256,256]{2,1,0:T(8,128)(2,1)S(1)}, u32[]{:S(2)}, u32[]{:S(2)}) collective-permute-start(bf16[4,256,256]{2,1,0:T(8,128)(2,1)S(1)} %all_to_all.20.refs_5_.p_own), channel_id=1, source_target_pairs={{0,4},{4,0},{8,12},{12,8},{16,20},{20,16},{24,28},{28,24},{32,36},... | collective-permute-start | bytes 1572872 | tf_op jit(solution)/shard_map/ppermute | solution.py:330
  72.0 3.2 %collective-permute-start.4 = (bf16[4,256,256]{2,1,0:T(8,128)(2,1)S(1)}, bf16[4,256,256]{2,1,0:T(8,128)(2,1)S(1)}, u32[]{:S(2)}, u32[]{:S(2)}) collective-permute-start(bf16[4,256,256]{2,1,0:T(8,128)(2,1)S(1)} %all_to_all.20.refs_5_.p_own), channel_id=1, source_target_pairs={{0,508},{4,8},{8,4},{12,16},{16,12},{20,24},{24,20},{28,32},{32,28... | collective-permute-start | bytes 1572872 | tf_op jit(solution)/shard_map/ppermute | solution.py:331
  75.2 1.9 %shard_map.39 = (f32[3,128,512]{2,1,0:T(8,128)S(1)}, f32[256,256]{1,0:T(8,128)S(1)}, bf16[1024,256]{1,0:T(8,128)(2,1)S(1)}) custom-call(s32[10,2]{1,0:T(8,128)S(1)} %copy.10.coords.refs_0_, f32[10,128,512]{2,1,0:T(8,128)S(1)} %copy-done.1, bf16[9,128,512]{2,1,0:T(8,128)(2,1)S(1)} %get-tuple-element.20.refs_2_.turned, bf16[256,1024]{1,0:T(8,128)(2,1)S(1)} %bitcast.4, ...), custom_call_target="tpu_custom_call" | custom-call | flops 402653184 | bytes 4194304 | tf_op jit(solution)/shard_map/pallas_call | solution.py:374
  77.2 8.6 %collective-permute-done.4.p_cross = bf16[4,256,256]{2,1,0:T(8,128)(2,1)S(1)} collective-permute-done((bf16[4,256,256]{2,1,0:T(8,128)(2,1)S(1)}, bf16[4,256,256]{2,1,0:T(8,128)(2,1)S(1)}, u32[]{:S(2)}, u32[]{:S(2)}) %collective-permute-start.4) | collective-permute-done | bytes 524320 | tf_op jit(solution)/shard_map/ppermute | solution.py:331
  85.8 2.6 %shard_map.40 = (f32[4,128,512]{2,1,0:T(8,128)S(1)}, bf16[256,256]{1,0:T(8,128)(2,1)S(1)}, bf16[256,256]{1,0:T(8,128)(2,1)S(1)}) custom-call(s32[10,2]{1,0:T(8,128)S(1)} %copy.10.coords.refs_0_, f32[10,128,512]{2,1,0:T(8,128)S(1)} %copy-done.1, bf16[9,128,512]{2,1,0:T(8,128)(2,1)S(1)} %get-tuple-element.20.refs_2_.turned, ...), custom_call_target="tpu_custom_call" | custom-call | flops 1207959552 | bytes 6291456 | tf_op jit(solution)/shard_map/pallas_call | solution.py:378
  88.4 3.2 %collective-permute-start.6 = (bf16[256,256]{1,0:T(8,128)(2,1)S(1)}, bf16[256,256]{1,0:T(8,128)(2,1)S(1)}, u32[]{:S(2)}, u32[]{:S(2)}) collective-permute-start(bf16[256,256]{1,0:T(8,128)(2,1)S(1)} %get-tuple-element.32), channel_id=1, source_target_pairs={{0,508},{4,8},{8,4},{12,16},{16,12},{20,24},{24,20},{28,32},{32,28... | collective-permute-start | bytes 393224 | tf_op jit(solution)/shard_map/ppermute | solution.py:331
  91.7 1.9 %collective-permute-start.7 = (bf16[256,256]{1,0:T(8,128)(2,1)S(1)}, bf16[256,256]{1,0:T(8,128)(2,1)S(1)}, u32[]{:S(2)}, u32[]{:S(2)}) collective-permute-start(bf16[256,256]{1,0:T(8,128)(2,1)S(1)} %get-tuple-element.33), channel_id=1, source_target_pairs={{0,4},{4,0},{8,12},{12,8},{16,20},{20,16},{24,28},{28,24},{32,36},... | collective-permute-start | bytes 393224 | tf_op jit(solution)/shard_map/ppermute | solution.py:330
  95.1 2.9 %collective-permute-done.6 = bf16[256,256]{1,0:T(8,128)(2,1)S(1)} collective-permute-done((bf16[256,256]{1,0:T(8,128)(2,1)S(1)}, bf16[256,256]{1,0:T(8,128)(2,1)S(1)}, u32[]{:S(2)}, u32[]{:S(2)}) %collective-permute-start.6) | collective-permute-done | bytes 131104 | tf_op jit(solution)/shard_map/ppermute | solution.py:331
  98.1 10.5 %all_to_all.21.refs_4_.p_own = bf16[4,256,256]{2,1,0:T(8,128)(2,1)S(1)} all-to-all(bf16[4,256,256]{2,1,0:T(8,128)(2,1)S(1)} %broadcast_in_dim.8), channel_id=1, replica_groups=mesh['tiles'=128,'samp'=4] {'samp'}, dimensions={0} | all-to-all | bytes 1048576 | tf_op jit(solution)/shard_map/all_to_all | solution.py:335
  108.6 1.9 %collective-permute-start.9 = (bf16[4,256,256]{2,1,0:T(8,128)(2,1)S(1)}, bf16[4,256,256]{2,1,0:T(8,128)(2,1)S(1)}, u32[]{:S(2)}, u32[]{:S(2)}) collective-permute-start(bf16[4,256,256]{2,1,0:T(8,128)(2,1)S(1)} %all_to_all.21.refs_4_.p_own), channel_id=1, source_target_pairs={{0,4},{4,0},{8,12},{12,8},{16,20},{20,16},{24,28},{28,24},{32,36},... | collective-permute-start | bytes 1572872 | tf_op jit(solution)/shard_map/ppermute | solution.py:330
  110.5 5.6 %collective-permute-start.8 = (bf16[4,256,256]{2,1,0:T(8,128)(2,1)S(1)}, bf16[4,256,256]{2,1,0:T(8,128)(2,1)S(1)}, u32[]{:S(2)}, u32[]{:S(2)}) collective-permute-start(bf16[4,256,256]{2,1,0:T(8,128)(2,1)S(1)} %all_to_all.21.refs_4_.p_own), channel_id=1, source_target_pairs={{0,508},{4,8},{8,4},{12,16},{16,12},{20,24},{24,20},{28,32},{32,28... | collective-permute-start | bytes 1572872 | tf_op jit(solution)/shard_map/ppermute | solution.py:331
  116.1 2.3 %shard_map.42.begun = f32[10,128,512]{2,1,0:T(8,128)} custom-call(s32[10,2]{1,0:T(8,128)S(1)} %copy.10.coords.refs_0_, f32[3,128,512]{2,1,0:T(8,128)S(1)} %get-tuple-element.34.refs_1_, bf16[256,1024]{1,0:T(8,128)(2,1)S(1)} %bitcast.7, bf16[3,256,256]{2,1,0:T(8,128)(2,1)S(1)} %get-tuple-element.23.refs_4_.stq.refs_3_, ...), custom_call_target="tpu_custom_call" | custom-call | flops 268435456 | bytes 3145728 | tf_op jit(solution)/shard_map/pallas_call | solution.py:391
  118.4 5.9 %collective-permute-done.8.p_cross = bf16[4,256,256]{2,1,0:T(8,128)(2,1)S(1)} collective-permute-done((bf16[4,256,256]{2,1,0:T(8,128)(2,1)S(1)}, bf16[4,256,256]{2,1,0:T(8,128)(2,1)S(1)}, u32[]{:S(2)}, u32[]{:S(2)}) %collective-permute-start.8) | collective-permute-done | bytes 524320 | tf_op jit(solution)/shard_map/ppermute | solution.py:331
  124.3 2.5 %shard_map.43 = f32[10,128,512]{2,1,0:T(8,128)} custom-call(s32[10,2]{1,0:T(8,128)S(1)} %copy.10.coords.refs_0_, f32[4,128,512]{2,1,0:T(8,128)S(1)} %get-tuple-element.28.outer, f32[4,128,512]{2,1,0:T(8,128)S(1)} %get-tuple-element.30.inner, bf16[256,1024]{1,0:T(8,128)(2,1)S(1)} %get-tuple-element.22.s_after, ...), custom_call_target="tpu_custom_call", output_to_operand_aliasing={{}: (8, {})} | custom-call | flops 536870912 | bytes 6291456 | tf_op jit(solution)/shard_map/pallas_call | solution.py:396
  (23 shorter events, 8.5 us)
Async XLA Ops:
  1.8 15.9 %all-to-all-start.1 = ((bf16[4,64,1024]{2,1,0:T(8,128)(2,1)}), bf16[4,64,1024]{2,1,0:T(8,128)(2,1)S(1)}, u32[]{:S(2)}, u32[]{:S(2)}) async-start(bf16[4,64,1024]{2,1,0:T(8,128)(2,1)} %broadcast_in_dim.6), calls=%async_computation.1 | async-start | bytes 1048576 | tf_op jit(solution)/shard_map/all_to_all | solution.py:335
  11.1 1.7 %copy-start = (f32[10,128,512]{2,1,0:T(8,128)S(1)}, f32[10,128,512]{2,1,0:T(8,128)}, u32[]{:S(2)}) copy-start(f32[10,128,512]{2,1,0:T(8,128)} %omega.7) | copy-start | bytes 7864324
  12.8 23.3 %copy-start.3 = (s32[10,2]{0,1:T(2,128)S(1)}, s32[10,2]{0,1:T(2,128)}, u32[]{:S(2)}) copy-start(s32[10,2]{0,1:T(2,128)} %param.5) | copy-start | bytes 244
  12.8 30.3 %copy-start.1 = (f32[10,128,512]{2,1,0:T(8,128)S(1)}, f32[10,128,512]{2,1,0:T(8,128)}, u32[]{:S(2)}) copy-start(f32[10,128,512]{2,1,0:T(8,128)} %omega.7) | copy-start | bytes 7864324
  13.7 1.0 copy-start.2
  17.7 18.5 %all-to-all-start = ((bf16[4,8,128,128]{3,2,1,0:T(8,128)(2,1)}), bf16[4,8,128,128]{3,2,1,0:T(8,128)(2,1)}, u32[]{:S(2)}, u32[]{:S(2)}) async-start(bf16[4,8,128,128]{3,2,1,0:T(8,128)(2,1)} %copy-done.2), calls=%async_computation | async-start | bytes 2097152 | tf_op jit(solution)/shard_map/all_to_all | solution.py:346
  23.4 12.9 %collective-permute-start.1 = (bf16[256,1024]{1,0:T(8,128)(2,1)S(1)}, bf16[256,1024]{1,0:T(8,128)(2,1)}, u32[]{:S(2)}, u32[]{:S(2)}) collective-permute-start(bf16[256,1024]{1,0:T(8,128)(2,1)S(1)} %bitcast.1), channel_id=1, source_target_pairs={{0,4},{4,0},{8,12},{12,8},{16,20},{20,16},{24,28},{28,24},{32,36},... | collective-permute-start | bytes 1572872 | tf_op jit(solution)/shard_map/ppermute | solution.py:330
  25.3 17.8 %collective-permute-start = (bf16[256,1024]{1,0:T(8,128)(2,1)S(1)}, bf16[256,1024]{1,0:T(8,128)(2,1)}, u32[]{:S(2)}, u32[]{:S(2)}) collective-permute-start(bf16[256,1024]{1,0:T(8,128)(2,1)S(1)} %bitcast.2), channel_id=1, source_target_pairs={{0,508},{4,8},{8,4},{12,16},{16,12},{20,24},{24,20},{28,32},{32,28... | collective-permute-start | bytes 1572872 | tf_op jit(solution)/shard_map/ppermute | solution.py:331
  46.9 9.6 %collective-permute-start.2 = (bf16[256,256]{1,0:T(8,128)(2,1)S(1)}, bf16[256,256]{1,0:T(8,128)(2,1)S(1)}, u32[]{:S(2)}, u32[]{:S(2)}) collective-permute-start(bf16[256,256]{1,0:T(8,128)(2,1)S(1)} %get-tuple-element.25), channel_id=1, source_target_pairs={{0,508},{4,8},{8,4},{12,16},{16,12},{20,24},{24,20},{28,32},{32,28... | collective-permute-start | bytes 393224 | tf_op jit(solution)/shard_map/ppermute | solution.py:331
  53.8 3.2 %collective-permute-start.3 = (bf16[256,256]{1,0:T(8,128)(2,1)S(1)}, bf16[256,256]{1,0:T(8,128)(2,1)S(1)}, u32[]{:S(2)}, u32[]{:S(2)}) collective-permute-start(bf16[256,256]{1,0:T(8,128)(2,1)S(1)} %get-tuple-element.26), channel_id=1, source_target_pairs={{0,4},{4,0},{8,12},{12,8},{16,20},{20,16},{24,28},{28,24},{32,36},... | collective-permute-start | bytes 393224 | tf_op jit(solution)/shard_map/ppermute | solution.py:330
  70.1 7.1 %collective-permute-start.5 = (bf16[4,256,256]{2,1,0:T(8,128)(2,1)S(1)}, bf16[4,256,256]{2,1,0:T(8,128)(2,1)S(1)}, u32[]{:S(2)}, u32[]{:S(2)}) collective-permute-start(bf16[4,256,256]{2,1,0:T(8,128)(2,1)S(1)} %all_to_all.20.refs_5_.p_own), channel_id=1, source_target_pairs={{0,4},{4,0},{8,12},{12,8},{16,20},{20,16},{24,28},{28,24},{32,36},... | collective-permute-start | bytes 1572872 | tf_op jit(solution)/shard_map/ppermute | solution.py:330
  72.0 13.8 %collective-permute-start.4 = (bf16[4,256,256]{2,1,0:T(8,128)(2,1)S(1)}, bf16[4,256,256]{2,1,0:T(8,128)(2,1)S(1)}, u32[]{:S(2)}, u32[]{:S(2)}) collective-permute-start(bf16[4,256,256]{2,1,0:T(8,128)(2,1)S(1)} %all_to_all.20.refs_5_.p_own), channel_id=1, source_target_pairs={{0,508},{4,8},{8,4},{12,16},{16,12},{20,24},{24,20},{28,32},{32,28... | collective-permute-start | bytes 1572872 | tf_op jit(solution)/shard_map/ppermute | solution.py:331
  88.4 9.6 %collective-permute-start.6 = (bf16[256,256]{1,0:T(8,128)(2,1)S(1)}, bf16[256,256]{1,0:T(8,128)(2,1)S(1)}, u32[]{:S(2)}, u32[]{:S(2)}) collective-permute-start(bf16[256,256]{1,0:T(8,128)(2,1)S(1)} %get-tuple-element.32), channel_id=1, source_target_pairs={{0,508},{4,8},{8,4},{12,16},{16,12},{20,24},{24,20},{28,32},{32,28... | collective-permute-start | bytes 393224 | tf_op jit(solution)/shard_map/ppermute | solution.py:331
  91.7 6.4 %collective-permute-start.7 = (bf16[256,256]{1,0:T(8,128)(2,1)S(1)}, bf16[256,256]{1,0:T(8,128)(2,1)S(1)}, u32[]{:S(2)}, u32[]{:S(2)}) collective-permute-start(bf16[256,256]{1,0:T(8,128)(2,1)S(1)} %get-tuple-element.33), channel_id=1, source_target_pairs={{0,4},{4,0},{8,12},{12,8},{16,20},{20,16},{24,28},{28,24},{32,36},... | collective-permute-start | bytes 393224 | tf_op jit(solution)/shard_map/ppermute | solution.py:330
  108.6 9.8 %collective-permute-start.9 = (bf16[4,256,256]{2,1,0:T(8,128)(2,1)S(1)}, bf16[4,256,256]{2,1,0:T(8,128)(2,1)S(1)}, u32[]{:S(2)}, u32[]{:S(2)}) collective-permute-start(bf16[4,256,256]{2,1,0:T(8,128)(2,1)S(1)} %all_to_all.21.refs_4_.p_own), channel_id=1, source_target_pairs={{0,4},{4,0},{8,12},{12,8},{16,20},{20,16},{24,28},{28,24},{32,36},... | collective-permute-start | bytes 1572872 | tf_op jit(solution)/shard_map/ppermute | solution.py:330
  110.5 13.8 %collective-permute-start.8 = (bf16[4,256,256]{2,1,0:T(8,128)(2,1)S(1)}, bf16[4,256,256]{2,1,0:T(8,128)(2,1)S(1)}, u32[]{:S(2)}, u32[]{:S(2)}) collective-permute-start(bf16[4,256,256]{2,1,0:T(8,128)(2,1)S(1)} %all_to_all.21.refs_4_.p_own), channel_id=1, source_target_pairs={{0,508},{4,8},{8,4},{12,16},{16,12},{20,24},{24,20},{28,32},{32,28... | collective-permute-start | bytes 1572872 | tf_op jit(solution)/shard_map/ppermute | solution.py:331

commit v4 on v3

--- a/solution.py
+++ b/solution.py
@@ -15,6 +15,7 @@
 VMEM = pl.BlockSpec(memory_space=pltpu.VMEM)
 SMEM = pl.BlockSpec(memory_space=pltpu.SMEM)
 ANY = pl.BlockSpec(memory_space=pl.ANY)
+HBM = pl.BlockSpec(memory_space=pltpu.HBM)
 bf16, f32 = jnp.bfloat16, jnp.float32
 
 OWN_PAIR = 8
@@ -60,6 +61,17 @@
 
 def is_even():
     return lax.rem(lax.axis_index("tiles"), 2) == 0
+
+
+def repeat_kernel(x, out, held, in_sem, out_sems):
+    load = pltpu.make_async_copy(x, held, in_sem)
+    load.start()
+    load.wait()
+    stores = [pltpu.make_async_copy(held, out.at[part], out_sems.at[part]) for part in range(out.shape[0])]
+    for store in stores:
+        store.start()
+    for store in stores:
+        store.wait()
 
 
 def cut_kernel(omega, out, held, pieces, in_sems, out_sems):
@@ -74,7 +86,7 @@
     for k in range(others):
         loads[k].wait()
         for part in range(out.shape[0]):
-            pieces[part, k] = held[k, :, part * rows : (part + 1) * rows].astype(bf16)
+            pieces[part, k] = held[k, :, part * rows : (part + 1) * rows].astype(bf16).T
         stores.append(pltpu.make_async_copy(pieces.at[:, k], out.at[:, k], out_sems.at[k]))
         stores[-1].start()
     for store in stores:
@@ -95,59 +107,91 @@
 
 def begin_kernel(
     blocks, coords, omega, parts, s_own, s_cross, s_chip,
-    s_before, s_after, stq, turned, cross, chip, own, slot_of, mats,
+    s_before, s_after, turned, cross, chip, own, slot_of, mats, s_sems, t_sems,
 ):
     rows, width = omega.shape[1:]
-    quarter = lax.axis_index("samp")
-    find_slots(blocks, coords, slot_of)
-
-    @pl.when(is_even())
-    def _():
-        s_before[...] = s_cross[...]
-        s_after[...] = s_chip[...]
-
-    @pl.when(jnp.logical_not(is_even()))
-    def _():
-        s_before[...] = s_chip[...]
-        s_after[...] = s_cross[...]
+    count = parts.shape[0]
+    find_slots(blocks, coords, slot_of)
+    even = is_even()
+
+    def windows(before, after):
+        return (
+            pltpu.make_async_copy(before, s_before, s_sems.at[0]),
+            pltpu.make_async_copy(after, s_after, s_sems.at[1]),
+        )
+
+    @pl.when(even)
+    def _():
+        for copy in windows(s_cross, s_chip):
+            copy.start()
+
+    @pl.when(jnp.logical_not(even))
+    def _():
+        for copy in windows(s_chip, s_cross):
+            copy.start()
+
+    def fill(pair):
+        slot = slot_of[pair]
+        unit = OWN_PAIR if pair == OWN_PAIR else pair % 4 * 2 + pair // 4
+        copies = [
+            pltpu.make_async_copy(
+                parts.at[part, slot - BLK_DEV],
+                turned.at[unit, :, part * rows : (part + 1) * rows],
+                t_sems.at[pair, part],
+            )
+            for part in range(count)
+        ]
+        return slot, unit, copies
+
+    for pair in range(OWN_PAIR + 1):
+        slot, unit, copies = fill(pair)
+
+        @pl.when(slot > 0)
+        def _(copies=copies):
+            for copy in copies:
+                copy.start()
+
+        @pl.when(slot == 0)
+        def _(unit=unit):
+            turned[unit] = jnp.zeros_like(turned[unit])
 
     def convert(pair, carry):
         slot = slot_of[pair]
-        unit = jnp.where(pair == OWN_PAIR, OWN_PAIR, lax.rem(pair, 4) * 2 + pair // 4)
 
         @pl.when(slot > 0)
         def _():
             mats[pair] = omega[slot].astype(bf16)
-            for part in range(width // rows):
-                turned[unit, :, part * rows : (part + 1) * rows] = parts[part, slot - BLK_DEV].T
 
         @pl.when(slot == 0)
         def _():
             mats[pair] = jnp.zeros_like(mats[pair])
-            turned[unit] = jnp.zeros_like(turned[unit])
 
         return carry
 
     lax.fori_loop(0, OWN_PAIR + 1, convert, 0)
+    left, right = s_own[:, :width], s_own[:, width:]
+    own[:rows] = dot_nt(omega[0].astype(bf16), left) + dot_nt(mats[OWN_PAIR], right)
+    own[rows:] = dot_nt(omega[1].astype(bf16), right)
+    for copy in windows(s_chip, s_chip):
+        copy.wait()
     total = dot_nt(mats[0:4].reshape(4 * rows, width), s_after[:, :width])
     total += dot_nt(mats[4:8].reshape(4 * rows, width), s_after[:, width:])
-    left, right = s_own[:, :width], s_own[:, width:]
-    own[:rows] = total[2 * rows : 3 * rows] + (
-        dot_nt(omega[0].astype(bf16), left) + dot_nt(mats[OWN_PAIR], right)
-    )
-    own[rows:] = total[3 * rows :] + (
-        dot_nt(omega[1].astype(bf16), right) + dot_nt(turned[OWN_PAIR], left)
-    )
+    own[...] += total[2 * rows :]
+    for pair in range(OWN_PAIR + 1):
+        slot, unit, copies = fill(pair)
+
+        @pl.when(slot > 0)
+        def _(copies=copies):
+            for copy in copies:
+                copy.wait()
+
+    own[rows:] += dot_nt(turned[OWN_PAIR], left)
     after = jnp.zeros(own.shape, f32)
     for a in range(2 * BLK_DEV):
         source = (s_before, s_own)[a // BLK_DEV]
         blk = a % BLK_DEV
         after += dot_nt(turned[2 * a : 2 * a + 2].reshape(2 * rows, width), source[:, blk * width : (blk + 1) * width])
     send_halves(cross, chip, total[: 2 * rows].astype(bf16), after.astype(bf16))
-    for side, ref in enumerate((s_before, s_own, s_after)):
-        for blk in range(BLK_DEV):
-            at = pl.multiple_of(blk * width + quarter * rows, rows)
-            stq[side, blk * rows : (blk + 1) * rows, :] = ref[:, pl.ds(at, rows)].T
 
 
 def natural(out, pieces):
@@ -159,38 +203,31 @@
             out[at : at + rows, :] = pieces[part, blk * rows : (blk + 1) * rows, :]
 
 
-def own_kernel(blocks, last, *refs):
-    if last:
-        coords, held, s_own, stq, p_own, out, slot_of, grad, nat_own, tiles, sems = refs
-    else:
-        coords, omega, turned, s_own, stq, p_own, tiles, t_own, nat_own, slot_of, grad, mats = refs
+def transpose_columns(stq, windows, quarter):
+    rows = stq.shape[1] // BLK_DEV
+    width = windows[0].shape[1] // BLK_DEV
+    for side, ref in enumerate(windows):
+        for blk in range(BLK_DEV):
+            at = pl.multiple_of(blk * width + quarter * rows, rows)
+            stq[side, blk * rows : (blk + 1) * rows, :] = ref[:, pl.ds(at, rows)].T
+
+
+def own_kernel(
+    blocks, coords, omega, turned, s_before, s_own, s_after, p_own,
+    tiles, t_own, nat_own, stq, cols_half, rows_half, slot_of, grad, mats,
+):
     rows, width = grad.shape[0] // 2, grad.shape[1] // 2
     quarter = lax.axis_index("samp")
     scale = step_size / (2.0 * s_own.shape[0])
     find_slots(blocks, coords, slot_of)
+    transpose_columns(stq, (s_before, s_own, s_after), quarter)
     natural(nat_own, p_own)
     grad[...] = dot_nn(p_own[quarter], s_own[...]) + dot_nt(stq[1], nat_own[...])
     slot = slot_of[OWN_PAIR]
     for i in range(BLK_DEV):
-        old = held[i] if last else omega[i]
         here = grad[i * rows : (i + 1) * rows, i * width : (i + 1) * width]
-        tiles[i] = shrink_diagonal(old - scale * here, quarter)
-    old = held[2] if last else omega[slot]
-    tiles[2] = shrink(old - scale * grad[:rows, width:])
-    if last:
-        copies = [pltpu.make_async_copy(tiles.at[i], out.at[i], sems.at[i]) for i in range(BLK_DEV)]
-        for copy in copies:
-            copy.start()
-
-        @pl.when(slot > 0)
-        def _():
-            copy = pltpu.make_async_copy(tiles.at[2], out.at[slot], sems.at[2])
-            copy.start()
-            copy.wait()
-
-        for copy in copies:
-            copy.wait()
-        return
+        tiles[i] = shrink_diagonal(omega[i] - scale * here, quarter)
+    tiles[2] = shrink(omega[slot] - scale * grad[:rows, width:])
     mats[:rows, :width] = tiles[0].astype(bf16)
     mats[rows:, width:] = tiles[1].astype(bf16)
 
@@ -206,6 +243,39 @@
         mats[rows:, :width] = jnp.zeros((rows, width), bf16)
 
     t_own[...] = dot_nt(mats[...], s_own[...])
+    cols_half[...] = dot_nt(stq[2], nat_own[...])
+    rows_half[...] = dot_nn(p_own[quarter], s_after[...])
+
+
+def own_last_kernel(
+    blocks, coords, held, s_own, s_after, stq, p_own, out, rows_half, slot_of, grad, nat_own, tiles, sems,
+):
+    rows, width = grad.shape[0] // 2, grad.shape[1] // 2
+    quarter = lax.axis_index("samp")
+    scale = step_size / (2.0 * s_own.shape[0])
+    find_slots(blocks, coords, slot_of)
+    natural(nat_own, p_own)
+    grad[...] = dot_nn(p_own[quarter], s_own[...]) + dot_nt(stq[1], nat_own[...])
+    slot = slot_of[OWN_PAIR]
+    copies = [pltpu.make_async_copy(tiles.at[i], out.at[i], sems.at[i]) for i in range(BLK_DEV)]
+    copies.append(pltpu.make_async_copy(tiles.at[2], out.at[slot], sems.at[2]))
+    for i in range(BLK_DEV):
+        here = grad[i * rows : (i + 1) * rows, i * width : (i + 1) * width]
+        tiles[i] = shrink_diagonal(held[i] - scale * here, quarter)
+        copies[i].start()
+    tiles[2] = shrink(held[2] - scale * grad[:rows, width:])
+
+    @pl.when(slot > 0)
+    def _():
+        copies[2].start()
+
+    rows_half[...] = dot_nn(p_own[quarter], s_after[...])
+    for i in range(BLK_DEV):
+        copies[i].wait()
+
+    @pl.when(slot > 0)
+    def _():
+        copies[2].wait()
 
 
 def order_halo(nat, ptq, p_cross, p_chip, quarter):
@@ -228,7 +298,7 @@
 
 
 def outer_kernel(
-    blocks, coords, omega, turned, s_before, s_own, s_after, stq, nat_own, p_cross, p_chip,
+    blocks, coords, omega, turned, s_before, s_own, s_after, stq, cols_half, p_cross, p_chip,
     tiles, cross, chip, slot_of, nat, ptq, grad, mats, half,
 ):
     rows, width = omega.shape[1:]
@@ -241,8 +311,8 @@
         blk = a % BLK_DEV
         at = slice(blk * width, (blk + 1) * width)
         source = (s_before, s_own)[a // BLK_DEV][:, at]
-        product = (nat.at[0], nat_own)[a // BLK_DEV][at, :]
-        half[...] = dot_nn(ptq[1], source) + dot_nt(stq[2], product)
+        other = dot_nt(stq[2], nat[0, at, :]) if a < BLK_DEV else cols_half[:, at]
+        half[...] = dot_nn(ptq[1], source) + other
         for b in range(BLK_DEV):
             tile = shrink(turned[2 * a + b].astype(f32) - scale * half[b * rows : (b + 1) * rows, :])
             tile = jnp.where(slot_of[b * 4 + a] > 0, tile, 0.0)
@@ -256,20 +326,20 @@
 
 
 def inner_kernel(
-    blocks, coords, omega, s_own, s_after, stq, p_own, p_cross, p_chip, t_own,
+    blocks, coords, omega, s_own, s_after, stq, rows_half, p_cross, p_chip, t_own,
     tiles, own, slot_of, nat, ptq, grad, mats,
 ):
     quarter = lax.axis_index("samp")
     scale = step_size / (2.0 * s_own.shape[0])
     find_slots(blocks, coords, slot_of)
     order_halo(nat, ptq, p_cross, p_chip, quarter)
-    grad[...] = dot_nn(p_own[quarter], s_after[...]) + dot_nt(stq[1], nat[1])
+    grad[...] = rows_half[...] + dot_nt(stq[1], nat[1])
     update_rows(slot_of, omega, grad, BLK_DEV, scale, tiles, mats)
     own[...] = t_own[...] + dot_nt(mats[...], s_after[...])
 
 
 def last_kernel(
-    blocks, coords, outer, inner, s_after, stq, p_own, p_cross, p_chip, begun,
+    blocks, coords, outer, inner, s_after, stq, rows_half, p_cross, p_chip, begun,
     out, slot_of, nat, ptq, grad, tiles, sems,
 ):
     rows, width = tiles.shape[1:]
@@ -278,8 +348,8 @@
     find_slots(blocks, coords, slot_of)
     order_halo(nat, ptq, p_cross, p_chip, quarter)
     for group in range(2):
-        lhs = ptq[0] if group == 0 else p_own[quarter]
-        grad[group] = dot_nn(lhs, s_after[...]) + dot_nt(stq[group], nat[1])
+        other = dot_nn(ptq[0], s_after[...]) if group == 0 else rows_half[...]
+        grad[group] = other + dot_nt(stq[group], nat[1])
         for a in range(2):
             for b in range(2):
                 unit = group * 4 + a * 2 + b
@@ -334,15 +404,20 @@
     def spread(x):
         return lax.all_to_all(jnp.broadcast_to(x[None], (parts,) + x.shape), "samp", 0, 0)
 
-    s_own = spread(samples).reshape(count, wide)
+    copies = call(
+        repeat_kernel, [HBM], pltpu.HBM((parts,) + samples.shape, bf16),
+        [pltpu.VMEM(samples.shape, bf16), pltpu.SemaphoreType.DMA, pltpu.SemaphoreType.DMA((parts,))],
+        0, 1 << 20, out_specs=HBM,
+    )(pltpu.with_memory_space_constraint(samples, pltpu.HBM))
+    s_own = lax.all_to_all(copies, "samp", 0, 0).reshape(count, wide)
     pieces = call(
-        cut_kernel, [ANY], shape((parts, others, rows, rows), bf16),
+        cut_kernel, [HBM], pltpu.HBM((parts, others, rows, rows), bf16),
         [
             pltpu.VMEM((others, rows, width), f32), pltpu.VMEM((parts, others, rows, rows), bf16),
             pltpu.SemaphoreType.DMA((others,)), pltpu.SemaphoreType.DMA((others,)),
         ],
-        0, 4 << 20, out_specs=ANY,
-    )(omega)
+        0, 4 << 20, out_specs=HBM,
+    )(pltpu.with_memory_space_constraint(omega, pltpu.HBM))
     turned_parts = lax.all_to_all(pieces, "samp", 0, 0)
     s_cross, s_chip = exchange(s_own, s_own)
 
@@ -350,10 +425,14 @@
     part = shape((both, count), bf16)
     full = shape((both, count), f32)
     unit = rows * width * count
-    s_before, s_after, stq, turned, to_cross, to_chip, own = call(
-        functools.partial(begin_kernel, blocks), [SMEM] + [VMEM] * 5,
-        (window, window, shape((3, both, count), bf16), shape((OWN_PAIR + 1, rows, width), bf16), part, part, full),
-        [slots, pltpu.VMEM((OWN_PAIR + 1, rows, width), bf16)], 20 * unit, 6 << 20,
+    s_before, s_after, turned, to_cross, to_chip, own = call(
+        functools.partial(begin_kernel, blocks), [SMEM, VMEM, ANY, VMEM, ANY, ANY],
+        (window, window, shape((OWN_PAIR + 1, rows, width), bf16), part, part, full),
+        [
+            slots, pltpu.VMEM((OWN_PAIR + 1, rows, width), bf16),
+            pltpu.SemaphoreType.DMA((2,)), pltpu.SemaphoreType.DMA((OWN_PAIR + 1, parts)),
+        ],
+        20 * unit, 6 << 20,
     )(coords, omega, turned_parts, s_own, s_cross, s_chip)
 
     def products(to_cross, to_chip, finish):
@@ -371,33 +450,38 @@
     four = shape((4, rows, width), f32)
 
     _, p_own, p_cross, p_chip = products(to_cross, to_chip, lambda: (None, own))
-    mine, t_own, nat_own = call(
-        functools.partial(own_kernel, blocks, False), [SMEM] + [VMEM] * 5,
-        (shape((3, rows, width), f32), full, shape((wide, count), bf16)), [slots, grad, mats], 12 * unit, 4 << 20,
-    )(coords, omega, turned, s_own, stq, p_own)
+    wide_half = shape((both, wide), f32)
+    mine, t_own, _, stq, cols_half, rows_half = call(
+        functools.partial(own_kernel, blocks), [SMEM] + [VMEM] * 6,
+        (
+            shape((3, rows, width), f32), full, shape((wide, count), bf16), shape((3, both, count), bf16),
+            wide_half, wide_half,
+        ),
+        [slots, grad, mats], 20 * unit, 6 << 20,
+    )(coords, omega, turned, s_before, s_own, s_after, p_own)
     outer, to_cross, to_chip = call(
         functools.partial(outer_kernel, blocks), [SMEM] + [VMEM] * 9,
-        (four, part, part), [slots, nat, ptq, grad, mats, pltpu.VMEM((both, width), f32)], 36 * unit, 6 << 20,
-    )(coords, omega, turned, s_before, s_own, s_after, stq, nat_own, p_cross, p_chip)
+        (four, part, part), [slots, nat, ptq, grad, mats, pltpu.VMEM((both, width), f32)], 32 * unit, 6 << 20,
+    )(coords, omega, turned, s_before, s_own, s_after, stq, cols_half, p_cross, p_chip)
 
     def finish():
         return call(
             functools.partial(inner_kernel, blocks), [SMEM] + [VMEM] * 8,
-            (four, full), [slots, nat, ptq, grad, mats], 12 * unit, 4 << 20,
-        )(coords, omega, s_own, s_after, stq, p_own, p_cross, p_chip, t_own)
+            (four, full), [slots, nat, ptq, grad, mats], 8 * unit, 4 << 20,
+        )(coords, omega, s_own, s_after, stq, rows_half, p_cross, p_chip, t_own)
 
     inner, p_own, p_cross, p_chip = products(to_cross, to_chip, finish)
     whole = shape(omega.shape, f32)
-    begun = call(
-        functools.partial(own_kernel, blocks, True), [SMEM] + [VMEM] * 4, whole,
+    begun, rows_half = call(
+        functools.partial(own_last_kernel, blocks), [SMEM] + [VMEM] * 5, (whole, wide_half),
         [slots, grad, pltpu.VMEM((wide, count), bf16), pltpu.VMEM((3, rows, width), f32), pltpu.SemaphoreType.DMA((3,))],
-        8 * unit, 3 << 20, out_specs=ANY,
-    )(coords, mine, s_own, stq, p_own)
+        12 * unit, 3 << 20, out_specs=(ANY, VMEM),
+    )(coords, mine, s_own, s_after, stq, p_own)
     return call(
         functools.partial(last_kernel, blocks), [SMEM] + [VMEM] * 7 + [ANY], whole,
         [slots, nat, ptq, pltpu.VMEM((2, both, wide), f32), pltpu.VMEM((8, rows, width), f32), pltpu.SemaphoreType.DMA((8,))],
-        16 * unit, 6 << 20, aliases={8: 0}, out_specs=ANY,
-    )(coords, outer, inner, s_after, stq, p_own, p_cross, p_chip, begun)
+        12 * unit, 6 << 20, aliases={8: 0}, out_specs=ANY,
+    )(coords, outer, inner, s_after, stq, rows_half, p_cross, p_chip, begun)
 
 
 def solution(mesh):

time: 128 us -> 127 us (level)
  local copies, waits for them, and re-layouts: 4.65 us -> 0.17 us
  Pallas kernels: 15.5 us -> 18.9 us
    pallas_call x4 -> x5, Pallas kernels: 8.85 us -> 12.7 us  [the longest x1 3.74 us: shards(): call(functools.partial(begin_kernel, blocks), [SMEM, VMEM, ANY, VMEM, ANY...]
    unnamed x9 -> x5, local copies, waits for them, and re-layouts: 2.81 us -> 0.1 us
    broadcast_in_dim x3 -> x2, local copies, waits for them, and re-layouts: 1.84 us -> 0.07 us  [spread(): jnp.broadcast_to(x[None], (parts,) + x.shape)]
  transfers between devices with their start and end apart: 12 -> 12, of which waited for: 7 -> 7; matrix products, arithmetic and copies ran while one was open for 0% -> 0% of each run, Pallas kernels for 5% -> 7%
where the time goes in v4:
time: 127 us
  starting transfers between devices  54.4 us (43%)
  waiting for transfers between devices  29.4 us (23%)
  blocking collectives  23.4 us (18%)
  Pallas kernels  18.9 us (15%)
    ppermute x5, starting transfers between devices, exchange(): from_cross = lax.ppermute(to_cross, 'tiles', cross)  29.9 us
    ppermute x5, waiting for transfers between devices, exchange(): from_cross = lax.ppermute(to_cross, 'tiles', cross)  24.8 us
    all_to_all x2, blocking collectives, spread(): lax.all_to_all(jnp.broadcast_to(x[None], (parts,) + x.shape), 'samp', 0, 0)  23.4 us
    ppermute x5, starting transfers between devices, exchange(): from_chip = lax.ppermute(to_chip, 'tiles', chip)  9.57 us
    all_to_all x1, starting transfers between devices, shards(): s_own = lax.all_to_all(copies, 'samp', 0, 0).reshape(count, wide)  9.33 us
    all_to_all x1, starting transfers between devices, shards(): turned_parts = lax.all_to_all(pieces, 'samp', 0, 0)  5.66 us
    all_to_all x1, waiting for transfers between devices, shards(): s_own = lax.all_to_all(copies, 'samp', 0, 0).reshape(count, wide)  4 us
    pallas_call x1, Pallas kernels, shards(): call(functools.partial(begin_kernel, blocks), [SMEM, VMEM, ANY, VMEM, ANY...  3.74 us
  transfers between devices with their start and end apart: 12, of which 7 were waited for; matrix products, arithmetic and copies ran while one was open for 0% of the time, Pallas kernels for 7%

profile of v4, /device:TPU:2, one launch (start us, length us, event | category | flops | bytes accessed | tf_op | source)
XLA Modules:
  0.0 126.6 jit_solution(16249796353247398140)
XLA Ops:
  1.7 9.3 %all-to-all-start.1 = ((bf16[4,64,1024]{2,1,0:T(8,128)(2,1)}), bf16[4,64,1024]{2,1,0:T(8,128)(2,1)S(1)}, u32[]{:S(2)}, u32[]{:S(2)}) async-start(bf16[4,64,1024]{2,1,0:T(8,128)(2,1)} %shard_map.38), calls=%async_computation.1 | async-start | bytes 1048576 | tf_op jit(solution)/shard_map/all_to_all | solution.py:412
  11.1 2.6 %shard_map.37 = bf16[4,8,128,128]{3,2,1,0:T(8,128)(2,1)} custom-call(f32[10,128,512]{2,1,0:T(8,128)} %omega.9), custom_call_target="tpu_custom_call" | custom-call | bytes 4194304 | tf_op jit(solution)/shard_map/pallas_call | solution.py:413
  13.7 4.0 %all-to-all-done.1 = bf16[4,64,1024]{2,1,0:T(8,128)(2,1)S(1)} async-done(((bf16[4,64,1024]{2,1,0:T(8,128)(2,1)}), bf16[4,64,1024]{2,1,0:T(8,128)(2,1)S(1)}, u32[]{:S(2)}, u32[]{:S(2)}) %all-to-all-start.1) | async-done | bytes 524320 | tf_op jit(solution)/shard_map/all_to_all | solution.py:412
  17.7 5.7 %all-to-all-start = ((bf16[4,8,128,128]{3,2,1,0:T(8,128)(2,1)}), bf16[4,8,128,128]{3,2,1,0:T(8,128)(2,1)}, u32[]{:S(2)}, u32[]{:S(2)}) async-start(bf16[4,8,128,128]{3,2,1,0:T(8,128)(2,1)} %shard_map.37), calls=%async_computation | async-start | bytes 2097152 | tf_op jit(solution)/shard_map/all_to_all | solution.py:421
  23.4 1.9 %collective-permute-start.1 = (bf16[256,1024]{1,0:T(8,128)(2,1)S(1)}, bf16[256,1024]{1,0:T(8,128)(2,1)}, u32[]{:S(2)}, u32[]{:S(2)}) collective-permute-start(bf16[256,1024]{1,0:T(8,128)(2,1)S(1)} %bitcast.1), channel_id=1, source_target_pairs={{0,4},{4,0},{8,12},{12,8},{16,20},{20,16},{24,28},{28,24},{32,36},... | collective-permute-start | bytes 1572872 | tf_op jit(solution)/shard_map/ppermute | solution.py:400
  25.3 10.9 %collective-permute-start = (bf16[256,1024]{1,0:T(8,128)(2,1)S(1)}, bf16[256,1024]{1,0:T(8,128)(2,1)}, u32[]{:S(2)}, u32[]{:S(2)}) collective-permute-start(bf16[256,1024]{1,0:T(8,128)(2,1)S(1)} %bitcast.2), channel_id=1, source_target_pairs={{0,508},{4,8},{8,4},{12,16},{16,12},{20,24},{24,20},{28,32},{32,28... | collective-permute-start | bytes 1572872 | tf_op jit(solution)/shard_map/ppermute | solution.py:401
  36.3 6.8 %collective-permute-done.s_cross = bf16[256,1024]{1,0:T(8,128)(2,1)} collective-permute-done((bf16[256,1024]{1,0:T(8,128)(2,1)S(1)}, bf16[256,1024]{1,0:T(8,128)(2,1)}, u32[]{:S(2)}, u32[]{:S(2)}) %collective-permute-start) | collective-permute-done | bytes 524320 | tf_op jit(solution)/shard_map/ppermute | solution.py:401
  43.1 3.7 %shard_map.39 = (bf16[256,1024]{1,0:T(8,128)(2,1)S(1)}, bf16[256,1024]{1,0:T(8,128)(2,1)S(1)}, bf16[9,128,512]{2,1,0:T(8,128)(2,1)S(1)}, bf16[256,256]{1,0:T(8,1...) custom-call(s32[10,2]{1,0:T(8,128)S(1)} %copy.10.coords, f32[10,128,512]{2,1,0:T(8,128)S(1)} %copy-done, ...), custom_call_target="tpu_custom_call" | custom-call | flops 671088640 | bytes 6291456 | tf_op jit(solution)/shard_map/pallas_call | solution.py:428
  46.9 7.0 %collective-permute-start.2 = (bf16[256,256]{1,0:T(8,128)(2,1)S(1)}, bf16[256,256]{1,0:T(8,128)(2,1)S(1)}, u32[]{:S(2)}, u32[]{:S(2)}) collective-permute-start(bf16[256,256]{1,0:T(8,128)(2,1)S(1)} %get-tuple-element.27), channel_id=1, source_target_pairs={{0,508},{4,8},{8,4},{12,16},{16,12},{20,24},{24,20},{28,32},{32,28... | collective-permute-start | bytes 393224 | tf_op jit(solution)/shard_map/ppermute | solution.py:401
  53.9 1.9 %collective-permute-start.3 = (bf16[256,256]{1,0:T(8,128)(2,1)S(1)}, bf16[256,256]{1,0:T(8,128)(2,1)S(1)}, u32[]{:S(2)}, u32[]{:S(2)}) collective-permute-start(bf16[256,256]{1,0:T(8,128)(2,1)S(1)} %get-tuple-element.28), channel_id=1, source_target_pairs={{0,4},{4,0},{8,12},{12,8},{16,20},{20,16},{24,28},{28,24},{32,36},... | collective-permute-start | bytes 393224 | tf_op jit(solution)/shard_map/ppermute | solution.py:400
  57.2 12.9 %all_to_all.20.p_own = bf16[4,256,256]{2,1,0:T(8,128)(2,1)S(1)} all-to-all(bf16[4,256,256]{2,1,0:T(8,128)(2,1)S(1)} %broadcast_in_dim.4), channel_id=1, replica_groups=mesh['tiles'=128,'samp'=4] {'samp'}, dimensions={0} | all-to-all | bytes 1048576 | tf_op jit(solution)/shard_map/all_to_all | solution.py:405
  72.0 3.2 %collective-permute-start.4 = (bf16[4,256,256]{2,1,0:T(8,128)(2,1)S(1)}, bf16[4,256,256]{2,1,0:T(8,128)(2,1)S(1)}, u32[]{:S(2)}, u32[]{:S(2)}) collective-permute-start(bf16[4,256,256]{2,1,0:T(8,128)(2,1)S(1)} %all_to_all.20.p_own), channel_id=1, source_target_pairs={{0,508},{4,8},{8,4},{12,16},{16,12},{20,24},{24,20},{28,32},{32,28... | collective-permute-start | bytes 1572872 | tf_op jit(solution)/shard_map/ppermute | solution.py:401
  75.3 2.4 %shard_map.40 = (f32[3,128,512]{2,1,0:T(8,128)S(1)}, f32[256,256]{1,0:T(8,128)S(1)}, bf16[1024,256]{1,0:T(8,128)(2,1)}, bf16[3,256,256]{2,1,0:T(8,128)(2,1)S(1)}...) custom-call(s32[10,2]{1,0:T(8,128)S(1)} %copy.10.coords, f32[10,128,512]{2,1,0:T(8,128)S(1)} %copy-done, ...), custom_call_target="tpu_custom_call" | custom-call | flops 671088640 | bytes 6291456 | tf_op jit(solution)/shard_map/pallas_call | solution.py:454
  77.6 8.2 %collective-permute-done.4.p_cross = bf16[4,256,256]{2,1,0:T(8,128)(2,1)S(1)} collective-permute-done((bf16[4,256,256]{2,1,0:T(8,128)(2,1)S(1)}, bf16[4,256,256]{2,1,0:T(8,128)(2,1)S(1)}, u32[]{:S(2)}, u32[]{:S(2)}) %collective-permute-start.4) | collective-permute-done | bytes 524320 | tf_op jit(solution)/shard_map/ppermute | solution.py:401
  85.9 2.3 %shard_map.41 = (f32[4,128,512]{2,1,0:T(8,128)S(1)}, bf16[256,256]{1,0:T(8,128)(2,1)S(1)}, bf16[256,256]{1,0:T(8,128)(2,1)S(1)}) custom-call(s32[10,2]{1,0:T(8,128)S(1)} %copy.10.coords, f32[10,128,512]{2,1,0:T(8,128)S(1)} %copy-done, bf16[9,128,512]{2,1,0:T(8,128)(2,1)S(1)} %get-tuple-element.23.turned, bf16[256,1024]{1,0:T(8,128)(2,1)S(1)} %get-tuple-element.24.s_before, ...), custom_call_target="tpu_custom_call" | custom-call | flops 1073741824 | bytes 6291456 | tf_op jit(solution)/shard_map/pallas_call | solution.py:462
  88.2 3.2 %collective-permute-start.6 = (bf16[256,256]{1,0:T(8,128)(2,1)S(1)}, bf16[256,256]{1,0:T(8,128)(2,1)S(1)}, u32[]{:S(2)}, u32[]{:S(2)}) collective-permute-start(bf16[256,256]{1,0:T(8,128)(2,1)S(1)} %get-tuple-element.37), channel_id=1, source_target_pairs={{0,508},{4,8},{8,4},{12,16},{16,12},{20,24},{24,20},{28,32},{32,28... | collective-permute-start | bytes 393224 | tf_op jit(solution)/shard_map/ppermute | solution.py:401
  91.4 1.9 %collective-permute-start.7 = (bf16[256,256]{1,0:T(8,128)(2,1)S(1)}, bf16[256,256]{1,0:T(8,128)(2,1)S(1)}, u32[]{:S(2)}, u32[]{:S(2)}) collective-permute-start(bf16[256,256]{1,0:T(8,128)(2,1)S(1)} %get-tuple-element.38), channel_id=1, source_target_pairs={{0,4},{4,0},{8,12},{12,8},{16,20},{20,16},{24,28},{28,24},{32,36},... | collective-permute-start | bytes 393224 | tf_op jit(solution)/shard_map/ppermute | solution.py:400
  94.7 3.1 %collective-permute-done.6 = bf16[256,256]{1,0:T(8,128)(2,1)S(1)} collective-permute-done((bf16[256,256]{1,0:T(8,128)(2,1)S(1)}, bf16[256,256]{1,0:T(8,128)(2,1)S(1)}, u32[]{:S(2)}, u32[]{:S(2)}) %collective-permute-start.6) | collective-permute-done | bytes 131104 | tf_op jit(solution)/shard_map/ppermute | solution.py:401
  97.9 10.5 %all_to_all.21.p_own = bf16[4,256,256]{2,1,0:T(8,128)(2,1)S(1)} all-to-all(bf16[4,256,256]{2,1,0:T(8,128)(2,1)S(1)} %broadcast_in_dim.5), channel_id=1, replica_groups=mesh['tiles'=128,'samp'=4] {'samp'}, dimensions={0} | all-to-all | bytes 1048576 | tf_op jit(solution)/shard_map/all_to_all | solution.py:405
  108.3 1.9 %collective-permute-start.9 = (bf16[4,256,256]{2,1,0:T(8,128)(2,1)S(1)}, bf16[4,256,256]{2,1,0:T(8,128)(2,1)S(1)}, u32[]{:S(2)}, u32[]{:S(2)}) collective-permute-start(bf16[4,256,256]{2,1,0:T(8,128)(2,1)S(1)} %all_to_all.21.p_own), channel_id=1, source_target_pairs={{0,4},{4,0},{8,12},{12,8},{16,20},{20,16},{24,28},{28,24},{32,36},... | collective-permute-start | bytes 1572872 | tf_op jit(solution)/shard_map/ppermute | solution.py:400
  110.3 5.6 %collective-permute-start.8 = (bf16[4,256,256]{2,1,0:T(8,128)(2,1)S(1)}, bf16[4,256,256]{2,1,0:T(8,128)(2,1)S(1)}, u32[]{:S(2)}, u32[]{:S(2)}) collective-permute-start(bf16[4,256,256]{2,1,0:T(8,128)(2,1)S(1)} %all_to_all.21.p_own), channel_id=1, source_target_pairs={{0,508},{4,8},{8,4},{12,16},{16,12},{20,24},{24,20},{28,32},{32,28... | collective-permute-start | bytes 1572872 | tf_op jit(solution)/shard_map/ppermute | solution.py:401
  115.8 2.3 %shard_map.43 = (f32[10,128,512]{2,1,0:T(8,128)}, f32[256,1024]{1,0:T(8,128)S(1)}) custom-call(s32[10,2]{1,0:T(8,128)S(1)} %copy.10.coords, f32[3,128,512]{2,1,0:T(8,128)S(1)} %get-tuple-element.35.held, bf16[256,1024]{1,0:T(8,128)(2,1)S(1)} %bitcast.7, bf16[256,1024]{1,0:T(8,128)(2,1)S(1)} %get-tuple-element.25.s_after, ...), custom_call_target="tpu_custom_call" | custom-call | flops 402653184 | bytes 3145728 | tf_op jit(solution)/shard_map/pallas_call | solution.py:475
  118.1 6.0 %collective-permute-done.8.p_cross = bf16[4,256,256]{2,1,0:T(8,128)(2,1)S(1)} collective-permute-done((bf16[4,256,256]{2,1,0:T(8,128)(2,1)S(1)}, bf16[4,256,256]{2,1,0:T(8,128)(2,1)S(1)}, u32[]{:S(2)}, u32[]{:S(2)}) %collective-permute-start.8) | collective-permute-done | bytes 524320 | tf_op jit(solution)/shard_map/ppermute | solution.py:401
  124.1 2.5 %shard_map.44 = f32[10,128,512]{2,1,0:T(8,128)} custom-call(s32[10,2]{1,0:T(8,128)S(1)} %copy.10.coords, f32[4,128,512]{2,1,0:T(8,128)S(1)} %get-tuple-element.31.outer, f32[4,128,512]{2,1,0:T(8,128)S(1)} %get-tuple-element.34.inner, bf16[256,1024]{1,0:T(8,128)(2,1)S(1)} %get-tuple-element.25.s_after, ...), custom_call_target="tpu_custom_call", output_to_operand_aliasing={{}: (8, {})} | custom-call | flops 402653184 | bytes 6291456 | tf_op jit(solution)/shard_map/pallas_call | solution.py:480
  (19 shorter events, 6.6 us)
Async XLA Ops:
  1.7 16.0 %all-to-all-start.1 = ((bf16[4,64,1024]{2,1,0:T(8,128)(2,1)}), bf16[4,64,1024]{2,1,0:T(8,128)(2,1)S(1)}, u32[]{:S(2)}, u32[]{:S(2)}) async-start(bf16[4,64,1024]{2,1,0:T(8,128)(2,1)} %shard_map.38), calls=%async_computation.1 | async-start | bytes 1048576 | tf_op jit(solution)/shard_map/all_to_all | solution.py:412
  11.1 25.1 %copy-start.1 = (s32[10,2]{0,1:T(2,128)S(1)}, s32[10,2]{0,1:T(2,128)}, u32[]{:S(2)}) copy-start(s32[10,2]{0,1:T(2,128)} %param.5) | copy-start | bytes 244
  11.1 32.0 %copy-start = (f32[10,128,512]{2,1,0:T(8,128)S(1)}, f32[10,128,512]{2,1,0:T(8,128)}, u32[]{:S(2)}) copy-start(f32[10,128,512]{2,1,0:T(8,128)} %omega.9) | copy-start | bytes 7864324
  17.7 18.6 %all-to-all-start = ((bf16[4,8,128,128]{3,2,1,0:T(8,128)(2,1)}), bf16[4,8,128,128]{3,2,1,0:T(8,128)(2,1)}, u32[]{:S(2)}, u32[]{:S(2)}) async-start(bf16[4,8,128,128]{3,2,1,0:T(8,128)(2,1)} %shard_map.37), calls=%async_computation | async-start | bytes 2097152 | tf_op jit(solution)/shard_map/all_to_all | solution.py:421
  23.4 12.9 %collective-permute-start.1 = (bf16[256,1024]{1,0:T(8,128)(2,1)S(1)}, bf16[256,1024]{1,0:T(8,128)(2,1)}, u32[]{:S(2)}, u32[]{:S(2)}) collective-permute-start(bf16[256,1024]{1,0:T(8,128)(2,1)S(1)} %bitcast.1), channel_id=1, source_target_pairs={{0,4},{4,0},{8,12},{12,8},{16,20},{20,16},{24,28},{28,24},{32,36},... | collective-permute-start | bytes 1572872 | tf_op jit(solution)/shard_map/ppermute | solution.py:400
  25.3 17.8 %collective-permute-start = (bf16[256,1024]{1,0:T(8,128)(2,1)S(1)}, bf16[256,1024]{1,0:T(8,128)(2,1)}, u32[]{:S(2)}, u32[]{:S(2)}) collective-permute-start(bf16[256,1024]{1,0:T(8,128)(2,1)S(1)} %bitcast.2), channel_id=1, source_target_pairs={{0,508},{4,8},{8,4},{12,16},{16,12},{20,24},{24,20},{28,32},{32,28... | collective-permute-start | bytes 1572872 | tf_op jit(solution)/shard_map/ppermute | solution.py:401
  46.9 9.6 %collective-permute-start.2 = (bf16[256,256]{1,0:T(8,128)(2,1)S(1)}, bf16[256,256]{1,0:T(8,128)(2,1)S(1)}, u32[]{:S(2)}, u32[]{:S(2)}) collective-permute-start(bf16[256,256]{1,0:T(8,128)(2,1)S(1)} %get-tuple-element.27), channel_id=1, source_target_pairs={{0,508},{4,8},{8,4},{12,16},{16,12},{20,24},{24,20},{28,32},{32,28... | collective-permute-start | bytes 393224 | tf_op jit(solution)/shard_map/ppermute | solution.py:401
  53.9 3.2 %collective-permute-start.3 = (bf16[256,256]{1,0:T(8,128)(2,1)S(1)}, bf16[256,256]{1,0:T(8,128)(2,1)S(1)}, u32[]{:S(2)}, u32[]{:S(2)}) collective-permute-start(bf16[256,256]{1,0:T(8,128)(2,1)S(1)} %get-tuple-element.28), channel_id=1, source_target_pairs={{0,4},{4,0},{8,12},{12,8},{16,20},{20,16},{24,28},{28,24},{32,36},... | collective-permute-start | bytes 393224 | tf_op jit(solution)/shard_map/ppermute | solution.py:400
  70.1 7.5 %collective-permute-start.5 = (bf16[4,256,256]{2,1,0:T(8,128)(2,1)S(1)}, bf16[4,256,256]{2,1,0:T(8,128)(2,1)S(1)}, u32[]{:S(2)}, u32[]{:S(2)}) collective-permute-start(bf16[4,256,256]{2,1,0:T(8,128)(2,1)S(1)} %all_to_all.20.p_own), channel_id=1, source_target_pairs={{0,4},{4,0},{8,12},{12,8},{16,20},{20,16},{24,28},{28,24},{32,36},... | collective-permute-start | bytes 1572872 | tf_op jit(solution)/shard_map/ppermute | solution.py:400
  72.0 13.8 %collective-permute-start.4 = (bf16[4,256,256]{2,1,0:T(8,128)(2,1)S(1)}, bf16[4,256,256]{2,1,0:T(8,128)(2,1)S(1)}, u32[]{:S(2)}, u32[]{:S(2)}) collective-permute-start(bf16[4,256,256]{2,1,0:T(8,128)(2,1)S(1)} %all_to_all.20.p_own), channel_id=1, source_target_pairs={{0,508},{4,8},{8,4},{12,16},{16,12},{20,24},{24,20},{28,32},{32,28... | collective-permute-start | bytes 1572872 | tf_op jit(solution)/shard_map/ppermute | solution.py:401
  88.2 9.6 %collective-permute-start.6 = (bf16[256,256]{1,0:T(8,128)(2,1)S(1)}, bf16[256,256]{1,0:T(8,128)(2,1)S(1)}, u32[]{:S(2)}, u32[]{:S(2)}) collective-permute-start(bf16[256,256]{1,0:T(8,128)(2,1)S(1)} %get-tuple-element.37), channel_id=1, source_target_pairs={{0,508},{4,8},{8,4},{12,16},{16,12},{20,24},{24,20},{28,32},{32,28... | collective-permute-start | bytes 393224 | tf_op jit(solution)/shard_map/ppermute | solution.py:401
  91.4 6.4 %collective-permute-start.7 = (bf16[256,256]{1,0:T(8,128)(2,1)S(1)}, bf16[256,256]{1,0:T(8,128)(2,1)S(1)}, u32[]{:S(2)}, u32[]{:S(2)}) collective-permute-start(bf16[256,256]{1,0:T(8,128)(2,1)S(1)} %get-tuple-element.38), channel_id=1, source_target_pairs={{0,4},{4,0},{8,12},{12,8},{16,20},{20,16},{24,28},{28,24},{32,36},... | collective-permute-start | bytes 393224 | tf_op jit(solution)/shard_map/ppermute | solution.py:400
  108.3 9.8 %collective-permute-start.9 = (bf16[4,256,256]{2,1,0:T(8,128)(2,1)S(1)}, bf16[4,256,256]{2,1,0:T(8,128)(2,1)S(1)}, u32[]{:S(2)}, u32[]{:S(2)}) collective-permute-start(bf16[4,256,256]{2,1,0:T(8,128)(2,1)S(1)} %all_to_all.21.p_own), channel_id=1, source_target_pairs={{0,4},{4,0},{8,12},{12,8},{16,20},{20,16},{24,28},{28,24},{32,36},... | collective-permute-start | bytes 1572872 | tf_op jit(solution)/shard_map/ppermute | solution.py:400
  110.3 13.8 %collective-permute-start.8 = (bf16[4,256,256]{2,1,0:T(8,128)(2,1)S(1)}, bf16[4,256,256]{2,1,0:T(8,128)(2,1)S(1)}, u32[]{:S(2)}, u32[]{:S(2)}) collective-permute-start(bf16[4,256,256]{2,1,0:T(8,128)(2,1)S(1)} %all_to_all.21.p_own), channel_id=1, source_target_pairs={{0,508},{4,8},{8,4},{12,16},{16,12},{20,24},{24,20},{28,32},{32,28... | collective-permute-start | bytes 1572872 | tf_op jit(solution)/shard_map/ppermute | solution.py:401

commit v5 on v4

v5 whole, which is shorter than its diff:
```python
import functools

import jax
import jax.numpy as jnp
from jax import lax
from jax.experimental import pallas as pl
from jax.experimental.pallas import tpu as pltpu
from jax.sharding import PartitionSpec as P


BLK_DEV = 2
step_size = 0.25
penalty = 0.2

VMEM = pl.BlockSpec(memory_space=pltpu.VMEM)
SMEM = pl.BlockSpec(memory_space=pltpu.SMEM)
ANY = pl.BlockSpec(memory_space=pl.ANY)
HBM = pl.BlockSpec(memory_space=pltpu.HBM)
bf16, f32 = jnp.bfloat16, jnp.float32

OWN_PAIR = 8
LIMIT = 12 << 20


def dot_nn(a, b):
    return jnp.dot(a, b, preferred_element_type=f32)


def dot_nt(a, b):
    return lax.dot_general(a, b, (((1,), (1,)), ((), ())), preferred_element_type=f32)


def shrink(value):
    level = step_size * penalty
    return value - jnp.clip(value, -level, level)


def shrink_diagonal(value, quarter):
    rows, width = value.shape
    row_ids = quarter * rows + lax.broadcasted_iota(jnp.int32, (rows, width), 0)
    col_ids = lax.broadcasted_iota(jnp.int32, (rows, width), 1)
    positive = 0.5 * (value + jnp.sqrt(value * value + 4.0 * step_size))
    return jnp.where(row_ids == col_ids, positive, shrink(value))


def find_slots(blocks, coords, slot_of):
    first = (lax.axis_index("tiles") - 1) * BLK_DEV
    for pair in range(OWN_PAIR + 1):
        slot_of[pair] = 0

    def place(slot, side):
        at = coords[slot, side] - first
        at = jnp.where(at < 0, at + blocks, at)
        return jnp.where(at >= blocks, at - blocks, at)

    for slot in range(BLK_DEV, coords.shape[0]):
        row, col = place(slot, 0), place(slot, 1)
        pair = jnp.where(col >= 2 * BLK_DEV, (col - 2 * BLK_DEV) * 2 * BLK_DEV + row, OWN_PAIR)
        slot_of[pair] = slot


def is_even():
    return lax.rem(lax.axis_index("tiles"), 2) == 0


def repeat_kernel(x, out, held, in_sem, out_sems):
    load = pltpu.make_async_copy(x, held, in_sem)
    load.start()
    load.wait()
    stores = [pltpu.make_async_copy(held, out.at[part], out_sems.at[part]) for part in range(out.shape[0])]
    for store in stores:
        store.start()
    for store in stores:
        store.wait()


def cut_kernel(omega, out, held, pieces, in_sems, out_sems):
    rows = omega.shape[1]
    others = held.shape[0]
    loads = [
        pltpu.make_async_copy(omega.at[BLK_DEV + k], held.at[k], in_sems.at[k]) for k in range(others)
    ]
    for load in loads:
        load.start()
    stores = []
    for k in range(others):
        loads[k].wait()
        for part in range(out.shape[0]):
            pieces[part, k] = held[k, :, part * rows : (part + 1) * rows].astype(bf16).T
        stores.append(pltpu.make_async_copy(pieces.at[:, k], out.at[:, k], out_sems.at[k]))
        stores[-1].start()
    for store in stores:
        store.wait()


def choose(even_is_first, first, second):
    even = is_even()

    @pl.when(even if even_is_first else jnp.logical_not(even))
    def _():
        first()

    @pl.when(jnp.logical_not(even) if even_is_first else even)
    def _():
        second()


def next_side():
    return jnp.where(is_even(), 2, 0)


def put_tile(slot, tile, mats, at):
    mats[at] = jnp.where(slot > 0, tile, 0.0).astype(bf16)


def spot(i, rows, start, width):
    return slice(i * rows, (i + 1) * rows), slice(start, start + width)


def first_rows(slot_of, omega, base, s_near, mats):
    rows, width = omega.shape[1:]
    for i in range(2):
        for blk in range(2):
            slot = slot_of[blk * 4 + base + i]
            put_tile(slot, omega[slot], mats, spot(i, rows, blk * width, width))
    return dot_nt(mats[...], s_near[...])


def first_cols(turned, s_near, s_own):
    rows, width = turned.shape[1:]
    total = jnp.zeros((2 * rows, s_own.shape[0]), f32)
    for a in range(2 * BLK_DEV):
        source = (s_near, s_own)[a // BLK_DEV]
        blk = a % BLK_DEV
        total += dot_nt(turned[2 * a : 2 * a + 2].reshape(2 * rows, width), source[:, blk * width : (blk + 1) * width])
    return total


def first_cross_kernel(blocks, coords, omega, parts, s_own, s_chip, turned, out, slot_of, mats, sems):
    rows, _ = omega.shape[1:]
    count = parts.shape[0]
    find_slots(blocks, coords, slot_of)

    def fill(pair):
        slot = slot_of[pair]
        unit = OWN_PAIR if pair == OWN_PAIR else pair % 4 * 2 + pair // 4
        copies = [
            pltpu.make_async_copy(
                parts.at[part, slot - BLK_DEV],
                turned.at[unit, :, part * rows : (part + 1) * rows],
                sems.at[pair, part],
            )
            for part in range(count)
        ]
        return slot, unit, copies

    for pair in range(OWN_PAIR + 1):
        slot, unit, copies = fill(pair)

        @pl.when(slot > 0)
        def _(copies=copies):
            for copy in copies:
                copy.start()

        @pl.when(slot == 0)
        def _(unit=unit):
            turned[unit] = jnp.zeros_like(turned[unit])

    @pl.when(is_even())
    def _():
        out[...] = first_rows(slot_of, omega, 0, s_chip, mats).astype(bf16)

    for pair in range(OWN_PAIR + 1):
        slot, unit, copies = fill(pair)

        @pl.when(slot > 0)
        def _(copies=copies):
            for copy in copies:
                copy.wait()

    @pl.when(jnp.logical_not(is_even()))
    def _():
        out[...] = first_cols(turned, s_chip, s_own).astype(bf16)


def first_chip_kernel(blocks, coords, omega, turned, s_own, s_cross, out, slot_of, mats):
    find_slots(blocks, coords, slot_of)

    def cols():
        out[...] = first_cols(turned, s_cross, s_own).astype(bf16)

    def rows():
        out[...] = first_rows(slot_of, omega, 0, s_cross, mats).astype(bf16)

    choose(True, cols, rows)


def first_own_kernel(blocks, coords, omega, turned, s_own, s_cross, s_chip, own, stq, slot_of, mats):
    rows, width = omega.shape[1:]
    quarter = lax.axis_index("samp")
    find_slots(blocks, coords, slot_of)
    mats[:rows, :width] = omega[0].astype(bf16)
    mats[rows:, width:] = omega[1].astype(bf16)
    slot = slot_of[OWN_PAIR]
    put_tile(slot, omega[slot], mats, spot(0, rows, width, width))
    mats[rows:, :width] = turned[OWN_PAIR]
    own[...] = dot_nt(mats[...], s_own[...])

    def add(s_next):
        own[...] += first_rows(slot_of, omega, BLK_DEV, s_next, mats)

    choose(True, lambda: add(s_chip), lambda: add(s_cross))
    for side, ref in enumerate((s_cross, s_own, s_chip)):
        for blk in range(BLK_DEV):
            at = pl.multiple_of(blk * width + quarter * rows, rows)
            stq[side, blk * rows : (blk + 1) * rows, :] = ref[:, pl.ds(at, rows)].T


def half_kernel(stq, p_own, out):
    count, both = p_own.shape[0], p_own.shape[1]
    rows = both // BLK_DEV
    far = stq[next_side()]
    for part in range(count):
        piece = dot_nt(far, p_own[part])
        for blk in range(BLK_DEV):
            at = (blk * count + part) * rows
            out[:, at : at + rows] = piece[:, blk * rows : (blk + 1) * rows]


def update_edge(old, slots, ptq, far, s_near, p_near, scale, grad, put):
    count, both = p_near.shape[0], p_near.shape[1]
    rows = both // BLK_DEV
    grad[...] = dot_nn(ptq, s_near[...])
    for part in range(count):
        piece = dot_nt(far, p_near[part])
        for i in range(2):
            for blk in range(2):
                at = spot(i, rows, (blk * count + part) * rows, rows)
                here = grad[at] + piece[i * rows : (i + 1) * rows, blk * rows : (blk + 1) * rows]
                slot = slots(i, blk)
                put(i, blk, part, slot, shrink(old(i, blk, part, slot) - scale * here))


def edge_kernel(
    blocks, far_side, coords, omega, turned, s_own, s_near, p_near, p_far, stq, own_half,
    tiles, out, slot_of, grad, mats,
):
    rows, width = omega.shape[1:]
    wide = s_own.shape[1]
    quarter = lax.axis_index("samp")
    scale = step_size / (2.0 * s_own.shape[0])
    find_slots(blocks, coords, slot_of)

    def columns(part):
        return slice(part * rows, (part + 1) * rows)

    def far_rows():
        return p_far[quarter] if far_side else p_far[...]

    def row_tiles():
        def put(i, blk, part, slot, tile):
            tiles[i * 2 + blk, :, columns(part)] = tile
            put_tile(slot, tile, mats, spot(i, rows, blk * width + part * rows, rows))

        update_edge(
            lambda i, blk, part, slot: omega[slot, :, columns(part)], lambda i, blk: slot_of[blk * 4 + i],
            far_rows(), stq[far_side], s_near, p_near, scale, grad, put,
        )
        out[...] = dot_nt(mats[:, :wide], s_near[...]).astype(bf16)

    def col_tiles():
        def put(i, blk, part, slot, tile):
            put_tile(slot, tile, mats, spot(i, rows, blk * width + part * rows, rows))

        update_edge(
            lambda i, blk, part, slot: turned[2 * blk + i, :, columns(part)].astype(f32),
            lambda i, blk: slot_of[i * 4 + blk],
            far_rows(), stq[far_side], s_near, p_near, scale, grad, put,
        )
        grad[...] = dot_nn(far_rows(), s_own[...]) + own_half[...]
        for i in range(2):
            for blk in range(2):
                tile = turned[2 * (BLK_DEV + blk) + i].astype(f32) - scale * grad[spot(i, rows, blk * width, width)]
                put_tile(slot_of[i * 4 + BLK_DEV + blk], shrink(tile), mats, spot(i, rows, wide + blk * width, width))
        total = dot_nt(mats[:, :wide], s_near[...]) + dot_nt(mats[:, wide:], s_own[...])
        out[...] = total.astype(bf16)

    choose(far_side == 0, row_tiles, col_tiles)


def natural(out, pieces):
    count, both = pieces.shape[0], pieces.shape[1]
    rows = both // BLK_DEV
    for blk in range(BLK_DEV):
        for part in range(count):
            at = (blk * count + part) * rows
            out[at : at + rows, :] = pieces[part, blk * rows : (blk + 1) * rows, :]


def own_kernel(blocks, coords, omega, turned, s_own, stq, p_own, tiles, t_own, slot_of, grad, mats, nat_own):
    rows, width = grad.shape[0] // 2, grad.shape[1] // 2
    quarter = lax.axis_index("samp")
    scale = step_size / (2.0 * s_own.shape[0])
    find_slots(blocks, coords, slot_of)
    natural(nat_own, p_own)
    grad[...] = dot_nn(p_own[quarter], s_own[...]) + dot_nt(stq[1], nat_own[...])
    slot = slot_of[OWN_PAIR]
    for i in range(BLK_DEV):
        here = grad[spot(i, rows, i * width, width)]
        tiles[i] = shrink_diagonal(omega[i] - scale * here, quarter)
        mats[spot(i, rows, i * width, width)] = tiles[i].astype(bf16)
    tiles[2] = shrink(omega[slot] - scale * grad[:rows, width:])
    put_tile(slot, tiles[2], mats, spot(0, rows, width, width))
    there = turned[OWN_PAIR].astype(f32) - scale * grad[rows:, :width]
    put_tile(slot, shrink(there), mats, spot(1, rows, 0, width))
    t_own[...] = dot_nt(mats[...], s_own[...])


def inner_kernel(
    blocks, coords, omega, s_cross, s_chip, stq, p_own, p_cross, p_chip, t_own, tiles, own, slot_of, grad, mats
):
    rows, width = omega.shape[1:]
    quarter = lax.axis_index("samp")
    scale = step_size / (2.0 * s_chip.shape[0])
    find_slots(blocks, coords, slot_of)

    def put(i, blk, part, slot, tile):
        tiles[i * 2 + blk, :, part * rows : (part + 1) * rows] = tile
        put_tile(slot, tile, mats, spot(i, rows, blk * width + part * rows, rows))

    def run(s_next, p_next):
        update_edge(
            lambda i, blk, part, slot: omega[slot, :, part * rows : (part + 1) * rows],
            lambda i, blk: slot_of[blk * 4 + BLK_DEV + i],
            p_own[quarter], stq[1], s_next, p_next, scale, grad, put,
        )
        own[...] = t_own[...] + dot_nt(mats[...], s_next[...])

    choose(True, lambda: run(s_chip, p_chip), lambda: run(s_cross, p_cross))


def own_last_kernel(
    blocks, coords, held, s_own, s_cross, s_chip, stq, p_own, out, rows_half, slot_of, grad, nat_own, tiles, sems,
):
    rows, width = grad.shape[0] // 2, grad.shape[1] // 2
    quarter = lax.axis_index("samp")
    scale = step_size / (2.0 * s_own.shape[0])
    find_slots(blocks, coords, slot_of)
    natural(nat_own, p_own)
    grad[...] = dot_nn(p_own[quarter], s_own[...]) + dot_nt(stq[1], nat_own[...])
    slot = slot_of[OWN_PAIR]
    copies = [pltpu.make_async_copy(tiles.at[i], out.at[i], sems.at[i]) for i in range(BLK_DEV)]
    copies.append(pltpu.make_async_copy(tiles.at[2], out.at[slot], sems.at[2]))
    for i in range(BLK_DEV):
        here = grad[i * rows : (i + 1) * rows, i * width : (i + 1) * width]
        tiles[i] = shrink_diagonal(held[i] - scale * here, quarter)
        copies[i].start()
    tiles[2] = shrink(held[2] - scale * grad[:rows, width:])

    @pl.when(slot > 0)
    def _():
        copies[2].start()

    def half(s_next):
        rows_half[...] = dot_nn(p_own[quarter], s_next[...])

    choose(True, lambda: half(s_chip), lambda: half(s_cross))
    for i in range(BLK_DEV):
        copies[i].wait()

    @pl.when(slot > 0)
    def _():
        copies[2].wait()


def last_kernel(
    blocks, coords, outer_cross, outer_chip, inner, s_cross, s_chip, stq, rows_half, p_cross, p_chip, begun,
    out, slot_of, grad, tiles, sems,
):
    rows, _ = tiles.shape[1:]
    quarter = lax.axis_index("samp")
    count = p_chip.shape[0]
    scale = step_size / (2.0 * s_chip.shape[0])
    find_slots(blocks, coords, slot_of)

    def copy(unit, slot):
        return pltpu.make_async_copy(tiles.at[unit], out.at[slot], sems.at[unit])

    def slot_at(group, i, blk):
        return slot_of[blk * 4 + group * BLK_DEV + i]

    def run(outer, s_next, p_next, p_far, far):
        grad[...] = dot_nn(p_far[quarter], s_next[...])
        for group in (1, 0):
            rest = (grad, rows_half)[group]
            for part in range(count):
                piece = dot_nt((far, stq[1])[group], p_next[part])
                for i in range(2):
                    for blk in range(2):
                        at = spot(i, rows, (blk * count + part) * rows, rows)
                        here = rest[at] + piece[i * rows : (i + 1) * rows, blk * rows : (blk + 1) * rows]
                        cols = slice(part * rows, (part + 1) * rows)
                        old = (outer, inner)[group][i * 2 + blk, :, cols]
                        tiles[group * 4 + i * 2 + blk, :, cols] = shrink(old - scale * here)
            for i in range(2):
                for blk in range(2):
                    unit, slot = group * 4 + i * 2 + blk, slot_at(group, i, blk)

                    @pl.when(slot > 0)
                    def _(unit=unit, slot=slot):
                        copy(unit, slot).start()

    choose(
        True,
        lambda: run(outer_cross, s_chip, p_chip, p_cross, stq[0]),
        lambda: run(outer_chip, s_cross, p_cross, p_chip, stq[2]),
    )
    for group in range(2):
        for i in range(2):
            for blk in range(2):
                unit, slot = group * 4 + i * 2 + blk, slot_at(group, i, blk)

                @pl.when(slot > 0)
                def _(unit=unit, slot=slot):
                    copy(unit, slot).wait()


def shards(samples, omega, coords):
    size = lax.axis_size("tiles")
    parts = lax.axis_size("samp")
    blocks = BLK_DEV * size
    tiles, rows, width = omega.shape
    others = tiles - BLK_DEV
    count = samples.shape[0] * parts
    wide = samples.shape[1]
    both = BLK_DEV * rows
    chip = [(i, i ^ 1) for i in range(size)]
    cross = [(i, (i - 1) % size if i % 2 == 0 else (i + 1) % size) for i in range(size)]
    shape = jax.ShapeDtypeStruct
    slots = pltpu.SMEM((OWN_PAIR + 1,), jnp.int32)
    params = pltpu.CompilerParams(vmem_limit_bytes=LIMIT)

    def call(body, in_specs, outs, scratch, macs, moved, aliases=None, out_specs=None):
        several = isinstance(outs, tuple)
        specs = out_specs or ((VMEM,) * len(outs) if several else VMEM)
        return pl.pallas_call(
            body, out_shape=outs, in_specs=in_specs, out_specs=specs, scratch_shapes=scratch,
            compiler_params=params, input_output_aliases=aliases or {},
            cost_estimate=pl.CostEstimate(flops=2 * macs, bytes_accessed=moved, transcendentals=0),
        )

    def permute(x, pairs):
        return lax.ppermute(x, "tiles", pairs)

    def spread(x):
        return lax.all_to_all(jnp.broadcast_to(x[None], (parts,) + x.shape), "samp", 0, 0)

    copies = call(
        repeat_kernel, [HBM], pltpu.HBM((parts,) + samples.shape, bf16),
        [pltpu.VMEM(samples.shape, bf16), pltpu.SemaphoreType.DMA, pltpu.SemaphoreType.DMA((parts,))],
        0, 1 << 20, out_specs=HBM,
    )(pltpu.with_memory_space_constraint(samples, pltpu.HBM))
    s_own = lax.all_to_all(copies, "samp", 0, 0).reshape(count, wide)
    pieces = call(
        cut_kernel, [HBM], pltpu.HBM((parts, others, rows, rows), bf16),
        [
            pltpu.VMEM((others, rows, width), f32), pltpu.VMEM((parts, others, rows, rows), bf16),
            pltpu.SemaphoreType.DMA((others,)), pltpu.SemaphoreType.DMA((others,)),
        ],
        0, 4 << 20, out_specs=HBM,
    )(pltpu.with_memory_space_constraint(omega, pltpu.HBM))
    turned_parts = lax.all_to_all(pieces, "samp", 0, 0)
    s_cross = permute(s_own, cross)
    s_chip = permute(s_own, chip)

    part = shape((both, count), bf16)
    full = shape((both, count), f32)
    four = shape((4, rows, width), f32)
    wide_half = shape((both, wide), f32)
    unit = rows * width * count
    grad = pltpu.VMEM((both, wide), f32)
    mats = pltpu.VMEM((both, wide), bf16)
    mats_two = pltpu.VMEM((both, 2 * wide), bf16)
    nat = pltpu.VMEM((wide, count), bf16)

    def run(body, args, in_specs, outs, scratch, units, out_specs=None, aliases=None):
        return call(body, in_specs, outs, scratch, units * unit, 4 << 20, aliases, out_specs)(*args)

    def kernel(body, *extra):
        return functools.partial(body, blocks, *extra)

    turned, to_cross = run(
        kernel(first_cross_kernel), (coords, omega, turned_parts, s_own, s_chip), [SMEM, VMEM, ANY, VMEM, VMEM],
        (shape((OWN_PAIR + 1, rows, width), bf16), part),
        [slots, mats, pltpu.SemaphoreType.DMA((OWN_PAIR + 1, parts))], 8,
    )
    from_cross = permute(to_cross, cross)
    to_chip = run(
        kernel(first_chip_kernel), (coords, omega, turned, s_own, s_cross), [SMEM] + [VMEM] * 4,
        part, [slots, mats], 8,
    )
    from_chip = permute(to_chip, chip)
    own, stq = run(
        kernel(first_own_kernel), (coords, omega, turned, s_own, s_cross, s_chip), [SMEM] + [VMEM] * 5,
        (full, shape((3, both, count), bf16)), [slots, mats], 8,
    )
    total = (own + from_cross.astype(f32) + from_chip.astype(f32)).astype(bf16)
    far_cross = permute(total, cross)
    p_own = spread(total)
    p_cross = permute(p_own, cross)
    p_chip = permute(p_own, chip)
    own_half = run(half_kernel, (stq, p_own), [VMEM] * 2, wide_half, [], 4)

    def edge(side, s_near, p_near, p_far):
        return run(
            kernel(edge_kernel, side), (coords, omega, turned, s_own, s_near, p_near, p_far, stq, own_half),
            [SMEM] + [VMEM] * 8, (four, part), [slots, grad, mats_two], 20,
        )

    outer_cross, to_cross = edge(0, s_chip, p_chip, far_cross)
    from_cross = permute(to_cross, cross)
    mine, t_own = run(
        kernel(own_kernel), (coords, omega, turned, s_own, stq, p_own), [SMEM] + [VMEM] * 5,
        (shape((3, rows, width), f32), full), [slots, grad, mats, nat], 12,
    )
    outer_chip, to_chip = edge(2, s_cross, p_cross, p_chip)
    from_chip = permute(to_chip, chip)
    inner, own = run(
        kernel(inner_kernel), (coords, omega, s_cross, s_chip, stq, p_own, p_cross, p_chip, t_own),
        [SMEM] + [VMEM] * 8, (four, full), [slots, grad, mats], 12,
    )
    total = (own + from_cross.astype(f32) + from_chip.astype(f32)).astype(bf16)
    p_own = spread(total)
    p_cross = permute(p_own, cross)
    p_chip = permute(p_own, chip)
    whole = shape(omega.shape, f32)
    begun, rows_half = run(
        kernel(own_last_kernel), (coords, mine, s_own, s_cross, s_chip, stq, p_own), [SMEM] + [VMEM] * 6,
        (whole, wide_half),
        [slots, grad, nat, pltpu.VMEM((3, rows, width), f32), pltpu.SemaphoreType.DMA((3,))],
        12, out_specs=(ANY, VMEM),
    )
    return run(
        kernel(last_kernel),
        (coords, outer_cross, outer_chip, inner, s_cross, s_chip, stq, rows_half, p_cross, p_chip, begun),
        [SMEM] + [VMEM] * 9 + [ANY], whole,
        [slots, grad, pltpu.VMEM((8, rows, width), f32), pltpu.SemaphoreType.DMA((8,))],
        12, out_specs=ANY, aliases={10: 0},
    )


def solution(mesh):
    in_specs = (P("samp", "tiles"), P("tiles", "samp", None), P("tiles", None))
    out_specs = P("tiles", "samp", None)

    return jax.shard_map(shards, mesh=mesh, in_specs=in_specs, out_specs=out_specs, check_vma=False)
```

time: 127 us -> 128 us (level)
  waiting for transfers between devices: 29.4 us -> 18 us
  starting transfers between devices: 54.4 us -> 61.8 us
  Pallas kernels: 18.9 us -> 25.4 us
  blocking collectives: 23.4 us -> 21.7 us
    ppermute x10 -> x11, waiting for transfers between devices: 25.4 us -> 14 us  [permute(): return lax.ppermute(x, 'tiles', pairs)]
    ppermute x10 -> x11, starting transfers between devices: 39.4 us -> 46.8 us  [permute(): return lax.ppermute(x, 'tiles', pairs)]
    pallas_call x6 -> x10, Pallas kernels: 14.5 us -> 21 us  [run(): call(body, in_specs, outs, scratch, units * unit, 4 << 20, aliases, out_s...]
    all_to_all x2, blocking collectives: 23.4 us -> 21.7 us  [spread(): lax.all_to_all(jnp.broadcast_to(x[None], (parts,) + x.shape), 'samp', 0, 0)]
  transfers between devices with their start and end apart: 12 -> 13, of which waited for: 7 -> 5; matrix products, arithmetic and copies ran while one was open for 0% -> 0% of each run, Pallas kernels for 7% -> 15%
where the time goes in v5:
time: 128 us; the launch traced here: 127 us
  starting transfers between devices  61.8 us (48%)
  Pallas kernels  25.4 us (20%)
  blocking collectives  21.7 us (17%)
  waiting for transfers between devices  18 us (14%)
    ppermute x11, starting transfers between devices, permute(): return lax.ppermute(x, 'tiles', pairs)  46.8 us
    all_to_all x2, blocking collectives, spread(): lax.all_to_all(jnp.broadcast_to(x[None], (parts,) + x.shape), 'samp', 0, 0)  21.7 us
    pallas_call x10, Pallas kernels, run(): call(body, in_specs, outs, scratch, units * unit, 4 << 20, aliases, out_s...  21 us
    ppermute x11, waiting for transfers between devices, permute(): return lax.ppermute(x, 'tiles', pairs)  14 us
    all_to_all x1, starting transfers between devices, shards(): s_own = lax.all_to_all(copies, 'samp', 0, 0).reshape(count, wide)  9.33 us
    all_to_all x1, starting transfers between devices, shards(): turned_parts = lax.all_to_all(pieces, 'samp', 0, 0)  5.66 us
    all_to_all x1, waiting for transfers between devices, shards(): s_own = lax.all_to_all(copies, 'samp', 0, 0).reshape(count, wide)  4 us
    pallas_call x1, Pallas kernels, shards(): call(cut_kernel, [HBM], pltpu.HBM((parts, others, rows, rows), bf16), [pl...  2.62 us
  transfers between devices with their start and end apart: 13, of which 5 were waited for; matrix products, arithmetic and copies ran while one was open for 0% of the time, Pallas kernels for 15%

profile of v5, /device:TPU:2, one launch (start us, length us, event | category | flops | bytes accessed | tf_op | source)
XLA Modules:
  0.0 127.5 jit_solution(13907055753549494189)
XLA Ops:
  1.8 9.3 %all-to-all-start.1 = ((bf16[4,64,1024]{2,1,0:T(8,128)(2,1)}), bf16[4,64,1024]{2,1,0:T(8,128)(2,1)S(1)}, u32[]{:S(2)}, u32[]{:S(2)}) async-start(bf16[4,64,1024]{2,1,0:T(8,128)(2,1)} %shard_map.38), calls=%async_computation.1 | async-start | bytes 1048576 | tf_op jit(solution)/shard_map/all_to_all | solution.py:463
  11.1 2.6 %shard_map.37 = bf16[4,8,128,128]{3,2,1,0:T(8,128)(2,1)} custom-call(f32[10,128,512]{2,1,0:T(8,128)} %omega.15), custom_call_target="tpu_custom_call" | custom-call | bytes 4194304 | tf_op jit(solution)/shard_map/pallas_call | solution.py:464
  13.7 4.0 %all-to-all-done.1 = bf16[4,64,1024]{2,1,0:T(8,128)(2,1)S(1)} async-done(((bf16[4,64,1024]{2,1,0:T(8,128)(2,1)}), bf16[4,64,1024]{2,1,0:T(8,128)(2,1)S(1)}, u32[]{:S(2)}, u32[]{:S(2)}) %all-to-all-start.1) | async-done | bytes 524320 | tf_op jit(solution)/shard_map/all_to_all | solution.py:463
  17.7 5.7 %all-to-all-start = ((bf16[4,8,128,128]{3,2,1,0:T(8,128)(2,1)}), bf16[4,8,128,128]{3,2,1,0:T(8,128)(2,1)}, u32[]{:S(2)}, u32[]{:S(2)}) async-start(bf16[4,8,128,128]{3,2,1,0:T(8,128)(2,1)} %shard_map.37), calls=%async_computation | async-start | bytes 2097152 | tf_op jit(solution)/shard_map/all_to_all | solution.py:472
  25.3 10.9 %collective-permute-start.1 = (bf16[256,1024]{1,0:T(8,128)(2,1)S(1)}, bf16[256,1024]{1,0:T(8,128)(2,1)}, u32[]{:S(2)}, u32[]{:S(2)}) collective-permute-start(bf16[256,1024]{1,0:T(8,128)(2,1)S(1)} %bitcast.2), channel_id=1, source_target_pairs={{0,508},{4,8},{8,4},{12,16},{16,12},{20,24},{24,20},{28,32},{32,28... | collective-permute-start | bytes 1572872 | tf_op jit(solution)/shard_map/ppermute | solution.py:453
  36.3 2.6 %shard_map.39 = (bf16[9,128,512]{2,1,0:T(8,128)(2,1)S(1)}, bf16[256,256]{1,0:T(8,128)(2,1)S(1)}) custom-call(s32[10,2]{1,0:T(8,128)S(1)} %copy.13.coords, f32[10,128,512]{2,1,0:T(8,128)S(1)} %copy-done, bf16[4,8,128,128]{3,2,1,0:T(8,128)(2,1)} %all-to-all-done.parts, bf16[256,1024]{1,0:T(8,128)(2,1)S(1)} %bitcast.3, ...), custom_call_target="tpu_custom_call" | custom-call | flops 268435456 | bytes 4194304 | tf_op jit(solution)/shard_map/pallas_call | solution.py:487
  38.9 4.2 %collective-permute-done.1.s_cross.s_near = bf16[256,1024]{1,0:T(8,128)(2,1)} collective-permute-done((bf16[256,1024]{1,0:T(8,128)(2,1)S(1)}, bf16[256,1024]{1,0:T(8,128)(2,1)}, u32[]{:S(2)}, u32[]{:S(2)}) %collective-permute-start.1) | collective-permute-done | bytes 524320 | tf_op jit(solution)/shard_map/ppermute | solution.py:453
  44.7 1.9 %collective-permute-start.3 = (bf16[256,256]{1,0:T(8,128)(2,1)S(1)}, bf16[256,256]{1,0:T(8,128)(2,1)S(1)}, u32[]{:S(2)}, u32[]{:S(2)}) collective-permute-start(bf16[256,256]{1,0:T(8,128)(2,1)S(1)} %shard_map.41), channel_id=1, source_target_pairs={{0,4},{4,0},{8,12},{12,8},{16,20},{20,16},{24,28},{28,24},{32,36},... | collective-permute-start | bytes 393224 | tf_op jit(solution)/shard_map/ppermute | solution.py:453
  46.6 6.8 %collective-permute-start.2 = (bf16[256,256]{1,0:T(8,128)(2,1)S(1)}, bf16[256,256]{1,0:T(8,128)(2,1)S(1)}, u32[]{:S(2)}, u32[]{:S(2)}) collective-permute-start(bf16[256,256]{1,0:T(8,128)(2,1)S(1)} %get-tuple-element.21), channel_id=1, source_target_pairs={{0,508},{4,8},{8,4},{12,16},{16,12},{20,24},{24,20},{28,32},{32,28... | collective-permute-start | bytes 393224 | tf_op jit(solution)/shard_map/ppermute | solution.py:453
  53.5 2.1 %shard_map.40 = (f32[256,256]{1,0:T(8,128)S(1)}, bf16[3,256,256]{2,1,0:T(8,128)(2,1)S(1)}) custom-call(s32[10,2]{1,0:T(8,128)S(1)} %copy.13.coords, f32[10,128,512]{2,1,0:T(8,128)S(1)} %copy-done, bf16[9,128,512]{2,1,0:T(8,128)(2,1)S(1)} %get-tuple-element.19.turned, bf16[256,1024]{1,0:T(8,128)(2,1)S(1)} %bitcast.5, ...), custom_call_target="tpu_custom_call" | custom-call | flops 268435456 | bytes 4194304 | tf_op jit(solution)/shard_map/pallas_call | solution.py:487
  56.3 11.2 %all_to_all.20.p_own = bf16[4,256,256]{2,1,0:T(8,128)(2,1)S(1)} all-to-all(bf16[4,256,256]{2,1,0:T(8,128)(2,1)S(1)} %broadcast_in_dim.4), channel_id=1, replica_groups=mesh['tiles'=128,'samp'=4] {'samp'}, dimensions={0} | all-to-all | bytes 1048576 | tf_op jit(solution)/shard_map/all_to_all | solution.py:456
  67.6 6.1 %collective-permute-start.6 = (bf16[4,256,256]{2,1,0:T(8,128)(2,1)S(1)}, bf16[4,256,256]{2,1,0:T(8,128)(2,1)S(1)}, u32[]{:S(2)}, u32[]{:S(2)}) collective-permute-start(bf16[4,256,256]{2,1,0:T(8,128)(2,1)S(1)} %all_to_all.20.p_own), channel_id=1, source_target_pairs={{0,508},{4,8},{8,4},{12,16},{16,12},{20,24},{24,20},{28,32},{32,28... | collective-permute-start | bytes 1572872 | tf_op jit(solution)/shard_map/ppermute | solution.py:453
  73.7 1.9 %collective-permute-start.4 = (bf16[4,256,256]{2,1,0:T(8,128)(2,1)S(1)}, bf16[4,256,256]{2,1,0:T(8,128)(2,1)S(1)}, u32[]{:S(2)}, u32[]{:S(2)}) collective-permute-start(bf16[4,256,256]{2,1,0:T(8,128)(2,1)S(1)} %all_to_all.20.p_own), channel_id=1, source_target_pairs={{0,4},{4,0},{8,12},{12,8},{16,20},{20,16},{24,28},{28,24},{32,36},... | collective-permute-start | bytes 1572872 | tf_op jit(solution)/shard_map/ppermute | solution.py:453
  75.6 2.7 %collective-permute-start.5 = (bf16[256,256]{1,0:T(8,128)(2,1)S(1)}, bf16[256,256]{1,0:T(8,128)(2,1)S(1)}, u32[]{:S(2)}, u32[]{:S(2)}) collective-permute-start(bf16[256,256]{1,0:T(8,128)(2,1)S(1)} %add_convert_fusion.1), channel_id=1, source_target_pairs={{0,508},{4,8},{8,4},{12,16},{16,12},{20,24},{24,20},{28,32},{32,28... | collective-permute-start | bytes 393224 | tf_op jit(solution)/shard_map/ppermute | solution.py:453
  78.7 2.7 %collective-permute-done.6.p_near.p_cross = bf16[4,256,256]{2,1,0:T(8,128)(2,1)S(1)} collective-permute-done((bf16[4,256,256]{2,1,0:T(8,128)(2,1)S(1)}, bf16[4,256,256]{2,1,0:T(8,128)(2,1)S(1)}, u32[]{:S(2)}, u32[]{:S(2)}) %collective-permute-start.6) | collective-permute-done | bytes 524320 | tf_op jit(solution)/shard_map/ppermute | solution.py:453
  81.4 2.6 %shard_map.44 = (f32[4,128,512]{2,1,0:T(8,128)S(1)}, bf16[256,256]{1,0:T(8,128)(2,1)S(1)}) custom-call(s32[10,2]{1,0:T(8,128)S(1)} %copy.13.coords, f32[10,128,512]{2,1,0:T(8,128)S(1)} %copy-done, bf16[9,128,512]{2,1,0:T(8,128)(2,1)S(1)} %get-tuple-element.19.turned, bf16[256,1024]{1,0:T(8,128)(2,1)S(1)} %bitcast.6, ...), custom_call_target="tpu_custom_call" | custom-call | flops 671088640 | bytes 4194304 | tf_op jit(solution)/shard_map/pallas_call | solution.py:487
  85.9 2.1 %shard_map.43 = (f32[4,128,512]{2,1,0:T(8,128)S(1)}, bf16[256,256]{1,0:T(8,128)(2,1)S(1)}) custom-call(s32[10,2]{1,0:T(8,128)S(1)} %copy.13.coords, f32[10,128,512]{2,1,0:T(8,128)S(1)} %copy-done, bf16[9,128,512]{2,1,0:T(8,128)(2,1)S(1)} %get-tuple-element.19.turned, bf16[256,1024]{1,0:T(8,128)(2,1)S(1)} %bitcast.7, ...), custom_call_target="tpu_custom_call" | custom-call | flops 671088640 | bytes 4194304 | tf_op jit(solution)/shard_map/pallas_call | solution.py:487
  88.0 6.1 %collective-permute-start.7 = (bf16[256,256]{1,0:T(8,128)(2,1)S(1)}, bf16[256,256]{1,0:T(8,128)(2,1)S(1)}, u32[]{:S(2)}, u32[]{:S(2)}) collective-permute-start(bf16[256,256]{1,0:T(8,128)(2,1)S(1)} %get-tuple-element.29), channel_id=1, source_target_pairs={{0,508},{4,8},{8,4},{12,16},{16,12},{20,24},{24,20},{28,32},{32,28... | collective-permute-start | bytes 393224 | tf_op jit(solution)/shard_map/ppermute | solution.py:453
  95.8 2.2 %shard_map.46 = (f32[4,128,512]{2,1,0:T(8,128)S(1)}, f32[256,256]{1,0:T(8,128)S(1)}) custom-call(s32[10,2]{1,0:T(8,128)S(1)} %copy.13.coords, f32[10,128,512]{2,1,0:T(8,128)S(1)} %copy-done, bf16[256,1024]{1,0:T(8,128)(2,1)} %collective-permute-done.1.s_cross.s_near, bf16[256,1024]{1,0:T(8,128)(2,1)} %collective-permute-done.s_chip.s_near, ...), custom_call_target="tpu_custom_call" | custom-call | flops 402653184 | bytes 4194304 | tf_op jit(solution)/shard_map/pallas_call | solution.py:487
  98.1 10.5 %all_to_all.21.p_own = bf16[4,256,256]{2,1,0:T(8,128)(2,1)S(1)} all-to-all(bf16[4,256,256]{2,1,0:T(8,128)(2,1)S(1)} %broadcast_in_dim.5), channel_id=1, replica_groups=mesh['tiles'=128,'samp'=4] {'samp'}, dimensions={0} | all-to-all | bytes 1048576 | tf_op jit(solution)/shard_map/all_to_all | solution.py:456
  110.5 4.6 %collective-permute-start.9 = (bf16[4,256,256]{2,1,0:T(8,128)(2,1)S(1)}, bf16[4,256,256]{2,1,0:T(8,128)(2,1)S(1)}, u32[]{:S(2)}, u32[]{:S(2)}) collective-permute-start(bf16[4,256,256]{2,1,0:T(8,128)(2,1)S(1)} %all_to_all.21.p_own), channel_id=1, source_target_pairs={{0,508},{4,8},{8,4},{12,16},{16,12},{20,24},{24,20},{28,32},{32,28... | collective-permute-start | bytes 1572872 | tf_op jit(solution)/shard_map/ppermute | solution.py:453
  115.1 2.8 %shard_map.47 = (f32[10,128,512]{2,1,0:T(8,128)}, f32[256,1024]{1,0:T(8,128)S(1)}) custom-call(s32[10,2]{1,0:T(8,128)S(1)} %copy.13.coords, f32[3,128,512]{2,1,0:T(8,128)S(1)} %get-tuple-element.27.held, bf16[256,1024]{1,0:T(8,128)(2,1)S(1)} %bitcast.9, bf16[256,1024]{1,0:T(8,128)(2,1)} %collective-permute-done.1.s_cross.s_near, ...), custom_call_target="tpu_custom_call" | custom-call | flops 402653184 | bytes 4194304 | tf_op jit(solution)/shard_map/pallas_call | solution.py:487
  117.9 6.5 %collective-permute-done.9.p_cross = bf16[4,256,256]{2,1,0:T(8,128)(2,1)S(1)} collective-permute-done((bf16[4,256,256]{2,1,0:T(8,128)(2,1)S(1)}, bf16[4,256,256]{2,1,0:T(8,128)(2,1)S(1)}, u32[]{:S(2)}, u32[]{:S(2)}) %collective-permute-start.9) | collective-permute-done | bytes 524320 | tf_op jit(solution)/shard_map/ppermute | solution.py:453
  124.3 3.1 %shard_map.48 = f32[10,128,512]{2,1,0:T(8,128)} custom-call(s32[10,2]{1,0:T(8,128)S(1)} %copy.13.coords, f32[4,128,512]{2,1,0:T(8,128)S(1)} %get-tuple-element.23.outer_cross, f32[4,128,512]{2,1,0:T(8,128)S(1)} %get-tuple-element.24.outer_chip, f32[4,128,512]{2,1,0:T(8,128)S(1)} %get-tuple-element.26.inner, ...), custom_call_target="tpu_custom_call", output_to_operand_aliasing={{}: (10, {})} | custom-call | flops 402653184 | bytes 4194304 | tf_op jit(solution)/shard_map/pallas_call | solution.py:487
  (25 shorter events, 12.0 us)
Async XLA Ops:
  1.8 16.0 %all-to-all-start.1 = ((bf16[4,64,1024]{2,1,0:T(8,128)(2,1)}), bf16[4,64,1024]{2,1,0:T(8,128)(2,1)S(1)}, u32[]{:S(2)}, u32[]{:S(2)}) async-start(bf16[4,64,1024]{2,1,0:T(8,128)(2,1)} %shard_map.38), calls=%async_computation.1 | async-start | bytes 1048576 | tf_op jit(solution)/shard_map/all_to_all | solution.py:463
  11.1 25.1 %copy-start.1 = (s32[10,2]{0,1:T(2,128)S(1)}, s32[10,2]{0,1:T(2,128)}, u32[]{:S(2)}) copy-start(s32[10,2]{0,1:T(2,128)} %param.5) | copy-start | bytes 244
  11.1 25.2 %copy-start = (f32[10,128,512]{2,1,0:T(8,128)S(1)}, f32[10,128,512]{2,1,0:T(8,128)}, u32[]{:S(2)}) copy-start(f32[10,128,512]{2,1,0:T(8,128)} %omega.15) | copy-start | bytes 7864324
  17.7 18.5 %all-to-all-start = ((bf16[4,8,128,128]{3,2,1,0:T(8,128)(2,1)}), bf16[4,8,128,128]{3,2,1,0:T(8,128)(2,1)}, u32[]{:S(2)}, u32[]{:S(2)}) async-start(bf16[4,8,128,128]{3,2,1,0:T(8,128)(2,1)} %shard_map.37), calls=%async_computation | async-start | bytes 2097152 | tf_op jit(solution)/shard_map/all_to_all | solution.py:472
  23.4 12.9 %collective-permute-start = (bf16[256,1024]{1,0:T(8,128)(2,1)S(1)}, bf16[256,1024]{1,0:T(8,128)(2,1)}, u32[]{:S(2)}, u32[]{:S(2)}) collective-permute-start(bf16[256,1024]{1,0:T(8,128)(2,1)S(1)} %bitcast.1), channel_id=1, source_target_pairs={{0,4},{4,0},{8,12},{12,8},{16,20},{20,16},{24,28},{28,24},{32,36},... | collective-permute-start | bytes 1572872 | tf_op jit(solution)/shard_map/ppermute | solution.py:453
  25.3 17.8 %collective-permute-start.1 = (bf16[256,1024]{1,0:T(8,128)(2,1)S(1)}, bf16[256,1024]{1,0:T(8,128)(2,1)}, u32[]{:S(2)}, u32[]{:S(2)}) collective-permute-start(bf16[256,1024]{1,0:T(8,128)(2,1)S(1)} %bitcast.2), channel_id=1, source_target_pairs={{0,508},{4,8},{8,4},{12,16},{16,12},{20,24},{24,20},{28,32},{32,28... | collective-permute-start | bytes 1572872 | tf_op jit(solution)/shard_map/ppermute | solution.py:453
  44.7 10.9 %collective-permute-start.3 = (bf16[256,256]{1,0:T(8,128)(2,1)S(1)}, bf16[256,256]{1,0:T(8,128)(2,1)S(1)}, u32[]{:S(2)}, u32[]{:S(2)}) collective-permute-start(bf16[256,256]{1,0:T(8,128)(2,1)S(1)} %shard_map.41), channel_id=1, source_target_pairs={{0,4},{4,0},{8,12},{12,8},{16,20},{20,16},{24,28},{28,24},{32,36},... | collective-permute-start | bytes 393224 | tf_op jit(solution)/shard_map/ppermute | solution.py:453
  46.6 9.6 %collective-permute-start.2 = (bf16[256,256]{1,0:T(8,128)(2,1)S(1)}, bf16[256,256]{1,0:T(8,128)(2,1)S(1)}, u32[]{:S(2)}, u32[]{:S(2)}) collective-permute-start(bf16[256,256]{1,0:T(8,128)(2,1)S(1)} %get-tuple-element.21), channel_id=1, source_target_pairs={{0,508},{4,8},{8,4},{12,16},{16,12},{20,24},{24,20},{28,32},{32,28... | collective-permute-start | bytes 393224 | tf_op jit(solution)/shard_map/ppermute | solution.py:453
  67.6 13.8 %collective-permute-start.6 = (bf16[4,256,256]{2,1,0:T(8,128)(2,1)S(1)}, bf16[4,256,256]{2,1,0:T(8,128)(2,1)S(1)}, u32[]{:S(2)}, u32[]{:S(2)}) collective-permute-start(bf16[4,256,256]{2,1,0:T(8,128)(2,1)S(1)} %all_to_all.20.p_own), channel_id=1, source_target_pairs={{0,508},{4,8},{8,4},{12,16},{16,12},{20,24},{24,20},{28,32},{32,28... | collective-permute-start | bytes 1572872 | tf_op jit(solution)/shard_map/ppermute | solution.py:453
  73.7 7.7 %collective-permute-start.4 = (bf16[4,256,256]{2,1,0:T(8,128)(2,1)S(1)}, bf16[4,256,256]{2,1,0:T(8,128)(2,1)S(1)}, u32[]{:S(2)}, u32[]{:S(2)}) collective-permute-start(bf16[4,256,256]{2,1,0:T(8,128)(2,1)S(1)} %all_to_all.20.p_own), channel_id=1, source_target_pairs={{0,4},{4,0},{8,12},{12,8},{16,20},{20,16},{24,28},{28,24},{32,36},... | collective-permute-start | bytes 1572872 | tf_op jit(solution)/shard_map/ppermute | solution.py:453
  75.6 10.3 %collective-permute-start.5 = (bf16[256,256]{1,0:T(8,128)(2,1)S(1)}, bf16[256,256]{1,0:T(8,128)(2,1)S(1)}, u32[]{:S(2)}, u32[]{:S(2)}) collective-permute-start(bf16[256,256]{1,0:T(8,128)(2,1)S(1)} %add_convert_fusion.1), channel_id=1, source_target_pairs={{0,508},{4,8},{8,4},{12,16},{16,12},{20,24},{24,20},{28,32},{32,28... | collective-permute-start | bytes 393224 | tf_op jit(solution)/shard_map/ppermute | solution.py:453
  84.0 14.0 %collective-permute-start.8 = (bf16[256,256]{1,0:T(8,128)(2,1)S(1)}, bf16[256,256]{1,0:T(8,128)(2,1)S(1)}, u32[]{:S(2)}, u32[]{:S(2)}) collective-permute-start(bf16[256,256]{1,0:T(8,128)(2,1)S(1)} %get-tuple-element.30), channel_id=1, source_target_pairs={{0,4},{4,0},{8,12},{12,8},{16,20},{20,16},{24,28},{28,24},{32,36},... | collective-permute-start | bytes 393224 | tf_op jit(solution)/shard_map/ppermute | solution.py:453
  88.0 10.0 %collective-permute-start.7 = (bf16[256,256]{1,0:T(8,128)(2,1)S(1)}, bf16[256,256]{1,0:T(8,128)(2,1)S(1)}, u32[]{:S(2)}, u32[]{:S(2)}) collective-permute-start(bf16[256,256]{1,0:T(8,128)(2,1)S(1)} %get-tuple-element.29), channel_id=1, source_target_pairs={{0,508},{4,8},{8,4},{12,16},{16,12},{20,24},{24,20},{28,32},{32,28... | collective-permute-start | bytes 393224 | tf_op jit(solution)/shard_map/ppermute | solution.py:453
  108.6 9.3 %collective-permute-start.10 = (bf16[4,256,256]{2,1,0:T(8,128)(2,1)S(1)}, bf16[4,256,256]{2,1,0:T(8,128)(2,1)S(1)}, u32[]{:S(2)}, u32[]{:S(2)}) collective-permute-start(bf16[4,256,256]{2,1,0:T(8,128)(2,1)S(1)} %all_to_all.21.p_own), channel_id=1, source_target_pairs={{0,4},{4,0},{8,12},{12,8},{16,20},{20,16},{24,28},{28,24},{32,36},... | collective-permute-start | bytes 1572872 | tf_op jit(solution)/shard_map/ppermute | solution.py:453
  110.5 13.8 %collective-permute-start.9 = (bf16[4,256,256]{2,1,0:T(8,128)(2,1)S(1)}, bf16[4,256,256]{2,1,0:T(8,128)(2,1)S(1)}, u32[]{:S(2)}, u32[]{:S(2)}) collective-permute-start(bf16[4,256,256]{2,1,0:T(8,128)(2,1)S(1)} %all_to_all.21.p_own), channel_id=1, source_target_pairs={{0,508},{4,8},{8,4},{12,16},{16,12},{20,24},{24,20},{28,32},{32,28... | collective-permute-start | bytes 1572872 | tf_op jit(solution)/shard_map/ppermute | solution.py:453

commit v6 on v4

--- a/solution.py
+++ b/solution.py
@@ -63,25 +63,19 @@
     return lax.rem(lax.axis_index("tiles"), 2) == 0
 
 
-def repeat_kernel(x, out, held, in_sem, out_sems):
-    load = pltpu.make_async_copy(x, held, in_sem)
-    load.start()
-    load.wait()
-    stores = [pltpu.make_async_copy(held, out.at[part], out_sems.at[part]) for part in range(out.shape[0])]
-    for store in stores:
-        store.start()
-    for store in stores:
-        store.wait()
-
-
-def cut_kernel(omega, out, held, pieces, in_sems, out_sems):
+def prepare_kernel(x, omega, copies, out, held, pieces, x_held, x_sem, in_sems, out_sems):
     rows = omega.shape[1]
     others = held.shape[0]
+    x_load = pltpu.make_async_copy(x, x_held, x_sem)
+    x_load.start()
     loads = [
         pltpu.make_async_copy(omega.at[BLK_DEV + k], held.at[k], in_sems.at[k]) for k in range(others)
     ]
     for load in loads:
         load.start()
+    x_load.wait()
+    for part in range(copies.shape[0]):
+        copies[part] = x_held[...]
     stores = []
     for k in range(others):
         loads[k].wait()
@@ -107,7 +101,7 @@
 
 def begin_kernel(
     blocks, coords, omega, parts, s_own, s_cross, s_chip,
-    s_before, s_after, turned, cross, chip, own, slot_of, mats, s_sems, t_sems,
+    s_before, s_after, turned, cross, chip, own, slot_of, mats, parts_held, s_sems, t_sem,
 ):
     rows, width = omega.shape[1:]
     count = parts.shape[0]
@@ -130,30 +124,8 @@
         for copy in windows(s_chip, s_cross):
             copy.start()
 
-    def fill(pair):
-        slot = slot_of[pair]
-        unit = OWN_PAIR if pair == OWN_PAIR else pair % 4 * 2 + pair // 4
-        copies = [
-            pltpu.make_async_copy(
-                parts.at[part, slot - BLK_DEV],
-                turned.at[unit, :, part * rows : (part + 1) * rows],
-                t_sems.at[pair, part],
-            )
-            for part in range(count)
-        ]
-        return slot, unit, copies
-
-    for pair in range(OWN_PAIR + 1):
-        slot, unit, copies = fill(pair)
-
-        @pl.when(slot > 0)
-        def _(copies=copies):
-            for copy in copies:
-                copy.start()
-
-        @pl.when(slot == 0)
-        def _(unit=unit):
-            turned[unit] = jnp.zeros_like(turned[unit])
+    parts_copy = pltpu.make_async_copy(parts, parts_held, t_sem)
+    parts_copy.start()
 
     def convert(pair, carry):
         slot = slot_of[pair]
@@ -177,13 +149,13 @@
     total = dot_nt(mats[0:4].reshape(4 * rows, width), s_after[:, :width])
     total += dot_nt(mats[4:8].reshape(4 * rows, width), s_after[:, width:])
     own[...] += total[2 * rows :]
+    parts_copy.wait()
     for pair in range(OWN_PAIR + 1):
-        slot, unit, copies = fill(pair)
-
-        @pl.when(slot > 0)
-        def _(copies=copies):
-            for copy in copies:
-                copy.wait()
+        slot = slot_of[pair]
+        unit = OWN_PAIR if pair == OWN_PAIR else pair % 4 * 2 + pair // 4
+        for part in range(count):
+            block = parts_held[part, jnp.maximum(slot - BLK_DEV, 0)]
+            turned[unit, :, part * rows : (part + 1) * rows] = jnp.where(slot > 0, block, jnp.zeros_like(block))
 
     own[rows:] += dot_nt(turned[OWN_PAIR], left)
     after = jnp.zeros(own.shape, f32)
@@ -213,13 +185,12 @@
 
 
 def own_kernel(
-    blocks, coords, omega, turned, s_before, s_own, s_after, p_own,
-    tiles, t_own, nat_own, stq, cols_half, rows_half, slot_of, grad, mats,
+    slot_of, omega, turned, s_before, s_own, s_after, p_own,
+    tiles, t_own, nat_own, stq, cols_half, rows_half, grad, mats,
 ):
     rows, width = grad.shape[0] // 2, grad.shape[1] // 2
     quarter = lax.axis_index("samp")
     scale = step_size / (2.0 * s_own.shape[0])
-    find_slots(blocks, coords, slot_of)
     transpose_columns(stq, (s_before, s_own, s_after), quarter)
     natural(nat_own, p_own)
     grad[...] = dot_nn(p_own[quarter], s_own[...]) + dot_nt(stq[1], nat_own[...])
@@ -248,12 +219,11 @@
 
 
 def own_last_kernel(
-    blocks, coords, held, s_own, s_after, stq, p_own, out, rows_half, slot_of, grad, nat_own, tiles, sems,
+    slot_of, held, s_own, s_after, stq, p_own, out, rows_half, grad, nat_own, tiles, sems,
 ):
     rows, width = grad.shape[0] // 2, grad.shape[1] // 2
     quarter = lax.axis_index("samp")
     scale = step_size / (2.0 * s_own.shape[0])
-    find_slots(blocks, coords, slot_of)
     natural(nat_own, p_own)
     grad[...] = dot_nn(p_own[quarter], s_own[...]) + dot_nt(stq[1], nat_own[...])
     slot = slot_of[OWN_PAIR]
@@ -298,13 +268,12 @@
 
 
 def outer_kernel(
-    blocks, coords, omega, turned, s_before, s_own, s_after, stq, cols_half, p_cross, p_chip,
-    tiles, cross, chip, slot_of, nat, ptq, grad, mats, half,
+    slot_of, omega, turned, s_before, s_own, s_after, stq, cols_half, p_cross, p_chip,
+    tiles, cross, chip, nat, ptq, grad, mats, half,
 ):
     rows, width = omega.shape[1:]
     quarter = lax.axis_index("samp")
     scale = step_size / (2.0 * s_own.shape[0])
-    find_slots(blocks, coords, slot_of)
     order_halo(nat, ptq, p_cross, p_chip, quarter)
     total = jnp.zeros(cross.shape, f32)
     for a in range(2 * BLK_DEV):
@@ -326,12 +295,11 @@
 
 
 def inner_kernel(
-    blocks, coords, omega, s_own, s_after, stq, rows_half, p_cross, p_chip, t_own,
-    tiles, own, slot_of, nat, ptq, grad, mats,
+    slot_of, omega, s_own, s_after, stq, rows_half, p_cross, p_chip, t_own,
+    tiles, own, nat, ptq, grad, mats,
 ):
     quarter = lax.axis_index("samp")
     scale = step_size / (2.0 * s_own.shape[0])
-    find_slots(blocks, coords, slot_of)
     order_halo(nat, ptq, p_cross, p_chip, quarter)
     grad[...] = rows_half[...] + dot_nt(stq[1], nat[1])
     update_rows(slot_of, omega, grad, BLK_DEV, scale, tiles, mats)
@@ -339,13 +307,12 @@
 
 
 def last_kernel(
-    blocks, coords, outer, inner, s_after, stq, rows_half, p_cross, p_chip, begun,
-    out, slot_of, nat, ptq, grad, tiles, sems,
+    slot_of, outer, inner, s_after, stq, rows_half, p_cross, p_chip, begun,
+    out, nat, ptq, grad, tiles, sems,
 ):
     rows, width = tiles.shape[1:]
     quarter = lax.axis_index("samp")
     scale = step_size / (2.0 * s_after.shape[0])
-    find_slots(blocks, coords, slot_of)
     order_halo(nat, ptq, p_cross, p_chip, quarter)
     for group in range(2):
         other = dot_nn(ptq[0], s_after[...]) if group == 0 else rows_half[...]
@@ -384,7 +351,6 @@
     chip = [(i, i ^ 1) for i in range(size)]
     cross = [(i, (i - 1) % size if i % 2 == 0 else (i + 1) % size) for i in range(size)]
     shape = jax.ShapeDtypeStruct
-    slots = pltpu.SMEM((OWN_PAIR + 1,), jnp.int32)
     params = pltpu.CompilerParams(vmem_limit_bytes=LIMIT)
 
     def call(body, in_specs, outs, scratch, macs, moved, aliases=None, out_specs=None):
@@ -404,20 +370,17 @@
     def spread(x):
         return lax.all_to_all(jnp.broadcast_to(x[None], (parts,) + x.shape), "samp", 0, 0)
 
-    copies = call(
-        repeat_kernel, [HBM], pltpu.HBM((parts,) + samples.shape, bf16),
-        [pltpu.VMEM(samples.shape, bf16), pltpu.SemaphoreType.DMA, pltpu.SemaphoreType.DMA((parts,))],
-        0, 1 << 20, out_specs=HBM,
-    )(pltpu.with_memory_space_constraint(samples, pltpu.HBM))
-    s_own = lax.all_to_all(copies, "samp", 0, 0).reshape(count, wide)
-    pieces = call(
-        cut_kernel, [HBM], pltpu.HBM((parts, others, rows, rows), bf16),
+    copies, pieces = call(
+        prepare_kernel, [HBM, HBM],
+        (shape((parts,) + samples.shape, bf16), pltpu.HBM((parts, others, rows, rows), bf16)),
         [
             pltpu.VMEM((others, rows, width), f32), pltpu.VMEM((parts, others, rows, rows), bf16),
+            pltpu.VMEM(samples.shape, bf16), pltpu.SemaphoreType.DMA,
             pltpu.SemaphoreType.DMA((others,)), pltpu.SemaphoreType.DMA((others,)),
         ],
-        0, 4 << 20, out_specs=HBM,
-    )(pltpu.with_memory_space_constraint(omega, pltpu.HBM))
+        0, 5 << 20, out_specs=(VMEM, HBM),
+    )(pltpu.with_memory_space_constraint(samples, pltpu.HBM), pltpu.with_memory_space_constraint(omega, pltpu.HBM))
+    s_own = lax.all_to_all(copies, "samp", 0, 0).reshape(count, wide)
     turned_parts = lax.all_to_all(pieces, "samp", 0, 0)
     s_cross, s_chip = exchange(s_own, s_own)
 
@@ -425,14 +388,17 @@
     part = shape((both, count), bf16)
     full = shape((both, count), f32)
     unit = rows * width * count
-    s_before, s_after, turned, to_cross, to_chip, own = call(
+    s_before, s_after, turned, to_cross, to_chip, own, slot_of = call(
         functools.partial(begin_kernel, blocks), [SMEM, VMEM, ANY, VMEM, ANY, ANY],
-        (window, window, shape((OWN_PAIR + 1, rows, width), bf16), part, part, full),
+        (
+            window, window, shape((OWN_PAIR + 1, rows, width), bf16), part, part, full,
+            shape((OWN_PAIR + 1,), jnp.int32),
+        ),
         [
-            slots, pltpu.VMEM((OWN_PAIR + 1, rows, width), bf16),
-            pltpu.SemaphoreType.DMA((2,)), pltpu.SemaphoreType.DMA((OWN_PAIR + 1, parts)),
+            pltpu.VMEM((OWN_PAIR + 1, rows, width), bf16), pltpu.VMEM((parts, others, rows, rows), bf16),
+            pltpu.SemaphoreType.DMA((2,)), pltpu.SemaphoreType.DMA,
         ],
-        20 * unit, 6 << 20,
+        20 * unit, 6 << 20, out_specs=(VMEM,) * 6 + (SMEM,),
     )(coords, omega, turned_parts, s_own, s_cross, s_chip)
 
     def products(to_cross, to_chip, finish):
@@ -452,36 +418,36 @@
     _, p_own, p_cross, p_chip = products(to_cross, to_chip, lambda: (None, own))
     wide_half = shape((both, wide), f32)
     mine, t_own, _, stq, cols_half, rows_half = call(
-        functools.partial(own_kernel, blocks), [SMEM] + [VMEM] * 6,
+        own_kernel, [SMEM] + [VMEM] * 6,
         (
             shape((3, rows, width), f32), full, shape((wide, count), bf16), shape((3, both, count), bf16),
             wide_half, wide_half,
         ),
-        [slots, grad, mats], 20 * unit, 6 << 20,
-    )(coords, omega, turned, s_before, s_own, s_after, p_own)
+        [grad, mats], 20 * unit, 6 << 20,
+    )(slot_of, omega, turned, s_before, s_own, s_after, p_own)
     outer, to_cross, to_chip = call(
-        functools.partial(outer_kernel, blocks), [SMEM] + [VMEM] * 9,
-        (four, part, part), [slots, nat, ptq, grad, mats, pltpu.VMEM((both, width), f32)], 32 * unit, 6 << 20,
-    )(coords, omega, turned, s_before, s_own, s_after, stq, cols_half, p_cross, p_chip)
+        outer_kernel, [SMEM] + [VMEM] * 9,
+        (four, part, part), [nat, ptq, grad, mats, pltpu.VMEM((both, width), f32)], 32 * unit, 6 << 20,
+    )(slot_of, omega, turned, s_before, s_own, s_after, stq, cols_half, p_cross, p_chip)
 
     def finish():
         return call(
-            functools.partial(inner_kernel, blocks), [SMEM] + [VMEM] * 8,
-            (four, full), [slots, nat, ptq, grad, mats], 8 * unit, 4 << 20,
-        )(coords, omega, s_own, s_after, stq, rows_half, p_cross, p_chip, t_own)
+            inner_kernel, [SMEM] + [VMEM] * 8,
+            (four, full), [nat, ptq, grad, mats], 8 * unit, 4 << 20,
+        )(slot_of, omega, s_own, s_after, stq, rows_half, p_cross, p_chip, t_own)
 
     inner, p_own, p_cross, p_chip = products(to_cross, to_chip, finish)
     whole = shape(omega.shape, f32)
     begun, rows_half = call(
-        functools.partial(own_last_kernel, blocks), [SMEM] + [VMEM] * 5, (whole, wide_half),
-        [slots, grad, pltpu.VMEM((wide, count), bf16), pltpu.VMEM((3, rows, width), f32), pltpu.SemaphoreType.DMA((3,))],
+        own_last_kernel, [SMEM] + [VMEM] * 5, (whole, wide_half),
+        [grad, pltpu.VMEM((wide, count), bf16), pltpu.VMEM((3, rows, width), f32), pltpu.SemaphoreType.DMA((3,))],
         12 * unit, 3 << 20, out_specs=(ANY, VMEM),
-    )(coords, mine, s_own, s_after, stq, p_own)
+    )(slot_of, mine, s_own, s_after, stq, p_own)
     return call(
-        functools.partial(last_kernel, blocks), [SMEM] + [VMEM] * 7 + [ANY], whole,
-        [slots, nat, ptq, pltpu.VMEM((2, both, wide), f32), pltpu.VMEM((8, rows, width), f32), pltpu.SemaphoreType.DMA((8,))],
+        last_kernel, [SMEM] + [VMEM] * 7 + [ANY], whole,
+        [nat, ptq, pltpu.VMEM((2, both, wide), f32), pltpu.VMEM((8, rows, width), f32), pltpu.SemaphoreType.DMA((8,))],
         12 * unit, 6 << 20, aliases={8: 0}, out_specs=ANY,
-    )(coords, outer, inner, s_after, stq, rows_half, p_cross, p_chip, begun)
+    )(slot_of, outer, inner, s_after, stq, rows_half, p_cross, p_chip, begun)
 
 
 def solution(mesh):

time: 127 us -> 128 us (level)
  blocking collectives: 23.4 us -> 38.3 us
  starting transfers between devices: 54.4 us -> 45.9 us
  waiting for transfers between devices: 29.4 us -> 25.9 us
  Pallas kernels: 18.9 us -> 17.3 us
    all_to_all x0 -> x1, blocking collectives: none -> 14.9 us  [shards(): s_own = lax.all_to_all(copies, 'samp', 0, 0).reshape(count, wide)]
    all_to_all x1 -> x0, starting transfers between devices: 9.33 us -> none  [shards(): s_own = lax.all_to_all(copies, 'samp', 0, 0).reshape(count, wide)]
    all_to_all x1 -> x0, waiting for transfers between devices: 4 us -> none  [shards(): s_own = lax.all_to_all(copies, 'samp', 0, 0).reshape(count, wide)]
    pallas_call x7 -> x6, Pallas kernels: 15.1 us -> 13.3 us  [the longest x1 3.18 us: shards(): call(prepare_kernel, [HBM, HBM], (shape((parts,) + samples.shape, bf16),...]
  transfers between devices with their start and end apart: 12 -> 11, of which waited for: 7 -> 6; matrix products, arithmetic and copies ran while one was open for 0% -> 0% of each run, Pallas kernels for 7% -> 4%
where the time goes in v6:
time: 128 us
  starting transfers between devices  45.9 us (36%)
  blocking collectives  38.3 us (30%)
  waiting for transfers between devices  25.9 us (20%)
  Pallas kernels  17.3 us (14%)
    ppermute x5, starting transfers between devices, exchange(): from_cross = lax.ppermute(to_cross, 'tiles', cross)  30.7 us
    ppermute x5, waiting for transfers between devices, exchange(): from_cross = lax.ppermute(to_cross, 'tiles', cross)  25.3 us
    all_to_all x2, blocking collectives, spread(): lax.all_to_all(jnp.broadcast_to(x[None], (parts,) + x.shape), 'samp', 0, 0)  23.4 us
    all_to_all x1, blocking collectives, shards(): s_own = lax.all_to_all(copies, 'samp', 0, 0).reshape(count, wide)  14.9 us
    ppermute x5, starting transfers between devices, exchange(): from_chip = lax.ppermute(to_chip, 'tiles', chip)  9.57 us
    all_to_all x1, starting transfers between devices, shards(): turned_parts = lax.all_to_all(pieces, 'samp', 0, 0)  5.65 us
    pallas_call x1, Pallas kernels, shards(): call(functools.partial(begin_kernel, blocks), [SMEM, VMEM, ANY, VMEM, ANY...  4.01 us
    pallas_call x1, Pallas kernels, shards(): call(prepare_kernel, [HBM, HBM], (shape((parts,) + samples.shape, bf16),...  3.18 us
  transfers between devices with their start and end apart: 11, of which 6 were waited for; matrix products, arithmetic and copies ran while one was open for 0% of the time, Pallas kernels for 4%

profile of v6, /device:TPU:2, one launch (start us, length us, event | category | flops | bytes accessed | tf_op | source)
XLA Modules:
  0.0 127.8 jit_solution(4154814946571748950)
XLA Ops:
  0.0 3.2 %shard_map.37 = (bf16[4,64,1024]{2,1,0:T(8,128)(2,1)S(1)}, bf16[4,8,128,128]{3,2,1,0:T(8,128)(2,1)}) custom-call(bf16[64,1024]{1,0:T(8,128)(2,1)} %x.1, f32[10,128,512]{2,1,0:T(8,128)} %omega.9), custom_call_target="tpu_custom_call" | custom-call | bytes 5242880 | tf_op jit(solution)/shard_map/pallas_call | solution.py:373
  3.2 14.9 %all_to_all.20 = bf16[4,64,1024]{2,1,0:T(8,128)(2,1)S(1)} all-to-all(bf16[4,64,1024]{2,1,0:T(8,128)(2,1)S(1)} %get-tuple-element.27), channel_id=1, replica_groups=mesh['tiles'=128,'samp'=4] {'samp'}, dimensions={0} | all-to-all | bytes 1048576 | tf_op jit(solution)/shard_map/all_to_all | solution.py:383
  18.1 5.7 %all-to-all-start = ((bf16[4,8,128,128]{3,2,1,0:T(8,128)(2,1)}), bf16[4,8,128,128]{3,2,1,0:T(8,128)(2,1)}, u32[]{:S(2)}, u32[]{:S(2)}) async-start(bf16[4,8,128,128]{3,2,1,0:T(8,128)(2,1)} %get-tuple-element.26), calls=%async_computation | async-start | bytes 2097152 | tf_op jit(solution)/shard_map/all_to_all | solution.py:384
  23.7 1.9 %collective-permute-start.1 = (bf16[256,1024]{1,0:T(8,128)(2,1)S(1)}, bf16[256,1024]{1,0:T(8,128)(2,1)}, u32[]{:S(2)}, u32[]{:S(2)}) collective-permute-start(bf16[256,1024]{1,0:T(8,128)(2,1)S(1)} %bitcast.1), channel_id=1, source_target_pairs={{0,4},{4,0},{8,12},{12,8},{16,20},{20,16},{24,28},{28,24},{32,36},... | collective-permute-start | bytes 1572872 | tf_op jit(solution)/shard_map/ppermute | solution.py:366
  25.7 11.7 %collective-permute-start = (bf16[256,1024]{1,0:T(8,128)(2,1)S(1)}, bf16[256,1024]{1,0:T(8,128)(2,1)}, u32[]{:S(2)}, u32[]{:S(2)}) collective-permute-start(bf16[256,1024]{1,0:T(8,128)(2,1)S(1)} %bitcast.2), channel_id=1, source_target_pairs={{0,508},{4,8},{8,4},{12,16},{16,12},{20,24},{24,20},{28,32},{32,28... | collective-permute-start | bytes 1572872 | tf_op jit(solution)/shard_map/ppermute | solution.py:367
  37.5 6.8 %collective-permute-done.s_cross = bf16[256,1024]{1,0:T(8,128)(2,1)} collective-permute-done((bf16[256,1024]{1,0:T(8,128)(2,1)S(1)}, bf16[256,1024]{1,0:T(8,128)(2,1)}, u32[]{:S(2)}, u32[]{:S(2)}) %collective-permute-start) | collective-permute-done | bytes 524320 | tf_op jit(solution)/shard_map/ppermute | solution.py:367
  44.3 4.0 %shard_map.38 = (bf16[256,1024]{1,0:T(8,128)(2,1)S(1)}, bf16[256,1024]{1,0:T(8,128)(2,1)S(1)}, bf16[9,128,512]{2,1,0:T(8,128)(2,1)S(1)}, bf16[256,256]{1,0:T(8,1...) custom-call(s32[10,2]{1,0:T(8,128)S(1)} %copy.5.coords, ...), custom_call_target="tpu_custom_call" | custom-call | flops 671088640 | bytes 6291456 | tf_op jit(solution)/shard_map/pallas_call | solution.py:391
  48.3 7.0 %collective-permute-start.2 = (bf16[256,256]{1,0:T(8,128)(2,1)S(1)}, bf16[256,256]{1,0:T(8,128)(2,1)S(1)}, u32[]{:S(2)}, u32[]{:S(2)}) collective-permute-start(bf16[256,256]{1,0:T(8,128)(2,1)S(1)} %get-tuple-element.33), channel_id=1, source_target_pairs={{0,508},{4,8},{8,4},{12,16},{16,12},{20,24},{24,20},{28,32},{32,28... | collective-permute-start | bytes 393224 | tf_op jit(solution)/shard_map/ppermute | solution.py:367
  55.3 1.9 %collective-permute-start.3 = (bf16[256,256]{1,0:T(8,128)(2,1)S(1)}, bf16[256,256]{1,0:T(8,128)(2,1)S(1)}, u32[]{:S(2)}, u32[]{:S(2)}) collective-permute-start(bf16[256,256]{1,0:T(8,128)(2,1)S(1)} %get-tuple-element.34), channel_id=1, source_target_pairs={{0,4},{4,0},{8,12},{12,8},{16,20},{20,16},{24,28},{28,24},{32,36},... | collective-permute-start | bytes 393224 | tf_op jit(solution)/shard_map/ppermute | solution.py:366
  58.7 12.9 %all_to_all.21.p_own = bf16[4,256,256]{2,1,0:T(8,128)(2,1)S(1)} all-to-all(bf16[4,256,256]{2,1,0:T(8,128)(2,1)S(1)} %broadcast_in_dim.4), channel_id=1, replica_groups=mesh['tiles'=128,'samp'=4] {'samp'}, dimensions={0} | all-to-all | bytes 1048576 | tf_op jit(solution)/shard_map/all_to_all | solution.py:371
  71.6 1.9 %collective-permute-start.5 = (bf16[4,256,256]{2,1,0:T(8,128)(2,1)S(1)}, bf16[4,256,256]{2,1,0:T(8,128)(2,1)S(1)}, u32[]{:S(2)}, u32[]{:S(2)}) collective-permute-start(bf16[4,256,256]{2,1,0:T(8,128)(2,1)S(1)} %all_to_all.21.p_own), channel_id=1, source_target_pairs={{0,4},{4,0},{8,12},{12,8},{16,20},{20,16},{24,28},{28,24},{32,36},... | collective-permute-start | bytes 1572872 | tf_op jit(solution)/shard_map/ppermute | solution.py:366
  73.5 3.2 %collective-permute-start.4 = (bf16[4,256,256]{2,1,0:T(8,128)(2,1)S(1)}, bf16[4,256,256]{2,1,0:T(8,128)(2,1)S(1)}, u32[]{:S(2)}, u32[]{:S(2)}) collective-permute-start(bf16[4,256,256]{2,1,0:T(8,128)(2,1)S(1)} %all_to_all.21.p_own), channel_id=1, source_target_pairs={{0,508},{4,8},{8,4},{12,16},{16,12},{20,24},{24,20},{28,32},{32,28... | collective-permute-start | bytes 1572872 | tf_op jit(solution)/shard_map/ppermute | solution.py:367
  76.7 2.2 %shard_map.39 = (f32[3,128,512]{2,1,0:T(8,128)S(1)}, f32[256,256]{1,0:T(8,128)S(1)}, bf16[1024,256]{1,0:T(8,128)(2,1)}, bf16[3,256,256]{2,1,0:T(8,128)(2,1)S(1)}...) custom-call(s32[9]{0:T(128)S(1)} %get-tuple-element.28.slot_of, f32[10,128,512]{2,1,0:T(8,128)S(1)} %copy-done, ...), custom_call_target="tpu_custom_call" | custom-call | flops 671088640 | bytes 6291456 | tf_op jit(solution)/shard_map/pallas_call | solution.py:420
  78.9 8.4 %collective-permute-done.4.p_cross = bf16[4,256,256]{2,1,0:T(8,128)(2,1)S(1)} collective-permute-done((bf16[4,256,256]{2,1,0:T(8,128)(2,1)S(1)}, bf16[4,256,256]{2,1,0:T(8,128)(2,1)S(1)}, u32[]{:S(2)}, u32[]{:S(2)}) %collective-permute-start.4) | collective-permute-done | bytes 524320 | tf_op jit(solution)/shard_map/ppermute | solution.py:367
  87.3 2.2 %shard_map.40 = (f32[4,128,512]{2,1,0:T(8,128)S(1)}, bf16[256,256]{1,0:T(8,128)(2,1)S(1)}, bf16[256,256]{1,0:T(8,128)(2,1)S(1)}) custom-call(s32[9]{0:T(128)S(1)} %get-tuple-element.28.slot_of, f32[10,128,512]{2,1,0:T(8,128)S(1)} %copy-done, bf16[9,128,512]{2,1,0:T(8,128)(2,1)S(1)} %get-tuple-element.29.turned, ...), custom_call_target="tpu_custom_call" | custom-call | flops 1073741824 | bytes 6291456 | tf_op jit(solution)/shard_map/pallas_call | solution.py:428
  89.5 3.2 %collective-permute-start.6 = (bf16[256,256]{1,0:T(8,128)(2,1)S(1)}, bf16[256,256]{1,0:T(8,128)(2,1)S(1)}, u32[]{:S(2)}, u32[]{:S(2)}) collective-permute-start(bf16[256,256]{1,0:T(8,128)(2,1)S(1)} %get-tuple-element.43), channel_id=1, source_target_pairs={{0,508},{4,8},{8,4},{12,16},{16,12},{20,24},{24,20},{28,32},{32,28... | collective-permute-start | bytes 393224 | tf_op jit(solution)/shard_map/ppermute | solution.py:367
  92.7 1.9 %collective-permute-start.7 = (bf16[256,256]{1,0:T(8,128)(2,1)S(1)}, bf16[256,256]{1,0:T(8,128)(2,1)S(1)}, u32[]{:S(2)}, u32[]{:S(2)}) collective-permute-start(bf16[256,256]{1,0:T(8,128)(2,1)S(1)} %get-tuple-element.44), channel_id=1, source_target_pairs={{0,4},{4,0},{8,12},{12,8},{16,20},{20,16},{24,28},{28,24},{32,36},... | collective-permute-start | bytes 393224 | tf_op jit(solution)/shard_map/ppermute | solution.py:366
  95.9 3.2 %collective-permute-done.6 = bf16[256,256]{1,0:T(8,128)(2,1)S(1)} collective-permute-done((bf16[256,256]{1,0:T(8,128)(2,1)S(1)}, bf16[256,256]{1,0:T(8,128)(2,1)S(1)}, u32[]{:S(2)}, u32[]{:S(2)}) %collective-permute-start.6) | collective-permute-done | bytes 131104 | tf_op jit(solution)/shard_map/ppermute | solution.py:367
  99.2 10.5 %all_to_all.22.p_own = bf16[4,256,256]{2,1,0:T(8,128)(2,1)S(1)} all-to-all(bf16[4,256,256]{2,1,0:T(8,128)(2,1)S(1)} %broadcast_in_dim.5), channel_id=1, replica_groups=mesh['tiles'=128,'samp'=4] {'samp'}, dimensions={0} | all-to-all | bytes 1048576 | tf_op jit(solution)/shard_map/all_to_all | solution.py:371
  109.7 1.9 %collective-permute-start.9 = (bf16[4,256,256]{2,1,0:T(8,128)(2,1)S(1)}, bf16[4,256,256]{2,1,0:T(8,128)(2,1)S(1)}, u32[]{:S(2)}, u32[]{:S(2)}) collective-permute-start(bf16[4,256,256]{2,1,0:T(8,128)(2,1)S(1)} %all_to_all.22.p_own), channel_id=1, source_target_pairs={{0,4},{4,0},{8,12},{12,8},{16,20},{20,16},{24,28},{28,24},{32,36},... | collective-permute-start | bytes 1572872 | tf_op jit(solution)/shard_map/ppermute | solution.py:366
  111.6 5.6 %collective-permute-start.8 = (bf16[4,256,256]{2,1,0:T(8,128)(2,1)S(1)}, bf16[4,256,256]{2,1,0:T(8,128)(2,1)S(1)}, u32[]{:S(2)}, u32[]{:S(2)}) collective-permute-start(bf16[4,256,256]{2,1,0:T(8,128)(2,1)S(1)} %all_to_all.22.p_own), channel_id=1, source_target_pairs={{0,508},{4,8},{8,4},{12,16},{16,12},{20,24},{24,20},{28,32},{32,28... | collective-permute-start | bytes 1572872 | tf_op jit(solution)/shard_map/ppermute | solution.py:367
  117.2 2.1 %shard_map.42 = (f32[10,128,512]{2,1,0:T(8,128)}, f32[256,1024]{1,0:T(8,128)S(1)}) custom-call(s32[9]{0:T(128)S(1)} %get-tuple-element.28.slot_of, f32[3,128,512]{2,1,0:T(8,128)S(1)} %get-tuple-element.41.held, bf16[256,1024]{1,0:T(8,128)(2,1)S(1)} %bitcast.7, bf16[256,1024]{1,0:T(8,128)(2,1)S(1)} %get-tuple-element.31.s_after, ...), custom_call_target="tpu_custom_call" | custom-call | flops 402653184 | bytes 3145728 | tf_op jit(solution)/shard_map/pallas_call | solution.py:441
  119.3 6.1 %collective-permute-done.8.p_cross = bf16[4,256,256]{2,1,0:T(8,128)(2,1)S(1)} collective-permute-done((bf16[4,256,256]{2,1,0:T(8,128)(2,1)S(1)}, bf16[4,256,256]{2,1,0:T(8,128)(2,1)S(1)}, u32[]{:S(2)}, u32[]{:S(2)}) %collective-permute-start.8) | collective-permute-done | bytes 524320 | tf_op jit(solution)/shard_map/ppermute | solution.py:367
  125.4 2.4 %shard_map.43 = f32[10,128,512]{2,1,0:T(8,128)} custom-call(s32[9]{0:T(128)S(1)} %get-tuple-element.28.slot_of, f32[4,128,512]{2,1,0:T(8,128)S(1)} %get-tuple-element.37.outer, f32[4,128,512]{2,1,0:T(8,128)S(1)} %get-tuple-element.40.inner, bf16[256,1024]{1,0:T(8,128)(2,1)S(1)} %get-tuple-element.31.s_after, ...), custom_call_target="tpu_custom_call", output_to_operand_aliasing={{}: (8, {})} | custom-call | flops 402653184 | bytes 6291456 | tf_op jit(solution)/shard_map/pallas_call | solution.py:446
  (17 shorter events, 2.8 us)
Async XLA Ops:
  0.0 44.3 %copy-start = (f32[10,128,512]{2,1,0:T(8,128)S(1)}, f32[10,128,512]{2,1,0:T(8,128)}, u32[]{:S(2)}) copy-start(f32[10,128,512]{2,1,0:T(8,128)} %omega.9) | copy-start | bytes 7864324
  0.0 37.4 %copy-start.1 = (s32[10,2]{0,1:T(2,128)S(1)}, s32[10,2]{0,1:T(2,128)}, u32[]{:S(2)}) copy-start(s32[10,2]{0,1:T(2,128)} %param.5) | copy-start | bytes 244
  18.1 19.4 %all-to-all-start = ((bf16[4,8,128,128]{3,2,1,0:T(8,128)(2,1)}), bf16[4,8,128,128]{3,2,1,0:T(8,128)(2,1)}, u32[]{:S(2)}, u32[]{:S(2)}) async-start(bf16[4,8,128,128]{3,2,1,0:T(8,128)(2,1)} %get-tuple-element.26), calls=%async_computation | async-start | bytes 2097152 | tf_op jit(solution)/shard_map/all_to_all | solution.py:384
  23.7 13.7 %collective-permute-start.1 = (bf16[256,1024]{1,0:T(8,128)(2,1)S(1)}, bf16[256,1024]{1,0:T(8,128)(2,1)}, u32[]{:S(2)}, u32[]{:S(2)}) collective-permute-start(bf16[256,1024]{1,0:T(8,128)(2,1)S(1)} %bitcast.1), channel_id=1, source_target_pairs={{0,4},{4,0},{8,12},{12,8},{16,20},{20,16},{24,28},{28,24},{32,36},... | collective-permute-start | bytes 1572872 | tf_op jit(solution)/shard_map/ppermute | solution.py:366
  25.7 18.7 %collective-permute-start = (bf16[256,1024]{1,0:T(8,128)(2,1)S(1)}, bf16[256,1024]{1,0:T(8,128)(2,1)}, u32[]{:S(2)}, u32[]{:S(2)}) collective-permute-start(bf16[256,1024]{1,0:T(8,128)(2,1)S(1)} %bitcast.2), channel_id=1, source_target_pairs={{0,508},{4,8},{8,4},{12,16},{16,12},{20,24},{24,20},{28,32},{32,28... | collective-permute-start | bytes 1572872 | tf_op jit(solution)/shard_map/ppermute | solution.py:367
  48.3 9.6 %collective-permute-start.2 = (bf16[256,256]{1,0:T(8,128)(2,1)S(1)}, bf16[256,256]{1,0:T(8,128)(2,1)S(1)}, u32[]{:S(2)}, u32[]{:S(2)}) collective-permute-start(bf16[256,256]{1,0:T(8,128)(2,1)S(1)} %get-tuple-element.33), channel_id=1, source_target_pairs={{0,508},{4,8},{8,4},{12,16},{16,12},{20,24},{24,20},{28,32},{32,28... | collective-permute-start | bytes 393224 | tf_op jit(solution)/shard_map/ppermute | solution.py:367
  55.3 3.2 %collective-permute-start.3 = (bf16[256,256]{1,0:T(8,128)(2,1)S(1)}, bf16[256,256]{1,0:T(8,128)(2,1)S(1)}, u32[]{:S(2)}, u32[]{:S(2)}) collective-permute-start(bf16[256,256]{1,0:T(8,128)(2,1)S(1)} %get-tuple-element.34), channel_id=1, source_target_pairs={{0,4},{4,0},{8,12},{12,8},{16,20},{20,16},{24,28},{28,24},{32,36},... | collective-permute-start | bytes 393224 | tf_op jit(solution)/shard_map/ppermute | solution.py:366
  71.6 7.3 %collective-permute-start.5 = (bf16[4,256,256]{2,1,0:T(8,128)(2,1)S(1)}, bf16[4,256,256]{2,1,0:T(8,128)(2,1)S(1)}, u32[]{:S(2)}, u32[]{:S(2)}) collective-permute-start(bf16[4,256,256]{2,1,0:T(8,128)(2,1)S(1)} %all_to_all.21.p_own), channel_id=1, source_target_pairs={{0,4},{4,0},{8,12},{12,8},{16,20},{20,16},{24,28},{28,24},{32,36},... | collective-permute-start | bytes 1572872 | tf_op jit(solution)/shard_map/ppermute | solution.py:366
  73.5 13.8 %collective-permute-start.4 = (bf16[4,256,256]{2,1,0:T(8,128)(2,1)S(1)}, bf16[4,256,256]{2,1,0:T(8,128)(2,1)S(1)}, u32[]{:S(2)}, u32[]{:S(2)}) collective-permute-start(bf16[4,256,256]{2,1,0:T(8,128)(2,1)S(1)} %all_to_all.21.p_own), channel_id=1, source_target_pairs={{0,508},{4,8},{8,4},{12,16},{16,12},{20,24},{24,20},{28,32},{32,28... | collective-permute-start | bytes 1572872 | tf_op jit(solution)/shard_map/ppermute | solution.py:367
  89.5 9.6 %collective-permute-start.6 = (bf16[256,256]{1,0:T(8,128)(2,1)S(1)}, bf16[256,256]{1,0:T(8,128)(2,1)S(1)}, u32[]{:S(2)}, u32[]{:S(2)}) collective-permute-start(bf16[256,256]{1,0:T(8,128)(2,1)S(1)} %get-tuple-element.43), channel_id=1, source_target_pairs={{0,508},{4,8},{8,4},{12,16},{16,12},{20,24},{24,20},{28,32},{32,28... | collective-permute-start | bytes 393224 | tf_op jit(solution)/shard_map/ppermute | solution.py:367
  92.7 6.4 %collective-permute-start.7 = (bf16[256,256]{1,0:T(8,128)(2,1)S(1)}, bf16[256,256]{1,0:T(8,128)(2,1)S(1)}, u32[]{:S(2)}, u32[]{:S(2)}) collective-permute-start(bf16[256,256]{1,0:T(8,128)(2,1)S(1)} %get-tuple-element.44), channel_id=1, source_target_pairs={{0,4},{4,0},{8,12},{12,8},{16,20},{20,16},{24,28},{28,24},{32,36},... | collective-permute-start | bytes 393224 | tf_op jit(solution)/shard_map/ppermute | solution.py:366
  109.7 9.6 %collective-permute-start.9 = (bf16[4,256,256]{2,1,0:T(8,128)(2,1)S(1)}, bf16[4,256,256]{2,1,0:T(8,128)(2,1)S(1)}, u32[]{:S(2)}, u32[]{:S(2)}) collective-permute-start(bf16[4,256,256]{2,1,0:T(8,128)(2,1)S(1)} %all_to_all.22.p_own), channel_id=1, source_target_pairs={{0,4},{4,0},{8,12},{12,8},{16,20},{20,16},{24,28},{28,24},{32,36},... | collective-permute-start | bytes 1572872 | tf_op jit(solution)/shard_map/ppermute | solution.py:366
  111.6 13.8 %collective-permute-start.8 = (bf16[4,256,256]{2,1,0:T(8,128)(2,1)S(1)}, bf16[4,256,256]{2,1,0:T(8,128)(2,1)S(1)}, u32[]{:S(2)}, u32[]{:S(2)}) collective-permute-start(bf16[4,256,256]{2,1,0:T(8,128)(2,1)S(1)} %all_to_all.22.p_own), channel_id=1, source_target_pairs={{0,508},{4,8},{8,4},{12,16},{16,12},{20,24},{24,20},{28,32},{32,28... | collective-permute-start | bytes 1572872 | tf_op jit(solution)/shard_map/ppermute | solution.py:367

commit v7 on v5

--- a/solution.py
+++ b/solution.py
@@ -227,23 +227,28 @@
             out[:, at : at + rows] = piece[:, blk * rows : (blk + 1) * rows]
 
 
-def update_edge(old, slots, ptq, far, s_near, p_near, scale, grad, put):
-    count, both = p_near.shape[0], p_near.shape[1]
+def natural(out, pieces):
+    count, both = pieces.shape[0], pieces.shape[1]
     rows = both // BLK_DEV
-    grad[...] = dot_nn(ptq, s_near[...])
-    for part in range(count):
-        piece = dot_nt(far, p_near[part])
-        for i in range(2):
-            for blk in range(2):
-                at = spot(i, rows, (blk * count + part) * rows, rows)
-                here = grad[at] + piece[i * rows : (i + 1) * rows, blk * rows : (blk + 1) * rows]
-                slot = slots(i, blk)
-                put(i, blk, part, slot, shrink(old(i, blk, part, slot) - scale * here))
+    for blk in range(BLK_DEV):
+        for part in range(count):
+            at = (blk * count + part) * rows
+            out[at : at + rows, :] = pieces[part, blk * rows : (blk + 1) * rows, :]
+
+
+def update_edge(old, slots, ptq, far, s_near, p_near, scale, grad, nat, put):
+    rows, width = grad.shape[0] // 2, grad.shape[1] // 2
+    natural(nat, p_near)
+    grad[...] = dot_nn(ptq, s_near[...]) + dot_nt(far, nat[...])
+    for i in range(2):
+        for blk in range(2):
+            slot = slots(i, blk)
+            put(i, blk, slot, shrink(old(i, blk, slot) - scale * grad[spot(i, rows, blk * width, width)]))
 
 
 def edge_kernel(
     blocks, far_side, coords, omega, turned, s_own, s_near, p_near, p_far, stq, own_half,
-    tiles, out, slot_of, grad, mats,
+    tiles, out, slot_of, grad, mats, nat,
 ):
     rows, width = omega.shape[1:]
     wide = s_own.shape[1]
@@ -251,31 +256,28 @@
     scale = step_size / (2.0 * s_own.shape[0])
     find_slots(blocks, coords, slot_of)
 
-    def columns(part):
-        return slice(part * rows, (part + 1) * rows)
-
     def far_rows():
         return p_far[quarter] if far_side else p_far[...]
 
     def row_tiles():
-        def put(i, blk, part, slot, tile):
-            tiles[i * 2 + blk, :, columns(part)] = tile
-            put_tile(slot, tile, mats, spot(i, rows, blk * width + part * rows, rows))
+        def put(i, blk, slot, tile):
+            tiles[i * 2 + blk] = tile
+            put_tile(slot, tile, mats, spot(i, rows, blk * width, width))
 
         update_edge(
-            lambda i, blk, part, slot: omega[slot, :, columns(part)], lambda i, blk: slot_of[blk * 4 + i],
-            far_rows(), stq[far_side], s_near, p_near, scale, grad, put,
+            lambda i, blk, slot: omega[slot], lambda i, blk: slot_of[blk * 4 + i],
+            far_rows(), stq[far_side], s_near, p_near, scale, grad, nat, put,
         )
         out[...] = dot_nt(mats[:, :wide], s_near[...]).astype(bf16)
 
     def col_tiles():
-        def put(i, blk, part, slot, tile):
-            put_tile(slot, tile, mats, spot(i, rows, blk * width + part * rows, rows))
+        def put(i, blk, slot, tile):
+            put_tile(slot, tile, mats, spot(i, rows, blk * width, width))
 
         update_edge(
-            lambda i, blk, part, slot: turned[2 * blk + i, :, columns(part)].astype(f32),
+            lambda i, blk, slot: turned[2 * blk + i].astype(f32),
             lambda i, blk: slot_of[i * 4 + blk],
-            far_rows(), stq[far_side], s_near, p_near, scale, grad, put,
+            far_rows(), stq[far_side], s_near, p_near, scale, grad, nat, put,
         )
         grad[...] = dot_nn(far_rows(), s_own[...]) + own_half[...]
         for i in range(2):
@@ -286,15 +288,6 @@
         out[...] = total.astype(bf16)
 
     choose(far_side == 0, row_tiles, col_tiles)
-
-
-def natural(out, pieces):
-    count, both = pieces.shape[0], pieces.shape[1]
-    rows = both // BLK_DEV
-    for blk in range(BLK_DEV):
-        for part in range(count):
-            at = (blk * count + part) * rows
-            out[at : at + rows, :] = pieces[part, blk * rows : (blk + 1) * rows, :]
 
 
 def own_kernel(blocks, coords, omega, turned, s_own, stq, p_own, tiles, t_own, slot_of, grad, mats, nat_own):
@@ -317,22 +310,22 @@
 
 
 def inner_kernel(
-    blocks, coords, omega, s_cross, s_chip, stq, p_own, p_cross, p_chip, t_own, tiles, own, slot_of, grad, mats
+    blocks, coords, omega, s_cross, s_chip, stq, p_own, p_cross, p_chip, t_own, tiles, own, slot_of, grad, mats, nat
 ):
     rows, width = omega.shape[1:]
     quarter = lax.axis_index("samp")
     scale = step_size / (2.0 * s_chip.shape[0])
     find_slots(blocks, coords, slot_of)
 
-    def put(i, blk, part, slot, tile):
-        tiles[i * 2 + blk, :, part * rows : (part + 1) * rows] = tile
-        put_tile(slot, tile, mats, spot(i, rows, blk * width + part * rows, rows))
+    def put(i, blk, slot, tile):
+        tiles[i * 2 + blk] = tile
+        put_tile(slot, tile, mats, spot(i, rows, blk * width, width))
 
     def run(s_next, p_next):
         update_edge(
-            lambda i, blk, part, slot: omega[slot, :, part * rows : (part + 1) * rows],
+            lambda i, blk, slot: omega[slot],
             lambda i, blk: slot_of[blk * 4 + BLK_DEV + i],
-            p_own[quarter], stq[1], s_next, p_next, scale, grad, put,
+            p_own[quarter], stq[1], s_next, p_next, scale, grad, nat, put,
         )
         own[...] = t_own[...] + dot_nt(mats[...], s_next[...])
 
@@ -375,11 +368,10 @@
 
 def last_kernel(
     blocks, coords, outer_cross, outer_chip, inner, s_cross, s_chip, stq, rows_half, p_cross, p_chip, begun,
-    out, slot_of, grad, tiles, sems,
+    out, slot_of, grad, nat, tiles, sems,
 ):
-    rows, _ = tiles.shape[1:]
+    rows, width = tiles.shape[1:]
     quarter = lax.axis_index("samp")
-    count = p_chip.shape[0]
     scale = step_size / (2.0 * s_chip.shape[0])
     find_slots(blocks, coords, slot_of)
 
@@ -390,21 +382,15 @@
         return slot_of[blk * 4 + group * BLK_DEV + i]
 
     def run(outer, s_next, p_next, p_far, far):
-        grad[...] = dot_nn(p_far[quarter], s_next[...])
+        natural(nat, p_next)
         for group in (1, 0):
-            rest = (grad, rows_half)[group]
-            for part in range(count):
-                piece = dot_nt((far, stq[1])[group], p_next[part])
-                for i in range(2):
-                    for blk in range(2):
-                        at = spot(i, rows, (blk * count + part) * rows, rows)
-                        here = rest[at] + piece[i * rows : (i + 1) * rows, blk * rows : (blk + 1) * rows]
-                        cols = slice(part * rows, (part + 1) * rows)
-                        old = (outer, inner)[group][i * 2 + blk, :, cols]
-                        tiles[group * 4 + i * 2 + blk, :, cols] = shrink(old - scale * here)
+            other = rows_half[...] if group else dot_nn(p_far[quarter], s_next[...])
+            grad[group] = other + dot_nt((far, stq[1])[group], nat[...])
             for i in range(2):
                 for blk in range(2):
+                    here = grad[(group,) + spot(i, rows, blk * width, width)]
                     unit, slot = group * 4 + i * 2 + blk, slot_at(group, i, blk)
+                    tiles[unit] = shrink((outer, inner)[group][i * 2 + blk] - scale * here)
 
                     @pl.when(slot > 0)
                     def _(unit=unit, slot=slot):
@@ -514,7 +500,7 @@
     def edge(side, s_near, p_near, p_far):
         return run(
             kernel(edge_kernel, side), (coords, omega, turned, s_own, s_near, p_near, p_far, stq, own_half),
-            [SMEM] + [VMEM] * 8, (four, part), [slots, grad, mats_two], 20,
+            [SMEM] + [VMEM] * 8, (four, part), [slots, grad, mats_two, nat], 20,
         )
 
     outer_cross, to_cross = edge(0, s_chip, p_chip, far_cross)
@@ -527,7 +513,7 @@
     from_chip = permute(to_chip, chip)
     inner, own = run(
         kernel(inner_kernel), (coords, omega, s_cross, s_chip, stq, p_own, p_cross, p_chip, t_own),
-        [SMEM] + [VMEM] * 8, (four, full), [slots, grad, mats], 12,
+        [SMEM] + [VMEM] * 8, (four, full), [slots, grad, mats, nat], 12,
     )
     total = (own + from_cross.astype(f32) + from_chip.astype(f32)).astype(bf16)
     p_own = spread(total)
@@ -544,7 +530,7 @@
         kernel(last_kernel),
         (coords, outer_cross, outer_chip, inner, s_cross, s_chip, stq, rows_half, p_cross, p_chip, begun),
         [SMEM] + [VMEM] * 9 + [ANY], whole,
-        [slots, grad, pltpu.VMEM((8, rows, width), f32), pltpu.SemaphoreType.DMA((8,))],
+        [slots, pltpu.VMEM((2, both, wide), f32), nat, pltpu.VMEM((8, rows, width), f32), pltpu.SemaphoreType.DMA((8,))],
         12, out_specs=ANY, aliases={10: 0},
     )
 

time: 128 us -> 128 us (level)
  no operation moved by 1% of the time
where the time goes in v7:
time: 128 us; the launch traced here: 127 us
  starting transfers between devices  62 us (48%)
  Pallas kernels  24.9 us (19%)
  blocking collectives  21.7 us (17%)
  waiting for transfers between devices  17.9 us (14%)
    ppermute x11, starting transfers between devices, permute(): return lax.ppermute(x, 'tiles', pairs)  47 us
    all_to_all x2, blocking collectives, spread(): lax.all_to_all(jnp.broadcast_to(x[None], (parts,) + x.shape), 'samp', 0, 0)  21.7 us
    pallas_call x10, Pallas kernels, run(): call(body, in_specs, outs, scratch, units * unit, 4 << 20, aliases, out_s...  20.5 us
    ppermute x11, waiting for transfers between devices, permute(): return lax.ppermute(x, 'tiles', pairs)  13.9 us
    all_to_all x1, starting transfers between devices, shards(): s_own = lax.all_to_all(copies, 'samp', 0, 0).reshape(count, wide)  9.33 us
    all_to_all x1, starting transfers between devices, shards(): turned_parts = lax.all_to_all(pieces, 'samp', 0, 0)  5.66 us
    all_to_all x1, waiting for transfers between devices, shards(): s_own = lax.all_to_all(copies, 'samp', 0, 0).reshape(count, wide)  4 us
    pallas_call x1, Pallas kernels, shards(): call(cut_kernel, [HBM], pltpu.HBM((parts, others, rows, rows), bf16), [pl...  2.62 us
  transfers between devices with their start and end apart: 13, of which 5 were waited for; matrix products, arithmetic and copies ran while one was open for 0% of the time, Pallas kernels for 15%

profile of v7, /device:TPU:2, one launch (start us, length us, event | category | flops | bytes accessed | tf_op | source)
XLA Modules:
  0.0 127.0 jit_solution(8094287179584827114)
XLA Ops:
  1.8 9.3 %all-to-all-start.1 = ((bf16[4,64,1024]{2,1,0:T(8,128)(2,1)}), bf16[4,64,1024]{2,1,0:T(8,128)(2,1)S(1)}, u32[]{:S(2)}, u32[]{:S(2)}) async-start(bf16[4,64,1024]{2,1,0:T(8,128)(2,1)} %shard_map.38), calls=%async_computation.1 | async-start | bytes 1048576 | tf_op jit(solution)/shard_map/all_to_all | solution.py:449
  11.1 2.6 %shard_map.37 = bf16[4,8,128,128]{3,2,1,0:T(8,128)(2,1)} custom-call(f32[10,128,512]{2,1,0:T(8,128)} %omega.15), custom_call_target="tpu_custom_call" | custom-call | bytes 4194304 | tf_op jit(solution)/shard_map/pallas_call | solution.py:450
  13.7 4.0 %all-to-all-done.1 = bf16[4,64,1024]{2,1,0:T(8,128)(2,1)S(1)} async-done(((bf16[4,64,1024]{2,1,0:T(8,128)(2,1)}), bf16[4,64,1024]{2,1,0:T(8,128)(2,1)S(1)}, u32[]{:S(2)}, u32[]{:S(2)}) %all-to-all-start.1) | async-done | bytes 524320 | tf_op jit(solution)/shard_map/all_to_all | solution.py:449
  17.7 5.7 %all-to-all-start = ((bf16[4,8,128,128]{3,2,1,0:T(8,128)(2,1)}), bf16[4,8,128,128]{3,2,1,0:T(8,128)(2,1)}, u32[]{:S(2)}, u32[]{:S(2)}) async-start(bf16[4,8,128,128]{3,2,1,0:T(8,128)(2,1)} %shard_map.37), calls=%async_computation | async-start | bytes 2097152 | tf_op jit(solution)/shard_map/all_to_all | solution.py:458
  25.3 10.9 %collective-permute-start.1 = (bf16[256,1024]{1,0:T(8,128)(2,1)S(1)}, bf16[256,1024]{1,0:T(8,128)(2,1)}, u32[]{:S(2)}, u32[]{:S(2)}) collective-permute-start(bf16[256,1024]{1,0:T(8,128)(2,1)S(1)} %bitcast.2), channel_id=1, source_target_pairs={{0,508},{4,8},{8,4},{12,16},{16,12},{20,24},{24,20},{28,32},{32,28... | collective-permute-start | bytes 1572872 | tf_op jit(solution)/shard_map/ppermute | solution.py:439
  36.3 2.6 %shard_map.39 = (bf16[9,128,512]{2,1,0:T(8,128)(2,1)S(1)}, bf16[256,256]{1,0:T(8,128)(2,1)S(1)}) custom-call(s32[10,2]{1,0:T(8,128)S(1)} %copy.13.coords, f32[10,128,512]{2,1,0:T(8,128)S(1)} %copy-done, bf16[4,8,128,128]{3,2,1,0:T(8,128)(2,1)} %all-to-all-done.parts, bf16[256,1024]{1,0:T(8,128)(2,1)S(1)} %bitcast.3, ...), custom_call_target="tpu_custom_call" | custom-call | flops 268435456 | bytes 4194304 | tf_op jit(solution)/shard_map/pallas_call | solution.py:473
  38.9 4.2 %collective-permute-done.1.s_cross.s_near = bf16[256,1024]{1,0:T(8,128)(2,1)} collective-permute-done((bf16[256,1024]{1,0:T(8,128)(2,1)S(1)}, bf16[256,1024]{1,0:T(8,128)(2,1)}, u32[]{:S(2)}, u32[]{:S(2)}) %collective-permute-start.1) | collective-permute-done | bytes 524320 | tf_op jit(solution)/shard_map/ppermute | solution.py:439
  44.7 1.9 %collective-permute-start.3 = (bf16[256,256]{1,0:T(8,128)(2,1)S(1)}, bf16[256,256]{1,0:T(8,128)(2,1)S(1)}, u32[]{:S(2)}, u32[]{:S(2)}) collective-permute-start(bf16[256,256]{1,0:T(8,128)(2,1)S(1)} %shard_map.41), channel_id=1, source_target_pairs={{0,4},{4,0},{8,12},{12,8},{16,20},{20,16},{24,28},{28,24},{32,36},... | collective-permute-start | bytes 393224 | tf_op jit(solution)/shard_map/ppermute | solution.py:439
  46.6 6.8 %collective-permute-start.2 = (bf16[256,256]{1,0:T(8,128)(2,1)S(1)}, bf16[256,256]{1,0:T(8,128)(2,1)S(1)}, u32[]{:S(2)}, u32[]{:S(2)}) collective-permute-start(bf16[256,256]{1,0:T(8,128)(2,1)S(1)} %get-tuple-element.21), channel_id=1, source_target_pairs={{0,508},{4,8},{8,4},{12,16},{16,12},{20,24},{24,20},{28,32},{32,28... | collective-permute-start | bytes 393224 | tf_op jit(solution)/shard_map/ppermute | solution.py:439
  53.5 2.1 %shard_map.40 = (f32[256,256]{1,0:T(8,128)S(1)}, bf16[3,256,256]{2,1,0:T(8,128)(2,1)S(1)}) custom-call(s32[10,2]{1,0:T(8,128)S(1)} %copy.13.coords, f32[10,128,512]{2,1,0:T(8,128)S(1)} %copy-done, bf16[9,128,512]{2,1,0:T(8,128)(2,1)S(1)} %get-tuple-element.19.turned, bf16[256,1024]{1,0:T(8,128)(2,1)S(1)} %bitcast.5, ...), custom_call_target="tpu_custom_call" | custom-call | flops 268435456 | bytes 4194304 | tf_op jit(solution)/shard_map/pallas_call | solution.py:473
  56.3 11.2 %all_to_all.20.p_own = bf16[4,256,256]{2,1,0:T(8,128)(2,1)S(1)} all-to-all(bf16[4,256,256]{2,1,0:T(8,128)(2,1)S(1)} %broadcast_in_dim.4), channel_id=1, replica_groups=mesh['tiles'=128,'samp'=4] {'samp'}, dimensions={0} | all-to-all | bytes 1048576 | tf_op jit(solution)/shard_map/all_to_all | solution.py:442
  67.6 6.1 %collective-permute-start.6 = (bf16[4,256,256]{2,1,0:T(8,128)(2,1)S(1)}, bf16[4,256,256]{2,1,0:T(8,128)(2,1)S(1)}, u32[]{:S(2)}, u32[]{:S(2)}) collective-permute-start(bf16[4,256,256]{2,1,0:T(8,128)(2,1)S(1)} %all_to_all.20.p_own), channel_id=1, source_target_pairs={{0,508},{4,8},{8,4},{12,16},{16,12},{20,24},{24,20},{28,32},{32,28... | collective-permute-start | bytes 1572872 | tf_op jit(solution)/shard_map/ppermute | solution.py:439
  73.7 1.9 %collective-permute-start.4 = (bf16[4,256,256]{2,1,0:T(8,128)(2,1)S(1)}, bf16[4,256,256]{2,1,0:T(8,128)(2,1)S(1)}, u32[]{:S(2)}, u32[]{:S(2)}) collective-permute-start(bf16[4,256,256]{2,1,0:T(8,128)(2,1)S(1)} %all_to_all.20.p_own), channel_id=1, source_target_pairs={{0,4},{4,0},{8,12},{12,8},{16,20},{20,16},{24,28},{28,24},{32,36},... | collective-permute-start | bytes 1572872 | tf_op jit(solution)/shard_map/ppermute | solution.py:439
  75.6 2.7 %collective-permute-start.5 = (bf16[256,256]{1,0:T(8,128)(2,1)S(1)}, bf16[256,256]{1,0:T(8,128)(2,1)S(1)}, u32[]{:S(2)}, u32[]{:S(2)}) collective-permute-start(bf16[256,256]{1,0:T(8,128)(2,1)S(1)} %add_convert_fusion.1), channel_id=1, source_target_pairs={{0,508},{4,8},{8,4},{12,16},{16,12},{20,24},{24,20},{28,32},{32,28... | collective-permute-start | bytes 393224 | tf_op jit(solution)/shard_map/ppermute | solution.py:439
  78.7 2.7 %collective-permute-done.6.p_near.p_cross = bf16[4,256,256]{2,1,0:T(8,128)(2,1)S(1)} collective-permute-done((bf16[4,256,256]{2,1,0:T(8,128)(2,1)S(1)}, bf16[4,256,256]{2,1,0:T(8,128)(2,1)S(1)}, u32[]{:S(2)}, u32[]{:S(2)}) %collective-permute-start.6) | collective-permute-done | bytes 524320 | tf_op jit(solution)/shard_map/ppermute | solution.py:439
  81.4 2.5 %shard_map.44 = (f32[4,128,512]{2,1,0:T(8,128)S(1)}, bf16[256,256]{1,0:T(8,128)(2,1)S(1)}) custom-call(s32[10,2]{1,0:T(8,128)S(1)} %copy.13.coords, f32[10,128,512]{2,1,0:T(8,128)S(1)} %copy-done, bf16[9,128,512]{2,1,0:T(8,128)(2,1)S(1)} %get-tuple-element.19.turned, bf16[256,1024]{1,0:T(8,128)(2,1)S(1)} %bitcast.6, ...), custom_call_target="tpu_custom_call" | custom-call | flops 671088640 | bytes 4194304 | tf_op jit(solution)/shard_map/pallas_call | solution.py:473
  85.8 1.9 %shard_map.43 = (f32[4,128,512]{2,1,0:T(8,128)S(1)}, bf16[256,256]{1,0:T(8,128)(2,1)S(1)}) custom-call(s32[10,2]{1,0:T(8,128)S(1)} %copy.13.coords, f32[10,128,512]{2,1,0:T(8,128)S(1)} %copy-done, bf16[9,128,512]{2,1,0:T(8,128)(2,1)S(1)} %get-tuple-element.19.turned, bf16[256,1024]{1,0:T(8,128)(2,1)S(1)} %bitcast.7, ...), custom_call_target="tpu_custom_call" | custom-call | flops 671088640 | bytes 4194304 | tf_op jit(solution)/shard_map/pallas_call | solution.py:473
  87.8 6.1 %collective-permute-start.7 = (bf16[256,256]{1,0:T(8,128)(2,1)S(1)}, bf16[256,256]{1,0:T(8,128)(2,1)S(1)}, u32[]{:S(2)}, u32[]{:S(2)}) collective-permute-start(bf16[256,256]{1,0:T(8,128)(2,1)S(1)} %get-tuple-element.29), channel_id=1, source_target_pairs={{0,508},{4,8},{8,4},{12,16},{16,12},{20,24},{24,20},{28,32},{32,28... | collective-permute-start | bytes 393224 | tf_op jit(solution)/shard_map/ppermute | solution.py:439
  95.6 2.1 %shard_map.46 = (f32[4,128,512]{2,1,0:T(8,128)S(1)}, f32[256,256]{1,0:T(8,128)S(1)}) custom-call(s32[10,2]{1,0:T(8,128)S(1)} %copy.13.coords, f32[10,128,512]{2,1,0:T(8,128)S(1)} %copy-done, bf16[256,1024]{1,0:T(8,128)(2,1)} %collective-permute-done.1.s_cross.s_near, bf16[256,1024]{1,0:T(8,128)(2,1)} %collective-permute-done.s_chip.s_near, ...), custom_call_target="tpu_custom_call" | custom-call | flops 402653184 | bytes 4194304 | tf_op jit(solution)/shard_map/pallas_call | solution.py:473
  97.8 10.5 %all_to_all.21.p_own = bf16[4,256,256]{2,1,0:T(8,128)(2,1)S(1)} all-to-all(bf16[4,256,256]{2,1,0:T(8,128)(2,1)S(1)} %broadcast_in_dim.5), channel_id=1, replica_groups=mesh['tiles'=128,'samp'=4] {'samp'}, dimensions={0} | all-to-all | bytes 1048576 | tf_op jit(solution)/shard_map/all_to_all | solution.py:442
  110.2 4.7 %collective-permute-start.9 = (bf16[4,256,256]{2,1,0:T(8,128)(2,1)S(1)}, bf16[4,256,256]{2,1,0:T(8,128)(2,1)S(1)}, u32[]{:S(2)}, u32[]{:S(2)}) collective-permute-start(bf16[4,256,256]{2,1,0:T(8,128)(2,1)S(1)} %all_to_all.21.p_own), channel_id=1, source_target_pairs={{0,508},{4,8},{8,4},{12,16},{16,12},{20,24},{24,20},{28,32},{32,28... | collective-permute-start | bytes 1572872 | tf_op jit(solution)/shard_map/ppermute | solution.py:439
  114.9 2.8 %shard_map.47 = (f32[10,128,512]{2,1,0:T(8,128)}, f32[256,1024]{1,0:T(8,128)S(1)}) custom-call(s32[10,2]{1,0:T(8,128)S(1)} %copy.13.coords, f32[3,128,512]{2,1,0:T(8,128)S(1)} %get-tuple-element.27.held, bf16[256,1024]{1,0:T(8,128)(2,1)S(1)} %bitcast.9, bf16[256,1024]{1,0:T(8,128)(2,1)} %collective-permute-done.1.s_cross.s_near, ...), custom_call_target="tpu_custom_call" | custom-call | flops 402653184 | bytes 4194304 | tf_op jit(solution)/shard_map/pallas_call | solution.py:473
  117.6 6.4 %collective-permute-done.9.p_cross = bf16[4,256,256]{2,1,0:T(8,128)(2,1)S(1)} collective-permute-done((bf16[4,256,256]{2,1,0:T(8,128)(2,1)S(1)}, bf16[4,256,256]{2,1,0:T(8,128)(2,1)S(1)}, u32[]{:S(2)}, u32[]{:S(2)}) %collective-permute-start.9) | collective-permute-done | bytes 524320 | tf_op jit(solution)/shard_map/ppermute | solution.py:439
  124.0 3.0 %shard_map.48 = f32[10,128,512]{2,1,0:T(8,128)} custom-call(s32[10,2]{1,0:T(8,128)S(1)} %copy.13.coords, f32[4,128,512]{2,1,0:T(8,128)S(1)} %get-tuple-element.23.outer_cross, f32[4,128,512]{2,1,0:T(8,128)S(1)} %get-tuple-element.24.outer_chip, f32[4,128,512]{2,1,0:T(8,128)S(1)} %get-tuple-element.26.inner, ...), custom_call_target="tpu_custom_call", output_to_operand_aliasing={{}: (10, {})} | custom-call | flops 402653184 | bytes 4194304 | tf_op jit(solution)/shard_map/pallas_call | solution.py:473
  (25 shorter events, 12.0 us)
Async XLA Ops:
  1.8 16.0 %all-to-all-start.1 = ((bf16[4,64,1024]{2,1,0:T(8,128)(2,1)}), bf16[4,64,1024]{2,1,0:T(8,128)(2,1)S(1)}, u32[]{:S(2)}, u32[]{:S(2)}) async-start(bf16[4,64,1024]{2,1,0:T(8,128)(2,1)} %shard_map.38), calls=%async_computation.1 | async-start | bytes 1048576 | tf_op jit(solution)/shard_map/all_to_all | solution.py:449
  11.1 25.1 %copy-start.1 = (s32[10,2]{0,1:T(2,128)S(1)}, s32[10,2]{0,1:T(2,128)}, u32[]{:S(2)}) copy-start(s32[10,2]{0,1:T(2,128)} %param.5) | copy-start | bytes 244
  11.1 25.2 %copy-start = (f32[10,128,512]{2,1,0:T(8,128)S(1)}, f32[10,128,512]{2,1,0:T(8,128)}, u32[]{:S(2)}) copy-start(f32[10,128,512]{2,1,0:T(8,128)} %omega.15) | copy-start | bytes 7864324
  17.7 18.5 %all-to-all-start = ((bf16[4,8,128,128]{3,2,1,0:T(8,128)(2,1)}), bf16[4,8,128,128]{3,2,1,0:T(8,128)(2,1)}, u32[]{:S(2)}, u32[]{:S(2)}) async-start(bf16[4,8,128,128]{3,2,1,0:T(8,128)(2,1)} %shard_map.37), calls=%async_computation | async-start | bytes 2097152 | tf_op jit(solution)/shard_map/all_to_all | solution.py:458
  23.4 12.9 %collective-permute-start = (bf16[256,1024]{1,0:T(8,128)(2,1)S(1)}, bf16[256,1024]{1,0:T(8,128)(2,1)}, u32[]{:S(2)}, u32[]{:S(2)}) collective-permute-start(bf16[256,1024]{1,0:T(8,128)(2,1)S(1)} %bitcast.1), channel_id=1, source_target_pairs={{0,4},{4,0},{8,12},{12,8},{16,20},{20,16},{24,28},{28,24},{32,36},... | collective-permute-start | bytes 1572872 | tf_op jit(solution)/shard_map/ppermute | solution.py:439
  25.3 17.8 %collective-permute-start.1 = (bf16[256,1024]{1,0:T(8,128)(2,1)S(1)}, bf16[256,1024]{1,0:T(8,128)(2,1)}, u32[]{:S(2)}, u32[]{:S(2)}) collective-permute-start(bf16[256,1024]{1,0:T(8,128)(2,1)S(1)} %bitcast.2), channel_id=1, source_target_pairs={{0,508},{4,8},{8,4},{12,16},{16,12},{20,24},{24,20},{28,32},{32,28... | collective-permute-start | bytes 1572872 | tf_op jit(solution)/shard_map/ppermute | solution.py:439
  44.7 10.9 %collective-permute-start.3 = (bf16[256,256]{1,0:T(8,128)(2,1)S(1)}, bf16[256,256]{1,0:T(8,128)(2,1)S(1)}, u32[]{:S(2)}, u32[]{:S(2)}) collective-permute-start(bf16[256,256]{1,0:T(8,128)(2,1)S(1)} %shard_map.41), channel_id=1, source_target_pairs={{0,4},{4,0},{8,12},{12,8},{16,20},{20,16},{24,28},{28,24},{32,36},... | collective-permute-start | bytes 393224 | tf_op jit(solution)/shard_map/ppermute | solution.py:439
  46.6 9.6 %collective-permute-start.2 = (bf16[256,256]{1,0:T(8,128)(2,1)S(1)}, bf16[256,256]{1,0:T(8,128)(2,1)S(1)}, u32[]{:S(2)}, u32[]{:S(2)}) collective-permute-start(bf16[256,256]{1,0:T(8,128)(2,1)S(1)} %get-tuple-element.21), channel_id=1, source_target_pairs={{0,508},{4,8},{8,4},{12,16},{16,12},{20,24},{24,20},{28,32},{32,28... | collective-permute-start | bytes 393224 | tf_op jit(solution)/shard_map/ppermute | solution.py:439
  67.6 13.8 %collective-permute-start.6 = (bf16[4,256,256]{2,1,0:T(8,128)(2,1)S(1)}, bf16[4,256,256]{2,1,0:T(8,128)(2,1)S(1)}, u32[]{:S(2)}, u32[]{:S(2)}) collective-permute-start(bf16[4,256,256]{2,1,0:T(8,128)(2,1)S(1)} %all_to_all.20.p_own), channel_id=1, source_target_pairs={{0,508},{4,8},{8,4},{12,16},{16,12},{20,24},{24,20},{28,32},{32,28... | collective-permute-start | bytes 1572872 | tf_op jit(solution)/shard_map/ppermute | solution.py:439
  73.7 7.7 %collective-permute-start.4 = (bf16[4,256,256]{2,1,0:T(8,128)(2,1)S(1)}, bf16[4,256,256]{2,1,0:T(8,128)(2,1)S(1)}, u32[]{:S(2)}, u32[]{:S(2)}) collective-permute-start(bf16[4,256,256]{2,1,0:T(8,128)(2,1)S(1)} %all_to_all.20.p_own), channel_id=1, source_target_pairs={{0,4},{4,0},{8,12},{12,8},{16,20},{20,16},{24,28},{28,24},{32,36},... | collective-permute-start | bytes 1572872 | tf_op jit(solution)/shard_map/ppermute | solution.py:439
  75.6 10.2 %collective-permute-start.5 = (bf16[256,256]{1,0:T(8,128)(2,1)S(1)}, bf16[256,256]{1,0:T(8,128)(2,1)S(1)}, u32[]{:S(2)}, u32[]{:S(2)}) collective-permute-start(bf16[256,256]{1,0:T(8,128)(2,1)S(1)} %add_convert_fusion.1), channel_id=1, source_target_pairs={{0,508},{4,8},{8,4},{12,16},{16,12},{20,24},{24,20},{28,32},{32,28... | collective-permute-start | bytes 393224 | tf_op jit(solution)/shard_map/ppermute | solution.py:439
  83.9 13.8 %collective-permute-start.8 = (bf16[256,256]{1,0:T(8,128)(2,1)S(1)}, bf16[256,256]{1,0:T(8,128)(2,1)S(1)}, u32[]{:S(2)}, u32[]{:S(2)}) collective-permute-start(bf16[256,256]{1,0:T(8,128)(2,1)S(1)} %get-tuple-element.30), channel_id=1, source_target_pairs={{0,4},{4,0},{8,12},{12,8},{16,20},{20,16},{24,28},{28,24},{32,36},... | collective-permute-start | bytes 393224 | tf_op jit(solution)/shard_map/ppermute | solution.py:439
  87.8 9.9 %collective-permute-start.7 = (bf16[256,256]{1,0:T(8,128)(2,1)S(1)}, bf16[256,256]{1,0:T(8,128)(2,1)S(1)}, u32[]{:S(2)}, u32[]{:S(2)}) collective-permute-start(bf16[256,256]{1,0:T(8,128)(2,1)S(1)} %get-tuple-element.29), channel_id=1, source_target_pairs={{0,508},{4,8},{8,4},{12,16},{16,12},{20,24},{24,20},{28,32},{32,28... | collective-permute-start | bytes 393224 | tf_op jit(solution)/shard_map/ppermute | solution.py:439
  108.3 9.4 %collective-permute-start.10 = (bf16[4,256,256]{2,1,0:T(8,128)(2,1)S(1)}, bf16[4,256,256]{2,1,0:T(8,128)(2,1)S(1)}, u32[]{:S(2)}, u32[]{:S(2)}) collective-permute-start(bf16[4,256,256]{2,1,0:T(8,128)(2,1)S(1)} %all_to_all.21.p_own), channel_id=1, source_target_pairs={{0,4},{4,0},{8,12},{12,8},{16,20},{20,16},{24,28},{28,24},{32,36},... | collective-permute-start | bytes 1572872 | tf_op jit(solution)/shard_map/ppermute | solution.py:439
  110.2 13.8 %collective-permute-start.9 = (bf16[4,256,256]{2,1,0:T(8,128)(2,1)S(1)}, bf16[4,256,256]{2,1,0:T(8,128)(2,1)S(1)}, u32[]{:S(2)}, u32[]{:S(2)}) collective-permute-start(bf16[4,256,256]{2,1,0:T(8,128)(2,1)S(1)} %all_to_all.21.p_own), channel_id=1, source_target_pairs={{0,508},{4,8},{8,4},{12,16},{16,12},{20,24},{24,20},{28,32},{32,28... | collective-permute-start | bytes 1572872 | tf_op jit(solution)/shard_map/ppermute | solution.py:439

commit v8 on v7

--- a/solution.py
+++ b/solution.py
@@ -136,7 +136,9 @@
     return total
 
 
-def first_cross_kernel(blocks, coords, omega, parts, s_own, s_chip, turned, out, slot_of, mats, sems):
+def first_cross_kernel(blocks, coords, omega, parts, s_own, s_in, turned, out, s_chip, slot_of, mats, sems, s_sem):
+    window = pltpu.make_async_copy(s_in, s_chip, s_sem)
+    window.start()
     rows, _ = omega.shape[1:]
     count = parts.shape[0]
     find_slots(blocks, coords, slot_of)
@@ -166,6 +168,8 @@
         def _(unit=unit):
             turned[unit] = jnp.zeros_like(turned[unit])
 
+    window.wait()
+
     @pl.when(is_even())
     def _():
         out[...] = first_rows(slot_of, omega, 0, s_chip, mats).astype(bf16)
@@ -183,8 +187,11 @@
         out[...] = first_cols(turned, s_chip, s_own).astype(bf16)
 
 
-def first_chip_kernel(blocks, coords, omega, turned, s_own, s_cross, out, slot_of, mats):
-    find_slots(blocks, coords, slot_of)
+def first_chip_kernel(blocks, coords, omega, turned, s_own, s_in, out, s_cross, slot_of, mats, s_sem):
+    window = pltpu.make_async_copy(s_in, s_cross, s_sem)
+    window.start()
+    find_slots(blocks, coords, slot_of)
+    window.wait()
 
     def cols():
         out[...] = first_cols(turned, s_cross, s_own).astype(bf16)
@@ -475,15 +482,15 @@
     def kernel(body, *extra):
         return functools.partial(body, blocks, *extra)
 
-    turned, to_cross = run(
-        kernel(first_cross_kernel), (coords, omega, turned_parts, s_own, s_chip), [SMEM, VMEM, ANY, VMEM, VMEM],
-        (shape((OWN_PAIR + 1, rows, width), bf16), part),
-        [slots, mats, pltpu.SemaphoreType.DMA((OWN_PAIR + 1, parts))], 8,
+    turned, to_cross, s_chip = run(
+        kernel(first_cross_kernel), (coords, omega, turned_parts, s_own, s_chip), [SMEM, VMEM, ANY, VMEM, ANY],
+        (shape((OWN_PAIR + 1, rows, width), bf16), part, shape((count, wide), bf16)),
+        [slots, mats, pltpu.SemaphoreType.DMA((OWN_PAIR + 1, parts)), pltpu.SemaphoreType.DMA], 8,
     )
     from_cross = permute(to_cross, cross)
-    to_chip = run(
-        kernel(first_chip_kernel), (coords, omega, turned, s_own, s_cross), [SMEM] + [VMEM] * 4,
-        part, [slots, mats], 8,
+    to_chip, s_cross = run(
+        kernel(first_chip_kernel), (coords, omega, turned, s_own, s_cross), [SMEM] + [VMEM] * 3 + [ANY],
+        (part, shape((count, wide), bf16)), [slots, mats, pltpu.SemaphoreType.DMA], 8,
     )
     from_chip = permute(to_chip, chip)
     own, stq = run(

time: 128 us -> 127 us (level)
  Pallas kernels: 24.9 us -> 22.4 us
    pallas_call x10, Pallas kernels: 20.5 us -> 18 us  [run(): call(body, in_specs, outs, scratch, units * unit, 4 << 20, aliases, out_s...]
  transfers between devices with their start and end apart: 13 -> 13, of which waited for: 5 -> 6; matrix products, arithmetic and copies ran while one was open for 0% -> 0% of each run, Pallas kernels for 15% -> 13%
where the time goes in v8:
time: 127 us; the launch traced here: 126 us
  starting transfers between devices  62.2 us (49%)
  Pallas kernels  22.4 us (18%)
  blocking collectives  21.7 us (17%)
  waiting for transfers between devices  19.1 us (15%)
    ppermute x11, starting transfers between devices, permute(): return lax.ppermute(x, 'tiles', pairs)  47.2 us
    all_to_all x2, blocking collectives, spread(): lax.all_to_all(jnp.broadcast_to(x[None], (parts,) + x.shape), 'samp', 0, 0)  21.7 us
    pallas_call x10, Pallas kernels, run(): call(body, in_specs, outs, scratch, units * unit, 4 << 20, aliases, out_s...  18 us
    ppermute x11, waiting for transfers between devices, permute(): return lax.ppermute(x, 'tiles', pairs)  15.1 us
    all_to_all x1, starting transfers between devices, shards(): s_own = lax.all_to_all(copies, 'samp', 0, 0).reshape(count, wide)  9.33 us
    all_to_all x1, starting transfers between devices, shards(): turned_parts = lax.all_to_all(pieces, 'samp', 0, 0)  5.67 us
    all_to_all x1, waiting for transfers between devices, shards(): s_own = lax.all_to_all(copies, 'samp', 0, 0).reshape(count, wide)  4 us
    pallas_call x1, Pallas kernels, shards(): call(cut_kernel, [HBM], pltpu.HBM((parts, others, rows, rows), bf16), [pl...  2.62 us
  transfers between devices with their start and end apart: 13, of which 6 were waited for; matrix products, arithmetic and copies ran while one was open for 0% of the time, Pallas kernels for 13%

profile of v8, /device:TPU:2, one launch (start us, length us, event | category | flops | bytes accessed | tf_op | source)
XLA Modules:
  0.0 125.9 jit_solution(5139759307927252913)
XLA Ops:
  1.8 9.3 %all-to-all-start.1 = ((bf16[4,64,1024]{2,1,0:T(8,128)(2,1)}), bf16[4,64,1024]{2,1,0:T(8,128)(2,1)S(1)}, u32[]{:S(2)}, u32[]{:S(2)}) async-start(bf16[4,64,1024]{2,1,0:T(8,128)(2,1)} %shard_map.38), calls=%async_computation.1 | async-start | bytes 1048576 | tf_op jit(solution)/shard_map/all_to_all | solution.py:456
  11.1 2.6 %shard_map.37 = bf16[4,8,128,128]{3,2,1,0:T(8,128)(2,1)} custom-call(f32[10,128,512]{2,1,0:T(8,128)} %omega.15), custom_call_target="tpu_custom_call" | custom-call | bytes 4194304 | tf_op jit(solution)/shard_map/pallas_call | solution.py:457
  13.7 4.0 %all-to-all-done.1 = bf16[4,64,1024]{2,1,0:T(8,128)(2,1)S(1)} async-done(((bf16[4,64,1024]{2,1,0:T(8,128)(2,1)}), bf16[4,64,1024]{2,1,0:T(8,128)(2,1)S(1)}, u32[]{:S(2)}, u32[]{:S(2)}) %all-to-all-start.1) | async-done | bytes 524320 | tf_op jit(solution)/shard_map/all_to_all | solution.py:456
  17.7 5.7 %all-to-all-start = ((bf16[4,8,128,128]{3,2,1,0:T(8,128)(2,1)}), bf16[4,8,128,128]{3,2,1,0:T(8,128)(2,1)}, u32[]{:S(2)}, u32[]{:S(2)}) async-start(bf16[4,8,128,128]{3,2,1,0:T(8,128)(2,1)} %shard_map.37), calls=%async_computation | async-start | bytes 2097152 | tf_op jit(solution)/shard_map/all_to_all | solution.py:465
  23.4 1.9 %collective-permute-start = (bf16[256,1024]{1,0:T(8,128)(2,1)S(1)}, bf16[256,1024]{1,0:T(8,128)(2,1)}, u32[]{:S(2)}, u32[]{:S(2)}) collective-permute-start(bf16[256,1024]{1,0:T(8,128)(2,1)S(1)} %bitcast.1), channel_id=1, source_target_pairs={{0,4},{4,0},{8,12},{12,8},{16,20},{20,16},{24,28},{28,24},{32,36},... | collective-permute-start | bytes 1572872 | tf_op jit(solution)/shard_map/ppermute | solution.py:446
  25.3 10.9 %collective-permute-start.1 = (bf16[256,1024]{1,0:T(8,128)(2,1)S(1)}, bf16[256,1024]{1,0:T(8,128)(2,1)}, u32[]{:S(2)}, u32[]{:S(2)}) collective-permute-start(bf16[256,1024]{1,0:T(8,128)(2,1)S(1)} %bitcast.2), channel_id=1, source_target_pairs={{0,508},{4,8},{8,4},{12,16},{16,12},{20,24},{24,20},{28,32},{32,28... | collective-permute-start | bytes 1572872 | tf_op jit(solution)/shard_map/ppermute | solution.py:446
  36.3 2.5 %shard_map.39 = (bf16[9,128,512]{2,1,0:T(8,128)(2,1)S(1)}, bf16[256,256]{1,0:T(8,128)(2,1)S(1)}, bf16[256,1024]{1,0:T(8,128)(2,1)S(1)}) custom-call(s32[10,2]{1,0:T(8,128)S(1)} %copy.13.coords, f32[10,128,512]{2,1,0:T(8,128)S(1)} %copy-done, bf16[4,8,128,128]{3,2,1,0:T(8,128)(2,1)} %all-to-all-done.parts, bf16[256,1024]{1,0:T(8,128)(2,1)S(1)} %bitcast.3, ...), custom_call_target="tpu_custom_call" | custom-call | flops 268435456 | bytes 4194304 | tf_op jit(solution)/shard_map/pallas_call | solution.py:480
  38.8 4.3 %collective-permute-done.1.s_in = bf16[256,1024]{1,0:T(8,128)(2,1)} collective-permute-done((bf16[256,1024]{1,0:T(8,128)(2,1)S(1)}, bf16[256,1024]{1,0:T(8,128)(2,1)}, u32[]{:S(2)}, u32[]{:S(2)}) %collective-permute-start.1) | collective-permute-done | bytes 524320 | tf_op jit(solution)/shard_map/ppermute | solution.py:446
  43.1 2.2 %shard_map.40 = (bf16[256,256]{1,0:T(8,128)(2,1)S(1)}, bf16[256,1024]{1,0:T(8,128)(2,1)S(1)}) custom-call(s32[10,2]{1,0:T(8,128)S(1)} %copy.13.coords, f32[10,128,512]{2,1,0:T(8,128)S(1)} %copy-done, bf16[9,128,512]{2,1,0:T(8,128)(2,1)S(1)} %get-tuple-element.22.turned, bf16[256,1024]{1,0:T(8,128)(2,1)S(1)} %bitcast.4, ...), custom_call_target="tpu_custom_call" | custom-call | flops 268435456 | bytes 4194304 | tf_op jit(solution)/shard_map/pallas_call | solution.py:480
  45.3 1.9 %collective-permute-start.3 = (bf16[256,256]{1,0:T(8,128)(2,1)S(1)}, bf16[256,256]{1,0:T(8,128)(2,1)S(1)}, u32[]{:S(2)}, u32[]{:S(2)}) collective-permute-start(bf16[256,256]{1,0:T(8,128)(2,1)S(1)} %get-tuple-element.27), channel_id=1, source_target_pairs={{0,4},{4,0},{8,12},{12,8},{16,20},{20,16},{24,28},{28,24},{32,36},... | collective-permute-start | bytes 393224 | tf_op jit(solution)/shard_map/ppermute | solution.py:446
  47.3 6.8 %collective-permute-start.2 = (bf16[256,256]{1,0:T(8,128)(2,1)S(1)}, bf16[256,256]{1,0:T(8,128)(2,1)S(1)}, u32[]{:S(2)}, u32[]{:S(2)}) collective-permute-start(bf16[256,256]{1,0:T(8,128)(2,1)S(1)} %get-tuple-element.26), channel_id=1, source_target_pairs={{0,508},{4,8},{8,4},{12,16},{16,12},{20,24},{24,20},{28,32},{32,28... | collective-permute-start | bytes 393224 | tf_op jit(solution)/shard_map/ppermute | solution.py:446
  57.0 11.2 %all_to_all.20.p_own = bf16[4,256,256]{2,1,0:T(8,128)(2,1)S(1)} all-to-all(bf16[4,256,256]{2,1,0:T(8,128)(2,1)S(1)} %broadcast_in_dim.4), channel_id=1, replica_groups=mesh['tiles'=128,'samp'=4] {'samp'}, dimensions={0} | all-to-all | bytes 1048576 | tf_op jit(solution)/shard_map/all_to_all | solution.py:449
  68.2 6.1 %collective-permute-start.6 = (bf16[4,256,256]{2,1,0:T(8,128)(2,1)S(1)}, bf16[4,256,256]{2,1,0:T(8,128)(2,1)S(1)}, u32[]{:S(2)}, u32[]{:S(2)}) collective-permute-start(bf16[4,256,256]{2,1,0:T(8,128)(2,1)S(1)} %all_to_all.20.p_own), channel_id=1, source_target_pairs={{0,508},{4,8},{8,4},{12,16},{16,12},{20,24},{24,20},{28,32},{32,28... | collective-permute-start | bytes 1572872 | tf_op jit(solution)/shard_map/ppermute | solution.py:446
  74.3 1.9 %collective-permute-start.4 = (bf16[4,256,256]{2,1,0:T(8,128)(2,1)S(1)}, bf16[4,256,256]{2,1,0:T(8,128)(2,1)S(1)}, u32[]{:S(2)}, u32[]{:S(2)}) collective-permute-start(bf16[4,256,256]{2,1,0:T(8,128)(2,1)S(1)} %all_to_all.20.p_own), channel_id=1, source_target_pairs={{0,4},{4,0},{8,12},{12,8},{16,20},{20,16},{24,28},{28,24},{32,36},... | collective-permute-start | bytes 1572872 | tf_op jit(solution)/shard_map/ppermute | solution.py:446
  76.2 2.8 %collective-permute-start.5 = (bf16[256,256]{1,0:T(8,128)(2,1)S(1)}, bf16[256,256]{1,0:T(8,128)(2,1)S(1)}, u32[]{:S(2)}, u32[]{:S(2)}) collective-permute-start(bf16[256,256]{1,0:T(8,128)(2,1)S(1)} %add_convert_fusion.1), channel_id=1, source_target_pairs={{0,508},{4,8},{8,4},{12,16},{16,12},{20,24},{24,20},{28,32},{32,28... | collective-permute-start | bytes 393224 | tf_op jit(solution)/shard_map/ppermute | solution.py:446
  79.3 2.7 %collective-permute-done.6.p_near.p_cross = bf16[4,256,256]{2,1,0:T(8,128)(2,1)S(1)} collective-permute-done((bf16[4,256,256]{2,1,0:T(8,128)(2,1)S(1)}, bf16[4,256,256]{2,1,0:T(8,128)(2,1)S(1)}, u32[]{:S(2)}, u32[]{:S(2)}) %collective-permute-start.6) | collective-permute-done | bytes 524320 | tf_op jit(solution)/shard_map/ppermute | solution.py:446
  82.0 2.1 %shard_map.44 = (f32[4,128,512]{2,1,0:T(8,128)S(1)}, bf16[256,256]{1,0:T(8,128)(2,1)S(1)}) custom-call(s32[10,2]{1,0:T(8,128)S(1)} %copy.13.coords, f32[10,128,512]{2,1,0:T(8,128)S(1)} %copy-done, bf16[9,128,512]{2,1,0:T(8,128)(2,1)S(1)} %get-tuple-element.22.turned, bf16[256,1024]{1,0:T(8,128)(2,1)S(1)} %bitcast.6, ...), custom_call_target="tpu_custom_call" | custom-call | flops 671088640 | bytes 4194304 | tf_op jit(solution)/shard_map/pallas_call | solution.py:480
  84.1 1.9 %collective-permute-start.8 = (bf16[256,256]{1,0:T(8,128)(2,1)S(1)}, bf16[256,256]{1,0:T(8,128)(2,1)S(1)}, u32[]{:S(2)}, u32[]{:S(2)}) collective-permute-start(bf16[256,256]{1,0:T(8,128)(2,1)S(1)} %get-tuple-element.36), channel_id=1, source_target_pairs={{0,4},{4,0},{8,12},{12,8},{16,20},{20,16},{24,28},{28,24},{32,36},... | collective-permute-start | bytes 393224 | tf_op jit(solution)/shard_map/ppermute | solution.py:446
  87.6 6.1 %collective-permute-start.7 = (bf16[256,256]{1,0:T(8,128)(2,1)S(1)}, bf16[256,256]{1,0:T(8,128)(2,1)S(1)}, u32[]{:S(2)}, u32[]{:S(2)}) collective-permute-start(bf16[256,256]{1,0:T(8,128)(2,1)S(1)} %get-tuple-element.35), channel_id=1, source_target_pairs={{0,508},{4,8},{8,4},{12,16},{16,12},{20,24},{24,20},{28,32},{32,28... | collective-permute-start | bytes 393224 | tf_op jit(solution)/shard_map/ppermute | solution.py:446
  97.3 10.5 %all_to_all.21.p_own = bf16[4,256,256]{2,1,0:T(8,128)(2,1)S(1)} all-to-all(bf16[4,256,256]{2,1,0:T(8,128)(2,1)S(1)} %broadcast_in_dim.5), channel_id=1, replica_groups=mesh['tiles'=128,'samp'=4] {'samp'}, dimensions={0} | all-to-all | bytes 1048576 | tf_op jit(solution)/shard_map/all_to_all | solution.py:449
  109.7 5.0 %collective-permute-start.9 = (bf16[4,256,256]{2,1,0:T(8,128)(2,1)S(1)}, bf16[4,256,256]{2,1,0:T(8,128)(2,1)S(1)}, u32[]{:S(2)}, u32[]{:S(2)}) collective-permute-start(bf16[4,256,256]{2,1,0:T(8,128)(2,1)S(1)} %all_to_all.21.p_own), channel_id=1, source_target_pairs={{0,508},{4,8},{8,4},{12,16},{16,12},{20,24},{24,20},{28,32},{32,28... | collective-permute-start | bytes 1572872 | tf_op jit(solution)/shard_map/ppermute | solution.py:446
  114.7 2.2 %shard_map.47 = (f32[10,128,512]{2,1,0:T(8,128)}, f32[256,1024]{1,0:T(8,128)S(1)}) custom-call(s32[10,2]{1,0:T(8,128)S(1)} %copy.13.coords, f32[3,128,512]{2,1,0:T(8,128)S(1)} %get-tuple-element.33.held, bf16[256,1024]{1,0:T(8,128)(2,1)S(1)} %bitcast.9, bf16[256,1024]{1,0:T(8,128)(2,1)S(1)} %get-tuple-element.24.s_cross.s_near, ...), custom_call_target="tpu_custom_call" | custom-call | flops 402653184 | bytes 4194304 | tf_op jit(solution)/shard_map/pallas_call | solution.py:480
  116.9 6.6 %collective-permute-done.9.p_cross = bf16[4,256,256]{2,1,0:T(8,128)(2,1)S(1)} collective-permute-done((bf16[4,256,256]{2,1,0:T(8,128)(2,1)S(1)}, bf16[4,256,256]{2,1,0:T(8,128)(2,1)S(1)}, u32[]{:S(2)}, u32[]{:S(2)}) %collective-permute-start.9) | collective-permute-done | bytes 524320 | tf_op jit(solution)/shard_map/ppermute | solution.py:446
  123.6 2.4 %shard_map.48 = f32[10,128,512]{2,1,0:T(8,128)} custom-call(s32[10,2]{1,0:T(8,128)S(1)} %copy.13.coords, f32[4,128,512]{2,1,0:T(8,128)S(1)} %get-tuple-element.29.outer_cross, f32[4,128,512]{2,1,0:T(8,128)S(1)} %get-tuple-element.30.outer_chip, f32[4,128,512]{2,1,0:T(8,128)S(1)} %get-tuple-element.32.inner, ...), custom_call_target="tpu_custom_call", output_to_operand_aliasing={{}: (10, {})} | custom-call | flops 402653184 | bytes 4194304 | tf_op jit(solution)/shard_map/pallas_call | solution.py:480
  (25 shorter events, 12.0 us)
Async XLA Ops:
  1.8 16.0 %all-to-all-start.1 = ((bf16[4,64,1024]{2,1,0:T(8,128)(2,1)}), bf16[4,64,1024]{2,1,0:T(8,128)(2,1)S(1)}, u32[]{:S(2)}, u32[]{:S(2)}) async-start(bf16[4,64,1024]{2,1,0:T(8,128)(2,1)} %shard_map.38), calls=%async_computation.1 | async-start | bytes 1048576 | tf_op jit(solution)/shard_map/all_to_all | solution.py:456
  11.1 25.1 %copy-start.1 = (s32[10,2]{0,1:T(2,128)S(1)}, s32[10,2]{0,1:T(2,128)}, u32[]{:S(2)}) copy-start(s32[10,2]{0,1:T(2,128)} %param.5) | copy-start | bytes 244
  11.1 25.2 %copy-start = (f32[10,128,512]{2,1,0:T(8,128)S(1)}, f32[10,128,512]{2,1,0:T(8,128)}, u32[]{:S(2)}) copy-start(f32[10,128,512]{2,1,0:T(8,128)} %omega.15) | copy-start | bytes 7864324
  17.7 18.6 %all-to-all-start = ((bf16[4,8,128,128]{3,2,1,0:T(8,128)(2,1)}), bf16[4,8,128,128]{3,2,1,0:T(8,128)(2,1)}, u32[]{:S(2)}, u32[]{:S(2)}) async-start(bf16[4,8,128,128]{3,2,1,0:T(8,128)(2,1)} %shard_map.37), calls=%async_computation | async-start | bytes 2097152 | tf_op jit(solution)/shard_map/all_to_all | solution.py:465
  23.4 12.9 %collective-permute-start = (bf16[256,1024]{1,0:T(8,128)(2,1)S(1)}, bf16[256,1024]{1,0:T(8,128)(2,1)}, u32[]{:S(2)}, u32[]{:S(2)}) collective-permute-start(bf16[256,1024]{1,0:T(8,128)(2,1)S(1)} %bitcast.1), channel_id=1, source_target_pairs={{0,4},{4,0},{8,12},{12,8},{16,20},{20,16},{24,28},{28,24},{32,36},... | collective-permute-start | bytes 1572872 | tf_op jit(solution)/shard_map/ppermute | solution.py:446
  25.3 17.8 %collective-permute-start.1 = (bf16[256,1024]{1,0:T(8,128)(2,1)S(1)}, bf16[256,1024]{1,0:T(8,128)(2,1)}, u32[]{:S(2)}, u32[]{:S(2)}) collective-permute-start(bf16[256,1024]{1,0:T(8,128)(2,1)S(1)} %bitcast.2), channel_id=1, source_target_pairs={{0,508},{4,8},{8,4},{12,16},{16,12},{20,24},{24,20},{28,32},{32,28... | collective-permute-start | bytes 1572872 | tf_op jit(solution)/shard_map/ppermute | solution.py:446
  45.3 10.3 %collective-permute-start.3 = (bf16[256,256]{1,0:T(8,128)(2,1)S(1)}, bf16[256,256]{1,0:T(8,128)(2,1)S(1)}, u32[]{:S(2)}, u32[]{:S(2)}) collective-permute-start(bf16[256,256]{1,0:T(8,128)(2,1)S(1)} %get-tuple-element.27), channel_id=1, source_target_pairs={{0,4},{4,0},{8,12},{12,8},{16,20},{20,16},{24,28},{28,24},{32,36},... | collective-permute-start | bytes 393224 | tf_op jit(solution)/shard_map/ppermute | solution.py:446
  47.3 9.6 %collective-permute-start.2 = (bf16[256,256]{1,0:T(8,128)(2,1)S(1)}, bf16[256,256]{1,0:T(8,128)(2,1)S(1)}, u32[]{:S(2)}, u32[]{:S(2)}) collective-permute-start(bf16[256,256]{1,0:T(8,128)(2,1)S(1)} %get-tuple-element.26), channel_id=1, source_target_pairs={{0,508},{4,8},{8,4},{12,16},{16,12},{20,24},{24,20},{28,32},{32,28... | collective-permute-start | bytes 393224 | tf_op jit(solution)/shard_map/ppermute | solution.py:446
  68.2 13.8 %collective-permute-start.6 = (bf16[4,256,256]{2,1,0:T(8,128)(2,1)S(1)}, bf16[4,256,256]{2,1,0:T(8,128)(2,1)S(1)}, u32[]{:S(2)}, u32[]{:S(2)}) collective-permute-start(bf16[4,256,256]{2,1,0:T(8,128)(2,1)S(1)} %all_to_all.20.p_own), channel_id=1, source_target_pairs={{0,508},{4,8},{8,4},{12,16},{16,12},{20,24},{24,20},{28,32},{32,28... | collective-permute-start | bytes 1572872 | tf_op jit(solution)/shard_map/ppermute | solution.py:446
  74.3 7.7 %collective-permute-start.4 = (bf16[4,256,256]{2,1,0:T(8,128)(2,1)S(1)}, bf16[4,256,256]{2,1,0:T(8,128)(2,1)S(1)}, u32[]{:S(2)}, u32[]{:S(2)}) collective-permute-start(bf16[4,256,256]{2,1,0:T(8,128)(2,1)S(1)} %all_to_all.20.p_own), channel_id=1, source_target_pairs={{0,4},{4,0},{8,12},{12,8},{16,20},{20,16},{24,28},{28,24},{32,36},... | collective-permute-start | bytes 1572872 | tf_op jit(solution)/shard_map/ppermute | solution.py:446
  76.2 9.8 %collective-permute-start.5 = (bf16[256,256]{1,0:T(8,128)(2,1)S(1)}, bf16[256,256]{1,0:T(8,128)(2,1)S(1)}, u32[]{:S(2)}, u32[]{:S(2)}) collective-permute-start(bf16[256,256]{1,0:T(8,128)(2,1)S(1)} %add_convert_fusion.1), channel_id=1, source_target_pairs={{0,508},{4,8},{8,4},{12,16},{16,12},{20,24},{24,20},{28,32},{32,28... | collective-permute-start | bytes 393224 | tf_op jit(solution)/shard_map/ppermute | solution.py:446
  84.1 12.8 %collective-permute-start.8 = (bf16[256,256]{1,0:T(8,128)(2,1)S(1)}, bf16[256,256]{1,0:T(8,128)(2,1)S(1)}, u32[]{:S(2)}, u32[]{:S(2)}) collective-permute-start(bf16[256,256]{1,0:T(8,128)(2,1)S(1)} %get-tuple-element.36), channel_id=1, source_target_pairs={{0,4},{4,0},{8,12},{12,8},{16,20},{20,16},{24,28},{28,24},{32,36},... | collective-permute-start | bytes 393224 | tf_op jit(solution)/shard_map/ppermute | solution.py:446
  87.6 9.6 %collective-permute-start.7 = (bf16[256,256]{1,0:T(8,128)(2,1)S(1)}, bf16[256,256]{1,0:T(8,128)(2,1)S(1)}, u32[]{:S(2)}, u32[]{:S(2)}) collective-permute-start(bf16[256,256]{1,0:T(8,128)(2,1)S(1)} %get-tuple-element.35), channel_id=1, source_target_pairs={{0,508},{4,8},{8,4},{12,16},{16,12},{20,24},{24,20},{28,32},{32,28... | collective-permute-start | bytes 393224 | tf_op jit(solution)/shard_map/ppermute | solution.py:446
  107.8 9.1 %collective-permute-start.10 = (bf16[4,256,256]{2,1,0:T(8,128)(2,1)S(1)}, bf16[4,256,256]{2,1,0:T(8,128)(2,1)S(1)}, u32[]{:S(2)}, u32[]{:S(2)}) collective-permute-start(bf16[4,256,256]{2,1,0:T(8,128)(2,1)S(1)} %all_to_all.21.p_own), channel_id=1, source_target_pairs={{0,4},{4,0},{8,12},{12,8},{16,20},{20,16},{24,28},{28,24},{32,36},... | collective-permute-start | bytes 1572872 | tf_op jit(solution)/shard_map/ppermute | solution.py:446
  109.7 13.8 %collective-permute-start.9 = (bf16[4,256,256]{2,1,0:T(8,128)(2,1)S(1)}, bf16[4,256,256]{2,1,0:T(8,128)(2,1)S(1)}, u32[]{:S(2)}, u32[]{:S(2)}) collective-permute-start(bf16[4,256,256]{2,1,0:T(8,128)(2,1)S(1)} %all_to_all.21.p_own), channel_id=1, source_target_pairs={{0,508},{4,8},{8,4},{12,16},{16,12},{20,24},{24,20},{28,32},{32,28... | collective-permute-start | bytes 1572872 | tf_op jit(solution)/shard_map/ppermute | solution.py:446

commit v9 on v8

--- a/solution.py
+++ b/solution.py
@@ -187,10 +187,9 @@
         out[...] = first_cols(turned, s_chip, s_own).astype(bf16)
 
 
-def first_chip_kernel(blocks, coords, omega, turned, s_own, s_in, out, s_cross, slot_of, mats, s_sem):
+def first_chip_kernel(blocks, slot_of, omega, turned, s_own, s_in, out, s_cross, mats, s_sem):
     window = pltpu.make_async_copy(s_in, s_cross, s_sem)
     window.start()
-    find_slots(blocks, coords, slot_of)
     window.wait()
 
     def cols():
@@ -202,10 +201,9 @@
     choose(True, cols, rows)
 
 
-def first_own_kernel(blocks, coords, omega, turned, s_own, s_cross, s_chip, own, stq, slot_of, mats):
+def first_own_kernel(blocks, slot_of, omega, turned, s_own, s_cross, s_chip, own, stq, mats):
     rows, width = omega.shape[1:]
     quarter = lax.axis_index("samp")
-    find_slots(blocks, coords, slot_of)
     mats[:rows, :width] = omega[0].astype(bf16)
     mats[rows:, width:] = omega[1].astype(bf16)
     slot = slot_of[OWN_PAIR]
@@ -254,14 +252,13 @@
 
 
 def edge_kernel(
-    blocks, far_side, coords, omega, turned, s_own, s_near, p_near, p_far, stq, own_half,
-    tiles, out, slot_of, grad, mats, nat,
+    blocks, far_side, slot_of, omega, turned, s_own, s_near, p_near, p_far, stq, own_half,
+    tiles, out, grad, mats, nat,
 ):
     rows, width = omega.shape[1:]
     wide = s_own.shape[1]
     quarter = lax.axis_index("samp")
     scale = step_size / (2.0 * s_own.shape[0])
-    find_slots(blocks, coords, slot_of)
 
     def far_rows():
         return p_far[quarter] if far_side else p_far[...]
@@ -297,11 +294,10 @@
     choose(far_side == 0, row_tiles, col_tiles)
 
 
-def own_kernel(blocks, coords, omega, turned, s_own, stq, p_own, tiles, t_own, slot_of, grad, mats, nat_own):
+def own_kernel(blocks, slot_of, omega, turned, s_own, stq, p_own, tiles, t_own, grad, mats, nat_own):
     rows, width = grad.shape[0] // 2, grad.shape[1] // 2
     quarter = lax.axis_index("samp")
     scale = step_size / (2.0 * s_own.shape[0])
-    find_slots(blocks, coords, slot_of)
     natural(nat_own, p_own)
     grad[...] = dot_nn(p_own[quarter], s_own[...]) + dot_nt(stq[1], nat_own[...])
     slot = slot_of[OWN_PAIR]
@@ -317,12 +313,11 @@
 
 
 def inner_kernel(
-    blocks, coords, omega, s_cross, s_chip, stq, p_own, p_cross, p_chip, t_own, tiles, own, slot_of, grad, mats, nat
+    blocks, slot_of, omega, s_cross, s_chip, stq, p_own, p_cross, p_chip, t_own, tiles, own, grad, mats, nat
 ):
     rows, width = omega.shape[1:]
     quarter = lax.axis_index("samp")
     scale = step_size / (2.0 * s_chip.shape[0])
-    find_slots(blocks, coords, slot_of)
 
     def put(i, blk, slot, tile):
         tiles[i * 2 + blk] = tile
@@ -340,12 +335,11 @@
 
 
 def own_last_kernel(
-    blocks, coords, held, s_own, s_cross, s_chip, stq, p_own, out, rows_half, slot_of, grad, nat_own, tiles, sems,
+    blocks, slot_of, held, s_own, s_cross, s_chip, stq, p_own, out, rows_half, grad, nat_own, tiles, sems,
 ):
     rows, width = grad.shape[0] // 2, grad.shape[1] // 2
     quarter = lax.axis_index("samp")
     scale = step_size / (2.0 * s_own.shape[0])
-    find_slots(blocks, coords, slot_of)
     natural(nat_own, p_own)
     grad[...] = dot_nn(p_own[quarter], s_own[...]) + dot_nt(stq[1], nat_own[...])
     slot = slot_of[OWN_PAIR]
@@ -374,13 +368,12 @@
 
 
 def last_kernel(
-    blocks, coords, outer_cross, outer_chip, inner, s_cross, s_chip, stq, rows_half, p_cross, p_chip, begun,
-    out, slot_of, grad, nat, tiles, sems,
+    blocks, slot_of, outer_cross, outer_chip, inner, s_cross, s_chip, stq, rows_half, p_cross, p_chip, begun,
+    out, grad, nat, tiles, sems,
 ):
     rows, width = tiles.shape[1:]
     quarter = lax.axis_index("samp")
     scale = step_size / (2.0 * s_chip.shape[0])
-    find_slots(blocks, coords, slot_of)
 
     def copy(unit, slot):
         return pltpu.make_async_copy(tiles.at[unit], out.at[slot], sems.at[unit])
@@ -430,7 +423,6 @@
     chip = [(i, i ^ 1) for i in range(size)]
     cross = [(i, (i - 1) % size if i % 2 == 0 else (i + 1) % size) for i in range(size)]
     shape = jax.ShapeDtypeStruct
-    slots = pltpu.SMEM((OWN_PAIR + 1,), jnp.int32)
     params = pltpu.CompilerParams(vmem_limit_bytes=LIMIT)
 
     def call(body, in_specs, outs, scratch, macs, moved, aliases=None, out_specs=None):
@@ -482,20 +474,24 @@
     def kernel(body, *extra):
         return functools.partial(body, blocks, *extra)
 
-    turned, to_cross, s_chip = run(
+    turned, to_cross, s_chip, slot_of = run(
         kernel(first_cross_kernel), (coords, omega, turned_parts, s_own, s_chip), [SMEM, VMEM, ANY, VMEM, ANY],
-        (shape((OWN_PAIR + 1, rows, width), bf16), part, shape((count, wide), bf16)),
-        [slots, mats, pltpu.SemaphoreType.DMA((OWN_PAIR + 1, parts)), pltpu.SemaphoreType.DMA], 8,
+        (
+            shape((OWN_PAIR + 1, rows, width), bf16), part, shape((count, wide), bf16),
+            shape((OWN_PAIR + 1,), jnp.int32),
+        ),
+        [mats, pltpu.SemaphoreType.DMA((OWN_PAIR + 1, parts)), pltpu.SemaphoreType.DMA], 8,
+        out_specs=(VMEM, VMEM, VMEM, SMEM),
     )
     from_cross = permute(to_cross, cross)
     to_chip, s_cross = run(
-        kernel(first_chip_kernel), (coords, omega, turned, s_own, s_cross), [SMEM] + [VMEM] * 3 + [ANY],
-        (part, shape((count, wide), bf16)), [slots, mats, pltpu.SemaphoreType.DMA], 8,
+        kernel(first_chip_kernel), (slot_of, omega, turned, s_own, s_cross), [SMEM] + [VMEM] * 3 + [ANY],
+        (part, shape((count, wide), bf16)), [mats, pltpu.SemaphoreType.DMA], 8,
     )
     from_chip = permute(to_chip, chip)
     own, stq = run(
-        kernel(first_own_kernel), (coords, omega, turned, s_own, s_cross, s_chip), [SMEM] + [VMEM] * 5,
-        (full, shape((3, both, count), bf16)), [slots, mats], 8,
+        kernel(first_own_kernel), (slot_of, omega, turned, s_own, s_cross, s_chip), [SMEM] + [VMEM] * 5,
+        (full, shape((3, both, count), bf16)), [mats], 8,
     )
     total = (own + from_cross.astype(f32) + from_chip.astype(f32)).astype(bf16)
     far_cross = permute(total, cross)
@@ -506,21 +502,21 @@
 
     def edge(side, s_near, p_near, p_far):
         return run(
-            kernel(edge_kernel, side), (coords, omega, turned, s_own, s_near, p_near, p_far, stq, own_half),
-            [SMEM] + [VMEM] * 8, (four, part), [slots, grad, mats_two, nat], 20,
+            kernel(edge_kernel, side), (slot_of, omega, turned, s_own, s_near, p_near, p_far, stq, own_half),
+            [SMEM] + [VMEM] * 8, (four, part), [grad, mats_two, nat], 20,
         )
 
     outer_cross, to_cross = edge(0, s_chip, p_chip, far_cross)
     from_cross = permute(to_cross, cross)
     mine, t_own = run(
-        kernel(own_kernel), (coords, omega, turned, s_own, stq, p_own), [SMEM] + [VMEM] * 5,
-        (shape((3, rows, width), f32), full), [slots, grad, mats, nat], 12,
+        kernel(own_kernel), (slot_of, omega, turned, s_own, stq, p_own), [SMEM] + [VMEM] * 5,
+        (shape((3, rows, width), f32), full), [grad, mats, nat], 12,
     )
     outer_chip, to_chip = edge(2, s_cross, p_cross, p_chip)
     from_chip = permute(to_chip, chip)
     inner, own = run(
-        kernel(inner_kernel), (coords, omega, s_cross, s_chip, stq, p_own, p_cross, p_chip, t_own),
-        [SMEM] + [VMEM] * 8, (four, full), [slots, grad, mats, nat], 12,
+        kernel(inner_kernel), (slot_of, omega, s_cross, s_chip, stq, p_own, p_cross, p_chip, t_own),
+        [SMEM] + [VMEM] * 8, (four, full), [grad, mats, nat], 12,
     )
     total = (own + from_cross.astype(f32) + from_chip.astype(f32)).astype(bf16)
     p_own = spread(total)
@@ -528,16 +524,16 @@
     p_chip = permute(p_own, chip)
     whole = shape(omega.shape, f32)
     begun, rows_half = run(
-        kernel(own_last_kernel), (coords, mine, s_own, s_cross, s_chip, stq, p_own), [SMEM] + [VMEM] * 6,
+        kernel(own_last_kernel), (slot_of, mine, s_own, s_cross, s_chip, stq, p_own), [SMEM] + [VMEM] * 6,
         (whole, wide_half),
-        [slots, grad, nat, pltpu.VMEM((3, rows, width), f32), pltpu.SemaphoreType.DMA((3,))],
+        [grad, nat, pltpu.VMEM((3, rows, width), f32), pltpu.SemaphoreType.DMA((3,))],
         12, out_specs=(ANY, VMEM),
     )
     return run(
         kernel(last_kernel),
-        (coords, outer_cross, outer_chip, inner, s_cross, s_chip, stq, rows_half, p_cross, p_chip, begun),
+        (slot_of, outer_cross, outer_chip, inner, s_cross, s_chip, stq, rows_half, p_cross, p_chip, begun),
         [SMEM] + [VMEM] * 9 + [ANY], whole,
-        [slots, pltpu.VMEM((2, both, wide), f32), nat, pltpu.VMEM((8, rows, width), f32), pltpu.SemaphoreType.DMA((8,))],
+        [pltpu.VMEM((2, both, wide), f32), nat, pltpu.VMEM((8, rows, width), f32), pltpu.SemaphoreType.DMA((8,))],
         12, out_specs=ANY, aliases={10: 0},
     )
 

time: 127 us -> 126 us (level)
  no operation moved by 1% of the time
where the time goes in v9:
time: 126 us; the launch traced here: 125 us
  starting transfers between devices  62.3 us (49%)
  Pallas kernels  21.7 us (17%)
  blocking collectives  21.7 us (17%)
  waiting for transfers between devices  19 us (15%)
    ppermute x11, starting transfers between devices, permute(): return lax.ppermute(x, 'tiles', pairs)  47.3 us
    all_to_all x2, blocking collectives, spread(): lax.all_to_all(jnp.broadcast_to(x[None], (parts,) + x.shape), 'samp', 0, 0)  21.7 us
    pallas_call x10, Pallas kernels, run(): call(body, in_specs, outs, scratch, units * unit, 4 << 20, aliases, out_s...  17.4 us
    ppermute x11, waiting for transfers between devices, permute(): return lax.ppermute(x, 'tiles', pairs)  15 us
    all_to_all x1, starting transfers between devices, shards(): s_own = lax.all_to_all(copies, 'samp', 0, 0).reshape(count, wide)  9.33 us
    all_to_all x1, starting transfers between devices, shards(): turned_parts = lax.all_to_all(pieces, 'samp', 0, 0)  5.67 us
    all_to_all x1, waiting for transfers between devices, shards(): s_own = lax.all_to_all(copies, 'samp', 0, 0).reshape(count, wide)  4 us
    pallas_call x1, Pallas kernels, shards(): call(cut_kernel, [HBM], pltpu.HBM((parts, others, rows, rows), bf16), [pl...  2.62 us
  transfers between devices with their start and end apart: 13, of which 6 were waited for; matrix products, arithmetic and copies ran while one was open for 0% of the time, Pallas kernels for 13%

profile of v9, /device:TPU:2, one launch (start us, length us, event | category | flops | bytes accessed | tf_op | source)
XLA Modules:
  0.0 125.3 jit_solution(14475318551471191825)
XLA Ops:
  1.8 9.3 %all-to-all-start.1 = ((bf16[4,64,1024]{2,1,0:T(8,128)(2,1)}), bf16[4,64,1024]{2,1,0:T(8,128)(2,1)S(1)}, u32[]{:S(2)}, u32[]{:S(2)}) async-start(bf16[4,64,1024]{2,1,0:T(8,128)(2,1)} %shard_map.38), calls=%async_computation.1 | async-start | bytes 1048576 | tf_op jit(solution)/shard_map/all_to_all | solution.py:448
  11.1 2.6 %shard_map.37 = bf16[4,8,128,128]{3,2,1,0:T(8,128)(2,1)} custom-call(f32[10,128,512]{2,1,0:T(8,128)} %omega.15), custom_call_target="tpu_custom_call" | custom-call | bytes 4194304 | tf_op jit(solution)/shard_map/pallas_call | solution.py:449
  13.7 4.0 %all-to-all-done.1 = bf16[4,64,1024]{2,1,0:T(8,128)(2,1)S(1)} async-done(((bf16[4,64,1024]{2,1,0:T(8,128)(2,1)}), bf16[4,64,1024]{2,1,0:T(8,128)(2,1)S(1)}, u32[]{:S(2)}, u32[]{:S(2)}) %all-to-all-start.1) | async-done | bytes 524320 | tf_op jit(solution)/shard_map/all_to_all | solution.py:448
  17.7 5.7 %all-to-all-start = ((bf16[4,8,128,128]{3,2,1,0:T(8,128)(2,1)}), bf16[4,8,128,128]{3,2,1,0:T(8,128)(2,1)}, u32[]{:S(2)}, u32[]{:S(2)}) async-start(bf16[4,8,128,128]{3,2,1,0:T(8,128)(2,1)} %shard_map.37), calls=%async_computation | async-start | bytes 2097152 | tf_op jit(solution)/shard_map/all_to_all | solution.py:457
  23.4 1.9 %collective-permute-start = (bf16[256,1024]{1,0:T(8,128)(2,1)S(1)}, bf16[256,1024]{1,0:T(8,128)(2,1)}, u32[]{:S(2)}, u32[]{:S(2)}) collective-permute-start(bf16[256,1024]{1,0:T(8,128)(2,1)S(1)} %bitcast.1), channel_id=1, source_target_pairs={{0,4},{4,0},{8,12},{12,8},{16,20},{20,16},{24,28},{28,24},{32,36},... | collective-permute-start | bytes 1572872 | tf_op jit(solution)/shard_map/ppermute | solution.py:438
  25.3 10.9 %collective-permute-start.1 = (bf16[256,1024]{1,0:T(8,128)(2,1)S(1)}, bf16[256,1024]{1,0:T(8,128)(2,1)}, u32[]{:S(2)}, u32[]{:S(2)}) collective-permute-start(bf16[256,1024]{1,0:T(8,128)(2,1)S(1)} %bitcast.2), channel_id=1, source_target_pairs={{0,508},{4,8},{8,4},{12,16},{16,12},{20,24},{24,20},{28,32},{32,28... | collective-permute-start | bytes 1572872 | tf_op jit(solution)/shard_map/ppermute | solution.py:438
  36.3 3.1 %shard_map.39 = (bf16[9,128,512]{2,1,0:T(8,128)(2,1)S(1)}, bf16[256,256]{1,0:T(8,128)(2,1)S(1)}, bf16[256,1024]{1,0:T(8,128)(2,1)S(1)}, s32[9]{0:T(128)S(1)}) custom-call(s32[10,2]{1,0:T(8,128)S(1)} %copy.5.coords, f32[10,128,512]{2,1,0:T(8,128)S(1)} %copy-done, bf16[4,8,128,128]{3,2,1,0:T(8,128)(2,1)} %all-to-all-done.parts, bf16[256,1024]{1,0:T(8,128)(2,1)S(1)} %bitcast.3, ...), custom_call_target="tpu_custom_call" | custom-call | flops 268435456 | bytes 4194304 | tf_op jit(solution)/shard_map/pallas_call | solution.py:472
  39.4 3.7 %collective-permute-done.1.s_in = bf16[256,1024]{1,0:T(8,128)(2,1)} collective-permute-done((bf16[256,1024]{1,0:T(8,128)(2,1)S(1)}, bf16[256,1024]{1,0:T(8,128)(2,1)}, u32[]{:S(2)}, u32[]{:S(2)}) %collective-permute-start.1) | collective-permute-done | bytes 524320 | tf_op jit(solution)/shard_map/ppermute | solution.py:438
  43.1 2.1 %shard_map.40 = (bf16[256,256]{1,0:T(8,128)(2,1)S(1)}, bf16[256,1024]{1,0:T(8,128)(2,1)S(1)}) custom-call(s32[9]{0:T(128)S(1)} %get-tuple-element.23.slot_of, f32[10,128,512]{2,1,0:T(8,128)S(1)} %copy-done, bf16[9,128,512]{2,1,0:T(8,128)(2,1)S(1)} %get-tuple-element.24.turned, bf16[256,1024]{1,0:T(8,128)(2,1)S(1)} %bitcast.4, ...), custom_call_target="tpu_custom_call" | custom-call | flops 268435456 | bytes 4194304 | tf_op jit(solution)/shard_map/pallas_call | solution.py:472
  45.2 1.9 %collective-permute-start.3 = (bf16[256,256]{1,0:T(8,128)(2,1)S(1)}, bf16[256,256]{1,0:T(8,128)(2,1)S(1)}, u32[]{:S(2)}, u32[]{:S(2)}) collective-permute-start(bf16[256,256]{1,0:T(8,128)(2,1)S(1)} %get-tuple-element.29), channel_id=1, source_target_pairs={{0,4},{4,0},{8,12},{12,8},{16,20},{20,16},{24,28},{28,24},{32,36},... | collective-permute-start | bytes 393224 | tf_op jit(solution)/shard_map/ppermute | solution.py:438
  47.1 6.9 %collective-permute-start.2 = (bf16[256,256]{1,0:T(8,128)(2,1)S(1)}, bf16[256,256]{1,0:T(8,128)(2,1)S(1)}, u32[]{:S(2)}, u32[]{:S(2)}) collective-permute-start(bf16[256,256]{1,0:T(8,128)(2,1)S(1)} %get-tuple-element.28), channel_id=1, source_target_pairs={{0,508},{4,8},{8,4},{12,16},{16,12},{20,24},{24,20},{28,32},{32,28... | collective-permute-start | bytes 393224 | tf_op jit(solution)/shard_map/ppermute | solution.py:438
  56.8 11.2 %all_to_all.20.p_own = bf16[4,256,256]{2,1,0:T(8,128)(2,1)S(1)} all-to-all(bf16[4,256,256]{2,1,0:T(8,128)(2,1)S(1)} %broadcast_in_dim.4), channel_id=1, replica_groups=mesh['tiles'=128,'samp'=4] {'samp'}, dimensions={0} | all-to-all | bytes 1048576 | tf_op jit(solution)/shard_map/all_to_all | solution.py:441
  68.1 6.1 %collective-permute-start.6 = (bf16[4,256,256]{2,1,0:T(8,128)(2,1)S(1)}, bf16[4,256,256]{2,1,0:T(8,128)(2,1)S(1)}, u32[]{:S(2)}, u32[]{:S(2)}) collective-permute-start(bf16[4,256,256]{2,1,0:T(8,128)(2,1)S(1)} %all_to_all.20.p_own), channel_id=1, source_target_pairs={{0,508},{4,8},{8,4},{12,16},{16,12},{20,24},{24,20},{28,32},{32,28... | collective-permute-start | bytes 1572872 | tf_op jit(solution)/shard_map/ppermute | solution.py:438
  74.2 1.9 %collective-permute-start.4 = (bf16[4,256,256]{2,1,0:T(8,128)(2,1)S(1)}, bf16[4,256,256]{2,1,0:T(8,128)(2,1)S(1)}, u32[]{:S(2)}, u32[]{:S(2)}) collective-permute-start(bf16[4,256,256]{2,1,0:T(8,128)(2,1)S(1)} %all_to_all.20.p_own), channel_id=1, source_target_pairs={{0,4},{4,0},{8,12},{12,8},{16,20},{20,16},{24,28},{28,24},{32,36},... | collective-permute-start | bytes 1572872 | tf_op jit(solution)/shard_map/ppermute | solution.py:438
  76.1 2.8 %collective-permute-start.5 = (bf16[256,256]{1,0:T(8,128)(2,1)S(1)}, bf16[256,256]{1,0:T(8,128)(2,1)S(1)}, u32[]{:S(2)}, u32[]{:S(2)}) collective-permute-start(bf16[256,256]{1,0:T(8,128)(2,1)S(1)} %add_convert_fusion.1), channel_id=1, source_target_pairs={{0,508},{4,8},{8,4},{12,16},{16,12},{20,24},{24,20},{28,32},{32,28... | collective-permute-start | bytes 393224 | tf_op jit(solution)/shard_map/ppermute | solution.py:438
  79.2 2.7 %collective-permute-done.6.p_near.p_cross = bf16[4,256,256]{2,1,0:T(8,128)(2,1)S(1)} collective-permute-done((bf16[4,256,256]{2,1,0:T(8,128)(2,1)S(1)}, bf16[4,256,256]{2,1,0:T(8,128)(2,1)S(1)}, u32[]{:S(2)}, u32[]{:S(2)}) %collective-permute-start.6) | collective-permute-done | bytes 524320 | tf_op jit(solution)/shard_map/ppermute | solution.py:438
  81.9 2.0 %shard_map.44 = (f32[4,128,512]{2,1,0:T(8,128)S(1)}, bf16[256,256]{1,0:T(8,128)(2,1)S(1)}) custom-call(s32[9]{0:T(128)S(1)} %get-tuple-element.23.slot_of, f32[10,128,512]{2,1,0:T(8,128)S(1)} %copy-done, bf16[9,128,512]{2,1,0:T(8,128)(2,1)S(1)} %get-tuple-element.24.turned, bf16[256,1024]{1,0:T(8,128)(2,1)S(1)} %bitcast.6, ...), custom_call_target="tpu_custom_call" | custom-call | flops 671088640 | bytes 4194304 | tf_op jit(solution)/shard_map/pallas_call | solution.py:472
  83.8 1.9 %collective-permute-start.8 = (bf16[256,256]{1,0:T(8,128)(2,1)S(1)}, bf16[256,256]{1,0:T(8,128)(2,1)S(1)}, u32[]{:S(2)}, u32[]{:S(2)}) collective-permute-start(bf16[256,256]{1,0:T(8,128)(2,1)S(1)} %get-tuple-element.38), channel_id=1, source_target_pairs={{0,4},{4,0},{8,12},{12,8},{16,20},{20,16},{24,28},{28,24},{32,36},... | collective-permute-start | bytes 393224 | tf_op jit(solution)/shard_map/ppermute | solution.py:438
  87.2 6.1 %collective-permute-start.7 = (bf16[256,256]{1,0:T(8,128)(2,1)S(1)}, bf16[256,256]{1,0:T(8,128)(2,1)S(1)}, u32[]{:S(2)}, u32[]{:S(2)}) collective-permute-start(bf16[256,256]{1,0:T(8,128)(2,1)S(1)} %get-tuple-element.37), channel_id=1, source_target_pairs={{0,508},{4,8},{8,4},{12,16},{16,12},{20,24},{24,20},{28,32},{32,28... | collective-permute-start | bytes 393224 | tf_op jit(solution)/shard_map/ppermute | solution.py:438
  96.9 10.5 %all_to_all.21.p_own = bf16[4,256,256]{2,1,0:T(8,128)(2,1)S(1)} all-to-all(bf16[4,256,256]{2,1,0:T(8,128)(2,1)S(1)} %broadcast_in_dim.5), channel_id=1, replica_groups=mesh['tiles'=128,'samp'=4] {'samp'}, dimensions={0} | all-to-all | bytes 1048576 | tf_op jit(solution)/shard_map/all_to_all | solution.py:441
  109.3 5.0 %collective-permute-start.9 = (bf16[4,256,256]{2,1,0:T(8,128)(2,1)S(1)}, bf16[4,256,256]{2,1,0:T(8,128)(2,1)S(1)}, u32[]{:S(2)}, u32[]{:S(2)}) collective-permute-start(bf16[4,256,256]{2,1,0:T(8,128)(2,1)S(1)} %all_to_all.21.p_own), channel_id=1, source_target_pairs={{0,508},{4,8},{8,4},{12,16},{16,12},{20,24},{24,20},{28,32},{32,28... | collective-permute-start | bytes 1572872 | tf_op jit(solution)/shard_map/ppermute | solution.py:438
  114.3 2.1 %shard_map.47 = (f32[10,128,512]{2,1,0:T(8,128)}, f32[256,1024]{1,0:T(8,128)S(1)}) custom-call(s32[9]{0:T(128)S(1)} %get-tuple-element.23.slot_of, f32[3,128,512]{2,1,0:T(8,128)S(1)} %get-tuple-element.35.held, bf16[256,1024]{1,0:T(8,128)(2,1)S(1)} %bitcast.9, bf16[256,1024]{1,0:T(8,128)(2,1)S(1)} %get-tuple-element.26.s_cross.s_near, ...), custom_call_target="tpu_custom_call" | custom-call | flops 402653184 | bytes 4194304 | tf_op jit(solution)/shard_map/pallas_call | solution.py:472
  116.4 6.7 %collective-permute-done.9.p_cross = bf16[4,256,256]{2,1,0:T(8,128)(2,1)S(1)} collective-permute-done((bf16[4,256,256]{2,1,0:T(8,128)(2,1)S(1)}, bf16[4,256,256]{2,1,0:T(8,128)(2,1)S(1)}, u32[]{:S(2)}, u32[]{:S(2)}) %collective-permute-start.9) | collective-permute-done | bytes 524320 | tf_op jit(solution)/shard_map/ppermute | solution.py:438
  123.1 2.2 %shard_map.48 = f32[10,128,512]{2,1,0:T(8,128)} custom-call(s32[9]{0:T(128)S(1)} %get-tuple-element.23.slot_of, f32[4,128,512]{2,1,0:T(8,128)S(1)} %get-tuple-element.31.outer_cross, f32[4,128,512]{2,1,0:T(8,128)S(1)} %get-tuple-element.32.outer_chip, f32[4,128,512]{2,1,0:T(8,128)S(1)} %get-tuple-element.34.inner, ...), custom_call_target="tpu_custom_call", output_to_operand_aliasing={{}: (10, {})} | custom-call | flops 402653184 | bytes 4194304 | tf_op jit(solution)/shard_map/pallas_call | solution.py:472
  (25 shorter events, 11.8 us)
Async XLA Ops:
  1.8 16.0 %all-to-all-start.1 = ((bf16[4,64,1024]{2,1,0:T(8,128)(2,1)}), bf16[4,64,1024]{2,1,0:T(8,128)(2,1)S(1)}, u32[]{:S(2)}, u32[]{:S(2)}) async-start(bf16[4,64,1024]{2,1,0:T(8,128)(2,1)} %shard_map.38), calls=%async_computation.1 | async-start | bytes 1048576 | tf_op jit(solution)/shard_map/all_to_all | solution.py:448
  11.1 25.1 %copy-start.1 = (s32[10,2]{0,1:T(2,128)S(1)}, s32[10,2]{0,1:T(2,128)}, u32[]{:S(2)}) copy-start(s32[10,2]{0,1:T(2,128)} %param.5) | copy-start | bytes 244
  11.1 25.2 %copy-start = (f32[10,128,512]{2,1,0:T(8,128)S(1)}, f32[10,128,512]{2,1,0:T(8,128)}, u32[]{:S(2)}) copy-start(f32[10,128,512]{2,1,0:T(8,128)} %omega.15) | copy-start | bytes 7864324
  17.7 18.6 %all-to-all-start = ((bf16[4,8,128,128]{3,2,1,0:T(8,128)(2,1)}), bf16[4,8,128,128]{3,2,1,0:T(8,128)(2,1)}, u32[]{:S(2)}, u32[]{:S(2)}) async-start(bf16[4,8,128,128]{3,2,1,0:T(8,128)(2,1)} %shard_map.37), calls=%async_computation | async-start | bytes 2097152 | tf_op jit(solution)/shard_map/all_to_all | solution.py:457
  23.4 12.9 %collective-permute-start = (bf16[256,1024]{1,0:T(8,128)(2,1)S(1)}, bf16[256,1024]{1,0:T(8,128)(2,1)}, u32[]{:S(2)}, u32[]{:S(2)}) collective-permute-start(bf16[256,1024]{1,0:T(8,128)(2,1)S(1)} %bitcast.1), channel_id=1, source_target_pairs={{0,4},{4,0},{8,12},{12,8},{16,20},{20,16},{24,28},{28,24},{32,36},... | collective-permute-start | bytes 1572872 | tf_op jit(solution)/shard_map/ppermute | solution.py:438
  25.3 17.8 %collective-permute-start.1 = (bf16[256,1024]{1,0:T(8,128)(2,1)S(1)}, bf16[256,1024]{1,0:T(8,128)(2,1)}, u32[]{:S(2)}, u32[]{:S(2)}) collective-permute-start(bf16[256,1024]{1,0:T(8,128)(2,1)S(1)} %bitcast.2), channel_id=1, source_target_pairs={{0,508},{4,8},{8,4},{12,16},{16,12},{20,24},{24,20},{28,32},{32,28... | collective-permute-start | bytes 1572872 | tf_op jit(solution)/shard_map/ppermute | solution.py:438
  45.2 10.2 %collective-permute-start.3 = (bf16[256,256]{1,0:T(8,128)(2,1)S(1)}, bf16[256,256]{1,0:T(8,128)(2,1)S(1)}, u32[]{:S(2)}, u32[]{:S(2)}) collective-permute-start(bf16[256,256]{1,0:T(8,128)(2,1)S(1)} %get-tuple-element.29), channel_id=1, source_target_pairs={{0,4},{4,0},{8,12},{12,8},{16,20},{20,16},{24,28},{28,24},{32,36},... | collective-permute-start | bytes 393224 | tf_op jit(solution)/shard_map/ppermute | solution.py:438
  47.1 9.6 %collective-permute-start.2 = (bf16[256,256]{1,0:T(8,128)(2,1)S(1)}, bf16[256,256]{1,0:T(8,128)(2,1)S(1)}, u32[]{:S(2)}, u32[]{:S(2)}) collective-permute-start(bf16[256,256]{1,0:T(8,128)(2,1)S(1)} %get-tuple-element.28), channel_id=1, source_target_pairs={{0,508},{4,8},{8,4},{12,16},{16,12},{20,24},{24,20},{28,32},{32,28... | collective-permute-start | bytes 393224 | tf_op jit(solution)/shard_map/ppermute | solution.py:438
  68.1 13.8 %collective-permute-start.6 = (bf16[4,256,256]{2,1,0:T(8,128)(2,1)S(1)}, bf16[4,256,256]{2,1,0:T(8,128)(2,1)S(1)}, u32[]{:S(2)}, u32[]{:S(2)}) collective-permute-start(bf16[4,256,256]{2,1,0:T(8,128)(2,1)S(1)} %all_to_all.20.p_own), channel_id=1, source_target_pairs={{0,508},{4,8},{8,4},{12,16},{16,12},{20,24},{24,20},{28,32},{32,28... | collective-permute-start | bytes 1572872 | tf_op jit(solution)/shard_map/ppermute | solution.py:438
  74.2 7.7 %collective-permute-start.4 = (bf16[4,256,256]{2,1,0:T(8,128)(2,1)S(1)}, bf16[4,256,256]{2,1,0:T(8,128)(2,1)S(1)}, u32[]{:S(2)}, u32[]{:S(2)}) collective-permute-start(bf16[4,256,256]{2,1,0:T(8,128)(2,1)S(1)} %all_to_all.20.p_own), channel_id=1, source_target_pairs={{0,4},{4,0},{8,12},{12,8},{16,20},{20,16},{24,28},{28,24},{32,36},... | collective-permute-start | bytes 1572872 | tf_op jit(solution)/shard_map/ppermute | solution.py:438
  76.1 9.6 %collective-permute-start.5 = (bf16[256,256]{1,0:T(8,128)(2,1)S(1)}, bf16[256,256]{1,0:T(8,128)(2,1)S(1)}, u32[]{:S(2)}, u32[]{:S(2)}) collective-permute-start(bf16[256,256]{1,0:T(8,128)(2,1)S(1)} %add_convert_fusion.1), channel_id=1, source_target_pairs={{0,508},{4,8},{8,4},{12,16},{16,12},{20,24},{24,20},{28,32},{32,28... | collective-permute-start | bytes 393224 | tf_op jit(solution)/shard_map/ppermute | solution.py:438
  83.8 12.3 %collective-permute-start.8 = (bf16[256,256]{1,0:T(8,128)(2,1)S(1)}, bf16[256,256]{1,0:T(8,128)(2,1)S(1)}, u32[]{:S(2)}, u32[]{:S(2)}) collective-permute-start(bf16[256,256]{1,0:T(8,128)(2,1)S(1)} %get-tuple-element.38), channel_id=1, source_target_pairs={{0,4},{4,0},{8,12},{12,8},{16,20},{20,16},{24,28},{28,24},{32,36},... | collective-permute-start | bytes 393224 | tf_op jit(solution)/shard_map/ppermute | solution.py:438
  87.2 9.6 %collective-permute-start.7 = (bf16[256,256]{1,0:T(8,128)(2,1)S(1)}, bf16[256,256]{1,0:T(8,128)(2,1)S(1)}, u32[]{:S(2)}, u32[]{:S(2)}) collective-permute-start(bf16[256,256]{1,0:T(8,128)(2,1)S(1)} %get-tuple-element.37), channel_id=1, source_target_pairs={{0,508},{4,8},{8,4},{12,16},{16,12},{20,24},{24,20},{28,32},{32,28... | collective-permute-start | bytes 393224 | tf_op jit(solution)/shard_map/ppermute | solution.py:438
  107.3 9.0 %collective-permute-start.10 = (bf16[4,256,256]{2,1,0:T(8,128)(2,1)S(1)}, bf16[4,256,256]{2,1,0:T(8,128)(2,1)S(1)}, u32[]{:S(2)}, u32[]{:S(2)}) collective-permute-start(bf16[4,256,256]{2,1,0:T(8,128)(2,1)S(1)} %all_to_all.21.p_own), channel_id=1, source_target_pairs={{0,4},{4,0},{8,12},{12,8},{16,20},{20,16},{24,28},{28,24},{32,36},... | collective-permute-start | bytes 1572872 | tf_op jit(solution)/shard_map/ppermute | solution.py:438
  109.3 13.8 %collective-permute-start.9 = (bf16[4,256,256]{2,1,0:T(8,128)(2,1)S(1)}, bf16[4,256,256]{2,1,0:T(8,128)(2,1)S(1)}, u32[]{:S(2)}, u32[]{:S(2)}) collective-permute-start(bf16[4,256,256]{2,1,0:T(8,128)(2,1)S(1)} %all_to_all.21.p_own), channel_id=1, source_target_pairs={{0,508},{4,8},{8,4},{12,16},{16,12},{20,24},{24,20},{28,32},{32,28... | collective-permute-start | bytes 1572872 | tf_op jit(solution)/shard_map/ppermute | solution.py:438
